TPU v7x, 768 devices: a whole 4x8x12 slice. The times are simulated.
768 devices in a mesh: dom: 192 (over z, y, core), sub: 4 (over x).
Axes of the slice: x: 4, y: 8, z: 12, core: 2. Of those that a mesh axis runs over, the one named last changes fastest.
Arguments:
- rhs: float32 [2, 589824], P(None, ('dom', 'sub')), may hold values from -6 to 6
- start: float32 [2, 589824], P(None, ('dom', 'sub')), may hold values from -6 to 6
- stiffness: bfloat16 [589824, 768], P(('dom', 'sub')), may hold values from -0.109375 to 0.109375
- local_inverse: bfloat16 [589824, 768], P(('dom', 'sub')), may hold values from -0.109375 to 0.109375
- basis: bfloat16 [24, 589824], P(None, ('dom', 'sub')), may hold values from -0.21875 to 0.21875
- weights: float32 [589824], P(('dom', 'sub')), may hold values from 0.3 to 1
- coarse_inverse: float32 [18432, 18432], P(('dom', 'sub')), may hold values from -0.1875 to 0.1875
- orders: int32 [768], P(('dom', 'sub')), may hold values from 192 to 768, as said below
- out_rows: int32 [768, 6, 128], P(('dom', 'sub')), may hold values from 0 to 191
- out_counts: int32 [768, 6], P(('dom', 'sub')), may hold values from 0 to 128, as said below
- in_rows: int32 [768, 6, 128], P(('dom', 'sub')), may hold values from 0 to 191
Outputs:
- solution: float32 [2, 589824], P(None, ('dom', 'sub'))
- residual: float32 [2, 589824], P(None, ('dom', 'sub'))
Inputs may be any that keep to these rules, and one draw needn't show every extreme that they name: `orders`: some subdomain has order exactly 768, another exactly 192. `out_rows`: every listed row lies below every subdomain's order. `in_rows`: every listed row lies below every subdomain's order. `out_counts`: some direction of some subdomain uses all 128 slots.
All inputs are finite; a program needn't handle non-finite values.
Results may differ from a plain program's by a relative error of at most 0.0019.
Values sent between devices are 32-bit elements; how exact they have to be, the bound alone decides.
No kernel may reach another device: no remote copies, remote signals or barrier semaphores. Data moves between devices by JAX's collectives and lax.ppermute only.
A program may use at most 32 MiB of HBM per device.

v0:
```python
import jax
import jax.numpy as jnp
from jax import lax
from jax.sharding import PartitionSpec as P

DIRECTIONS = (("sub", 1), ("sub", -1), ("dom", 1), ("dom", -1), ("dom", 2), ("dom", -2))


def passed_along(block, axis, distance):
    devices = range(lax.axis_size(axis))
    route = [(i - distance, i) for i in devices if i - distance in devices]
    return lax.ppermute(block, axis, route)


def assemble(terms, out_rows, out_counts, in_rows):
    slot_ids = jnp.arange(out_rows.shape[2])
    summed = terms
    for index_dir, (axis_name, offset) in enumerate(DIRECTIONS):
        used = (slot_ids < out_counts[0, index_dir]).astype(jnp.float32)
        picked = terms[:, out_rows[0, index_dir]] * used[None, :]
        if axis_name == "sub":
            arrived = passed_along(picked, "sub", offset)
        else:
            arrived = passed_along(picked, "dom", offset)
        summed = summed.at[:, in_rows[0, index_dir]].add(arrived)
    return summed


def per_device(
    rhs,
    start,
    stiffness,
    local_inverse,
    basis,
    weights,
    coarse_inverse,
    orders,
    out_rows,
    out_counts,
    in_rows,
):
    order_pad = stiffness.shape[0]
    row_mask = (jnp.arange(order_pad) < orders[0]).astype(jnp.float32)[None, :]
    iterate = start * row_mask
    weight_rows = weights[None, :]
    iterate_bf = iterate.astype(jnp.bfloat16)
    product = jnp.dot(iterate_bf, stiffness, preferred_element_type=jnp.float32)
    residual = row_mask * (rhs - assemble(product, out_rows, out_counts, in_rows))
    residual_bf = residual.astype(jnp.bfloat16)
    coarse_in = lax.dot_general(
        residual_bf, basis, (((1,), (1,)), ((), ())), preferred_element_type=jnp.float32
    )
    coarse_out = lax.dot_general(
        lax.all_gather(coarse_in, ("dom", "sub"), axis=1, tiled=True),
        coarse_inverse,
        (((1,), (1,)), ((), ())),
        precision=lax.Precision.HIGHEST,
        preferred_element_type=jnp.float32,
    )
    local_fix = jnp.dot(residual_bf, local_inverse, preferred_element_type=jnp.float32)
    coarse_fix = jnp.dot(coarse_out.astype(jnp.bfloat16), basis, preferred_element_type=jnp.float32)
    correction = weight_rows * row_mask * (local_fix + coarse_fix)
    iterate = iterate + assemble(correction, out_rows, out_counts, in_rows)
    return (iterate, residual)


def solution(mesh):
    return jax.shard_map(
        per_device,
        mesh=mesh,
        in_specs=(
            P(None, ("dom", "sub")),
            P(None, ("dom", "sub")),
            P(("dom", "sub"), None),
            P(("dom", "sub"), None),
            P(None, ("dom", "sub")),
            P(("dom", "sub")),
            P(("dom", "sub"), None),
            P(("dom", "sub")),
            P(("dom", "sub"), None, None),
            P(("dom", "sub"), None),
            P(("dom", "sub"), None, None),
        ),
        out_specs=(P(None, ("dom", "sub")), P(None, ("dom", "sub"))),
        check_vma=False,
    )
```

profile of v0, /device:TPU:66, one launch (start us, length us, event | category | flops | bytes accessed | tf_op | source)
XLA Modules:
  0.0 212.5 jit_solution(9446099652281297560)
XLA Ops:
  0.6 0.9 fusion.43
  2.2 1.5 fusion.44
  3.7 0.6 compare_convert_fusion.5
  4.4 1.9 fusion.27
  6.3 0.6 gather_fusion
  7.0 3.4 %collective-permute-start = (f32[2,128]{0,1:T(8,128)S(1)}, f32[2,128]{0,1:T(8,128)S(1)}, u32[]{:S(2)}, u32[]{:S(2)}) collective-permute-start(f32[2,128]{0,1:T(8,128)S(1)} %multiply_bitcast_fusion.11), channel_id=1, source_target_pairs={{0,1},{1,2},{2,3},{4,5},{5,6},{6,7},{8,9},{9,10},{10,11},{12,13},{... | collective-permute-start | bytes 3080 | tf_op jit(solution)/shard_map/ppermute | solution.py:12
  10.4 0.6 gather_fusion.1
  11.1 0.6 compare_convert_fusion.4
  11.7 0.1 multiply_bitcast_fusion.10
  11.8 2.4 %collective-permute-start.1 = (f32[2,128]{0,1:T(8,128)S(1)}, f32[2,128]{0,1:T(8,128)S(1)}, u32[]{:S(2)}, u32[]{:S(2)}) collective-permute-start(f32[2,128]{0,1:T(8,128)S(1)} %multiply_bitcast_fusion.10), channel_id=1, source_target_pairs={{1,0},{2,1},{3,2},{5,4},{6,5},{7,6},{9,8},{10,9},{11,10},{13,12},{... | collective-permute-start | bytes 3080 | tf_op jit(solution)/shard_map/ppermute | solution.py:12
  14.3 0.6 gather_fusion.2
  14.9 0.6 compare_convert_fusion.3
  15.5 0.1 multiply_bitcast_fusion.9
  15.6 1.9 collective-permute-start.2
  17.5 0.6 gather_fusion.3
  18.1 0.7 compare_convert_fusion.2
  18.8 0.1 multiply_bitcast_fusion.8
  18.9 5.8 %collective-permute-start.3 = (f32[2,128]{0,1:T(8,128)S(1)}, f32[2,128]{0,1:T(8,128)S(1)}, u32[]{:S(2)}, u32[]{:S(2)}) collective-permute-start(f32[2,128]{0,1:T(8,128)S(1)} %multiply_bitcast_fusion.8), channel_id=1, source_target_pairs={{4,0},{8,4},{12,8},{16,12},{20,16},{24,20},{28,24},{32,28},{36,32}... | collective-permute-start | bytes 3080 | tf_op jit(solution)/shard_map/ppermute | solution.py:12
  24.7 0.6 gather_fusion.4
  25.4 0.6 compare_convert_fusion.1
  26.0 0.1 multiply_bitcast_fusion.7
  26.1 1.9 collective-permute-start.4
  28.0 0.6 gather_fusion.5
  28.6 0.6 compare_convert_fusion
  29.3 0.1 multiply_bitcast_fusion.6
  29.4 6.0 %collective-permute-start.5 = (f32[2,128]{0,1:T(8,128)S(1)}, f32[2,128]{0,1:T(8,128)S(1)}, u32[]{:S(2)}, u32[]{:S(2)}) collective-permute-start(f32[2,128]{0,1:T(8,128)S(1)} %multiply_bitcast_fusion.6), channel_id=1, source_target_pairs={{8,0},{12,4},{16,8},{20,12},{24,16},{28,20},{32,24},{36,28},{40,32... | collective-permute-start | bytes 3080 | tf_op jit(solution)/shard_map/ppermute | solution.py:12
  35.5 1.4 scatter_custom_fusion
  36.9 1.4 scatter_custom_fusion.1
  38.4 1.4 scatter_custom_fusion.2
  39.8 1.4 scatter_custom_fusion.3
  41.2 1.4 scatter_custom_fusion.4
  42.7 1.4 scatter_custom_fusion.5
  44.1 0.1 copy.53
  44.3 0.1 convolution_bitcast_fusion
  44.4 128.4 %all-gather = f32[768,24,2]{1,2,0:T(2,128)S(1)} all-gather(f32[1,24,2]{1,2,0:T(2,128)S(1)} %convolution_bitcast_fusion), channel_id=1, replica_groups=mesh['dom'=192,'sub'=4] {'dom','sub'}, dimensions={0}, use_global_device_ids=true | all-gather | bytes 147648 | tf_op jit(solution)/shard_map/all_gather | solution.py:54
  172.9 0.5 reshape.570
  173.4 1.5 fusion.30
  174.9 1.8 convolution_convert_fusion
  176.7 0.1 multiply_add_fusion
  176.8 0.2 copy.55
  177.0 0.7 gather_fusion.6
  177.7 0.6 gather_fusion.7
  178.3 0.6 gather_fusion.8
  179.0 0.6 gather_fusion.9
  179.6 0.6 gather_fusion.10
  180.3 0.6 gather_fusion.11
  181.0 2.8 %collective-permute-start.6 = (f32[2,128]{0,1:T(8,128)S(1)}, f32[2,128]{0,1:T(8,128)S(1)}, u32[]{:S(2)}, u32[]{:S(2)}) collective-permute-start(f32[2,128]{0,1:T(8,128)S(1)} %multiply_bitcast_fusion.5), channel_id=1, source_target_pairs={{0,1},{1,2},{2,3},{4,5},{5,6},{6,7},{8,9},{9,10},{10,11},{12,13},{... | collective-permute-start | bytes 3080 | tf_op jit(solution)/shard_map/ppermute | solution.py:12
  183.7 0.1 multiply_bitcast_fusion.4
  183.8 3.1 %collective-permute-start.7 = (f32[2,128]{0,1:T(8,128)S(1)}, f32[2,128]{0,1:T(8,128)S(1)}, u32[]{:S(2)}, u32[]{:S(2)}) collective-permute-start(f32[2,128]{0,1:T(8,128)S(1)} %multiply_bitcast_fusion.4), channel_id=1, source_target_pairs={{1,0},{2,1},{3,2},{5,4},{6,5},{7,6},{9,8},{10,9},{11,10},{13,12},{... | collective-permute-start | bytes 3080 | tf_op jit(solution)/shard_map/ppermute | solution.py:12
  186.9 0.1 multiply_bitcast_fusion.3
  187.0 1.9 collective-permute-start.8
  188.9 0.1 multiply_bitcast_fusion.2
  189.0 5.8 %collective-permute-start.9 = (f32[2,128]{0,1:T(8,128)S(1)}, f32[2,128]{0,1:T(8,128)S(1)}, u32[]{:S(2)}, u32[]{:S(2)}) collective-permute-start(f32[2,128]{0,1:T(8,128)S(1)} %multiply_bitcast_fusion.2), channel_id=1, source_target_pairs={{4,0},{8,4},{12,8},{16,12},{20,16},{24,20},{28,24},{32,28},{36,32}... | collective-permute-start | bytes 3080 | tf_op jit(solution)/shard_map/ppermute | solution.py:12
  194.8 0.1 multiply_bitcast_fusion.1
  194.9 1.9 collective-permute-start.10
  196.9 6.0 %collective-permute-start.11 = (f32[2,128]{0,1:T(8,128)S(1)}, f32[2,128]{0,1:T(8,128)S(1)}, u32[]{:S(2)}, u32[]{:S(2)}) collective-permute-start(f32[2,128]{0,1:T(8,128)S(1)} %multiply_bitcast_fusion), channel_id=1, source_target_pairs={{8,0},{12,4},{16,8},{20,12},{24,16},{28,20},{32,24},{36,28},{40,32... | collective-permute-start | bytes 3080 | tf_op jit(solution)/shard_map/ppermute | solution.py:12
  202.9 0.2 copy.56
  203.1 1.4 scatter_custom_fusion.6
  204.6 1.4 scatter_custom_fusion.7
  206.0 1.4 scatter_custom_fusion.8
  207.4 1.4 scatter_custom_fusion.9
  208.9 1.4 scatter_custom_fusion.10
  210.3 1.4 scatter_custom_fusion.11
  211.7 0.7 copy.62
  (37 shorter events, 0.4 us)
Async XLA Ops:
  0.6 174.3 %copy-start = (f32[24,18432]{1,0:T(8,128)S(1)}, f32[24,18432]{1,0:T(8,128)}, u32[]{:S(2)}) copy-start(f32[24,18432]{1,0:T(8,128)} %param.17) | copy-start | bytes 5308420
  4.4 25.0 %copy-start.5 = (f32[768]{0:T(1024)S(1)}, f32[768]{0:T(1024)}, u32[]{:S(2)}) copy-start(f32[768]{0:T(1024)} %param.16) | copy-start | bytes 9220
  4.4 31.1 %copy-start.6 = (s32[1,6,128]{2,0,1:T(1,128)S(1)}, s32[1,6,128]{2,0,1:T(1,128)}, u32[]{:S(2)}) copy-start(s32[1,6,128]{2,0,1:T(1,128)} %param.21) | copy-start | bytes 9220
  7.0 22.4 %collective-permute-start = (f32[2,128]{0,1:T(8,128)S(1)}, f32[2,128]{0,1:T(8,128)S(1)}, u32[]{:S(2)}, u32[]{:S(2)}) collective-permute-start(f32[2,128]{0,1:T(8,128)S(1)} %multiply_bitcast_fusion.11), channel_id=1, source_target_pairs={{0,1},{1,2},{2,3},{4,5},{5,6},{6,7},{8,9},{9,10},{10,11},{12,13},{... | collective-permute-start | bytes 3080 | tf_op jit(solution)/shard_map/ppermute | solution.py:12
  11.8 25.1 %collective-permute-start.1 = (f32[2,128]{0,1:T(8,128)S(1)}, f32[2,128]{0,1:T(8,128)S(1)}, u32[]{:S(2)}, u32[]{:S(2)}) collective-permute-start(f32[2,128]{0,1:T(8,128)S(1)} %multiply_bitcast_fusion.10), channel_id=1, source_target_pairs={{1,0},{2,1},{3,2},{5,4},{6,5},{7,6},{9,8},{10,9},{11,10},{13,12},{... | collective-permute-start | bytes 3080 | tf_op jit(solution)/shard_map/ppermute | solution.py:12
  15.6 22.8 %collective-permute-start.2 = (f32[2,128]{0,1:T(8,128)S(1)}, f32[2,128]{0,1:T(8,128)S(1)}, u32[]{:S(2)}, u32[]{:S(2)}) collective-permute-start(f32[2,128]{0,1:T(8,128)S(1)} %multiply_bitcast_fusion.9), channel_id=1, source_target_pairs={{0,4},{4,8},{8,12},{12,16},{16,20},{20,24},{24,28},{28,32},{32,36}... | collective-permute-start | bytes 3080 | tf_op jit(solution)/shard_map/ppermute | solution.py:12
  18.9 20.9 %collective-permute-start.3 = (f32[2,128]{0,1:T(8,128)S(1)}, f32[2,128]{0,1:T(8,128)S(1)}, u32[]{:S(2)}, u32[]{:S(2)}) collective-permute-start(f32[2,128]{0,1:T(8,128)S(1)} %multiply_bitcast_fusion.8), channel_id=1, source_target_pairs={{4,0},{8,4},{12,8},{16,12},{20,16},{24,20},{28,24},{32,28},{36,32}... | collective-permute-start | bytes 3080 | tf_op jit(solution)/shard_map/ppermute | solution.py:12
  26.1 15.2 %collective-permute-start.4 = (f32[2,128]{0,1:T(8,128)S(1)}, f32[2,128]{0,1:T(8,128)S(1)}, u32[]{:S(2)}, u32[]{:S(2)}) collective-permute-start(f32[2,128]{0,1:T(8,128)S(1)} %multiply_bitcast_fusion.7), channel_id=1, source_target_pairs={{0,8},{4,12},{8,16},{12,20},{16,24},{20,28},{24,32},{28,36},{32,40... | collective-permute-start | bytes 3080 | tf_op jit(solution)/shard_map/ppermute | solution.py:12
  29.4 13.3 %collective-permute-start.5 = (f32[2,128]{0,1:T(8,128)S(1)}, f32[2,128]{0,1:T(8,128)S(1)}, u32[]{:S(2)}, u32[]{:S(2)}) collective-permute-start(f32[2,128]{0,1:T(8,128)S(1)} %multiply_bitcast_fusion.6), channel_id=1, source_target_pairs={{8,0},{12,4},{16,8},{20,12},{24,16},{28,20},{32,24},{36,28},{40,32... | collective-permute-start | bytes 3080 | tf_op jit(solution)/shard_map/ppermute | solution.py:12
  38.3 5.9 %copy-start.4 = (f32[2,768]{1,0:T(2,128)S(1)}, f32[2,768]{1,0:T(2,128)}, u32[]{:S(2)}) copy-start(f32[2,768]{1,0:T(2,128)} %param.11) | copy-start | bytes 18436
  38.3 5.9 %copy-start.1 = (bf16[24,768]{1,0:T(8,128)(2,1)S(1)}, bf16[24,768]{1,0:T(8,128)(2,1)}, u32[]{:S(2)}) copy-start(bf16[24,768]{1,0:T(8,128)(2,1)} %param.15) | copy-start | bytes 110596
  44.3 129.1 %copy-start.3 = (f32[2,768]{1,0:T(2,128)}, f32[2,768]{1,0:T(2,128)S(1)}, u32[]{:S(2)}) copy-start(f32[2,768]{1,0:T(2,128)S(1)} %subtract_multiply_fusion) | copy-start | bytes 18436
  174.9 1.8 copy-start.2
  181.0 15.9 %collective-permute-start.6 = (f32[2,128]{0,1:T(8,128)S(1)}, f32[2,128]{0,1:T(8,128)S(1)}, u32[]{:S(2)}, u32[]{:S(2)}) collective-permute-start(f32[2,128]{0,1:T(8,128)S(1)} %multiply_bitcast_fusion.5), channel_id=1, source_target_pairs={{0,1},{1,2},{2,3},{4,5},{5,6},{6,7},{8,9},{9,10},{10,11},{12,13},{... | collective-permute-start | bytes 3080 | tf_op jit(solution)/shard_map/ppermute | solution.py:12
  183.8 20.7 %collective-permute-start.7 = (f32[2,128]{0,1:T(8,128)S(1)}, f32[2,128]{0,1:T(8,128)S(1)}, u32[]{:S(2)}, u32[]{:S(2)}) collective-permute-start(f32[2,128]{0,1:T(8,128)S(1)} %multiply_bitcast_fusion.4), channel_id=1, source_target_pairs={{1,0},{2,1},{3,2},{5,4},{6,5},{7,6},{9,8},{10,9},{11,10},{13,12},{... | collective-permute-start | bytes 3080 | tf_op jit(solution)/shard_map/ppermute | solution.py:12
  187.0 19.0 %collective-permute-start.8 = (f32[2,128]{0,1:T(8,128)S(1)}, f32[2,128]{0,1:T(8,128)S(1)}, u32[]{:S(2)}, u32[]{:S(2)}) collective-permute-start(f32[2,128]{0,1:T(8,128)S(1)} %multiply_bitcast_fusion.3), channel_id=1, source_target_pairs={{0,4},{4,8},{8,12},{12,16},{16,20},{20,24},{24,28},{28,32},{32,36}... | collective-permute-start | bytes 3080 | tf_op jit(solution)/shard_map/ppermute | solution.py:12
  189.0 18.4 %collective-permute-start.9 = (f32[2,128]{0,1:T(8,128)S(1)}, f32[2,128]{0,1:T(8,128)S(1)}, u32[]{:S(2)}, u32[]{:S(2)}) collective-permute-start(f32[2,128]{0,1:T(8,128)S(1)} %multiply_bitcast_fusion.2), channel_id=1, source_target_pairs={{4,0},{8,4},{12,8},{16,12},{20,16},{24,20},{28,24},{32,28},{36,32}... | collective-permute-start | bytes 3080 | tf_op jit(solution)/shard_map/ppermute | solution.py:12
  194.9 14.0 %collective-permute-start.10 = (f32[2,128]{0,1:T(8,128)S(1)}, f32[2,128]{0,1:T(8,128)S(1)}, u32[]{:S(2)}, u32[]{:S(2)}) collective-permute-start(f32[2,128]{0,1:T(8,128)S(1)} %multiply_bitcast_fusion.1), channel_id=1, source_target_pairs={{0,8},{4,12},{8,16},{12,20},{16,24},{20,28},{24,32},{28,36},{32,40... | collective-permute-start | bytes 3080 | tf_op jit(solution)/shard_map/ppermute | solution.py:12
  196.9 13.4 %collective-permute-start.11 = (f32[2,128]{0,1:T(8,128)S(1)}, f32[2,128]{0,1:T(8,128)S(1)}, u32[]{:S(2)}, u32[]{:S(2)}) collective-permute-start(f32[2,128]{0,1:T(8,128)S(1)} %multiply_bitcast_fusion), channel_id=1, source_target_pairs={{8,0},{12,4},{16,8},{20,12},{24,16},{28,20},{32,24},{36,28},{40,32... | collective-permute-start | bytes 3080 | tf_op jit(solution)/shard_map/ppermute | solution.py:12
where the time goes:
time: 213 us; the launch traced here: 212 us
  blocking collectives  128 us (60%)
  starting transfers between devices  42.9 us (20%)
  other arithmetic  22.7 us (11%)
  local copies, waits for them, and re-layouts  11.1 us (5%)
  matrix products  5.44 us (3%)
    all_gather x1, blocking collectives, per_device(): lax.all_gather(coarse_in, ('dom', 'sub'), axis=1, tiled=True)  128 us
    ppermute x12, starting transfers between devices, passed_along(): return lax.ppermute(block, axis, route)  42.9 us
    scatter-add x12, other arithmetic, assemble(): summed = summed.at[:, in_rows[0, index_dir]].add(arrived)  17 us
    gather x12, local copies, waits for them, and re-layouts, assemble(): picked = terms[:, out_rows[0, index_dir]] * used[None, :]  7.74 us
  transfers between devices with their start and end apart: 12, of which 0 were waited for; matrix products, arithmetic and copies ran while one was open for 10% of the time, Pallas kernels for 0%

commit v1 on v0

v1 whole, which is shorter than its diff:
```python
import jax
import jax.numpy as jnp
from jax import lax
from jax.experimental import pallas as pl
from jax.experimental.pallas import tpu as pltpu
from jax.sharding import Mesh
from jax.sharding import PartitionSpec as P

Z, Y, C, X = 12, 8, 2, 4
PLANE = Y * C * X
N = 768
NV = 24
H = 128
EDGE = 256
F32, BF16 = jnp.float32, jnp.bfloat16
ALL = ("z", "y", "c", "x")
CHIPS = ("z", "y", "c")


def vmem(count):
    return [pl.BlockSpec(memory_space=pltpu.VMEM)] * count


def thirds(value):
    high = value.astype(BF16)
    rest = value - high.astype(F32)
    middle = rest.astype(BF16)
    low = (rest - middle.astype(F32)).astype(BF16)
    return jnp.concatenate([high, middle, low], axis=0)


def times_selection(value, selection):
    parts = jnp.dot(thirds(value), selection, preferred_element_type=F32)
    return parts[0:2] + parts[2:4] + parts[4:6]


def parities():
    chip = lax.axis_index("z") * Y + lax.axis_index("y")
    return lax.axis_index("x") % 2 == 0, chip % 2 == 0, lax.axis_index("c") == 0


def mask_of(orders_ref, width=N, first=0):
    return lax.broadcasted_iota(jnp.int32, (1, width), 1) + first < orders_ref[0, 0]


def send_messages(field, select, own_x, own_c, own_y):
    picked = times_selection(field, select)
    way = [picked[:, j * H : (j + 1) * H] for j in range(6)]
    even_x, even_chip, _ = parities()
    own_x[0] = jnp.where(even_x, way[0], way[1])
    own_x[1] = jnp.where(even_x, way[1], way[0])
    own_c[...] = picked[:, 2 * H : 4 * H]
    own_y[0] = jnp.where(even_chip, way[4], way[5])
    own_y[1] = jnp.where(even_chip, way[5], way[4])


def arrivals(xa, xb, pair, ya, yb):
    even_x, even_chip, first_core = parities()
    xa, xb, pair = xa[...], xb[...], pair[...]
    below = jnp.where(even_chip, yb[...], ya[...])
    above = jnp.where(even_chip, ya[...], yb[...])
    return jnp.concatenate(
        [
            jnp.where(even_x, xb, xa),
            jnp.where(even_x, xa, xb),
            jnp.where(first_core, below[:, H:], pair[:, :H]),
            jnp.where(first_core, pair[:, H:], above[:, H:]),
            below[:, :H],
            above[:, :H],
        ],
        axis=1,
    )


def first_kernel(start, stiff, orders, out_rows, counts, select, edge, own_x, own_c, own_y):
    rows = lax.broadcasted_iota(jnp.int32, (EDGE, H), 0)
    slots = lax.broadcasted_iota(jnp.int32, (1, H), 1)
    for j in range(6):
        listed = jnp.where(slots < counts[0, j], out_rows[0, j : j + 1, :], -1)
        select[:, j * H : (j + 1) * H] = (rows == listed).astype(F32).astype(BF16)
    iterate = jnp.where(mask_of(orders), start[...], 0.0)
    product = jnp.dot(iterate.astype(BF16), stiff[...], preferred_element_type=F32)
    edge[...] = product
    send_messages(product, select[...], own_x, own_c, own_y)


def rest_kernel(start, stiff_b, stiff_c, orders, in_rows, spread, rest):
    rows = lax.broadcasted_iota(jnp.int32, (EDGE, H), 0)
    for j in range(6):
        hit = (rows == in_rows[0, j : j + 1, :]).astype(F32)
        spread[j * H : (j + 1) * H, :] = hit.T.astype(BF16)
    iterate = jnp.where(mask_of(orders), start[...], 0.0).astype(BF16)
    rest[:, :EDGE] = jnp.dot(iterate, stiff_b[...], preferred_element_type=F32)
    rest[:, EDGE:] = jnp.dot(iterate, stiff_c[...], preferred_element_type=F32)


def residual_kernel(edge, rest, xa, xb, pair, ya, yb, spread, rhs, orders, basis, residual, rounded, rows):
    summed = edge[...] + times_selection(arrivals(xa, xb, pair, ya, yb), spread[...])
    total = jnp.concatenate([summed, rest[...]], axis=1)
    value = jnp.where(mask_of(orders), rhs[...] - total, 0.0)
    residual[...] = value
    low = value.astype(BF16)
    rounded[...] = low
    padded = jnp.concatenate([value, jnp.zeros((6, N), F32)], axis=0).astype(BF16)
    coarse = lax.dot_general(padded, basis[...], (((1,), (1,)), ((), ())), preferred_element_type=F32)
    place = lax.axis_index("y") * (C * X) + lax.axis_index("c") * X + lax.axis_index("x")
    shift = (24 * place) % 128
    turned = pltpu.roll(coarse, shift, 1)
    turned_far = pltpu.roll(turned, 64, 1)
    rows[...] = jnp.broadcast_to(turned[0:1] + turned_far[1:2], (PLANE, 128))


def repack_kernel(rows, out, packed):
    taken = rows[...]
    far = pltpu.roll(taken, 64, 1)
    place = lax.broadcasted_iota(jnp.int32, (PLANE, 128), 0)
    lane = lax.broadcasted_iota(jnp.int32, (PLANE, 128), 1)
    within = (lane - NV * place + NV * PLANE) & 127
    row = jnp.where(within < NV, (NV * (place & 15) + within) >> 7, -1)
    for load, field in enumerate((taken, far)):
        for r in range(3):
            kept = jnp.where(row == r, field, 0.0)
            for group in range(4):
                packed[load * 12 + group * 3 + r : load * 12 + group * 3 + r + 1, :] = jnp.sum(
                    kept[group * 16 : (group + 1) * 16], axis=0, keepdims=True
                )
    whole = packed[...]
    for z in range(Z):
        out[z] = whole


def local_kernel(rounded, inverse, local):
    local[...] = jnp.dot(rounded[...], inverse[...], preferred_element_type=F32)


def coarse_kernel(gathered, inverse, basis, weights, orders, local, select, correction, own_x, own_c, own_y):
    sums = [[jnp.zeros((NV, 128), F32) for _ in range(2)] for _ in range(2)]
    for t in range(Z * 12):
        z, r = divmod(t, 12)
        block = inverse[:, t * 128 : (t + 1) * 128]
        for load in range(2):
            sums[load][t % 2] += block * gathered[z, load * 12 + r : load * 12 + r + 1, :]
    vectors = basis[...].astype(F32)
    fixes = []
    for load in range(2):
        coarse = jnp.sum(sums[load][0] + sums[load][1], axis=1, keepdims=True)
        coarse = coarse.astype(BF16).astype(F32)
        fixes.append(jnp.sum(vectors * coarse, axis=0, keepdims=True))
    fix = jnp.concatenate(fixes, axis=0)
    value = jnp.where(mask_of(orders), weights[...] * (local[...] + fix), 0.0)
    correction[...] = value
    send_messages(value[:, :EDGE], select[...], own_x, own_c, own_y)


def last_kernel(start, orders, correction, xa, xb, pair, ya, yb, spread, solved):
    arrived = times_selection(arrivals(xa, xb, pair, ya, yb), spread[...])
    value = jnp.where(mask_of(orders), start[...], 0.0) + correction[...]
    solved[...] = value
    solved[:, :EDGE] = value[:, :EDGE] + arrived


def message_shapes():
    return [
        jax.ShapeDtypeStruct((2, 2, H), F32),
        jax.ShapeDtypeStruct((2, 2 * H), F32),
        jax.ShapeDtypeStruct((2, 2, H), F32),
    ]


def exchange(own_x, own_c, own_y):
    chips = Z * Y
    pairs_c = [(d, d ^ 1) for d in range(C)]
    even_x = [(d, d ^ 1) for d in range(X)]
    odd_x = [(1, 2), (2, 1)]
    even_chips = [(2 * q + c, 2 * (q ^ 1) + c) for q in range(chips) for c in range(C)]
    odd_chips = []
    for q in range(1, chips - 1, 2):
        for c in range(C):
            odd_chips += [(2 * q + c, 2 * q + 2 + c), (2 * q + 2 + c, 2 * q + c)]
    pair = lax.ppermute(own_c, "c", pairs_c)
    xa = lax.ppermute(own_x[0], "x", even_x)
    xb = lax.ppermute(own_x[1], "x", odd_x)
    even_chip = parities()[1]
    up, down = pair[:, :H], pair[:, H:]
    ya = jnp.concatenate([own_y[0], jnp.where(even_chip, up, down)], axis=1)
    yb = jnp.concatenate([own_y[1], jnp.where(even_chip, down, up)], axis=1)
    ya = lax.ppermute(ya, CHIPS, even_chips)
    yb = lax.ppermute(yb, CHIPS, odd_chips)
    return xa, xb, pair, ya, yb


def per_device(
    rhs, start, stiffness, local_inverse, basis, weights, coarse_inverse, orders, out_rows, out_counts, in_rows
):
    smem = pl.BlockSpec(memory_space=pltpu.SMEM)
    orders = orders.reshape(1, 1)
    whole = lambda shape: pl.BlockSpec(shape, lambda i: (0,) * len(shape))
    smem_grid = pl.BlockSpec(memory_space=pltpu.SMEM)
    select, edge, own_x, own_c, own_y = pl.pallas_call(
        first_kernel,
        grid=(1,),
        in_specs=[whole((2, N)), whole((N, EDGE)), smem_grid, whole((1, 6, H)), smem_grid],
        out_specs=[whole((EDGE, 6 * H)), whole((2, EDGE)), whole((2, 2, H)), whole((2, 2 * H)), whole((2, 2, H))],
        out_shape=[jax.ShapeDtypeStruct((EDGE, 6 * H), BF16), jax.ShapeDtypeStruct((2, EDGE), F32)]
        + message_shapes(),
    )(start, stiffness, orders, out_rows, out_counts)
    spread, rest = pl.pallas_call(
        rest_kernel,
        grid=(1,),
        in_specs=[
            whole((2, N)),
            pl.BlockSpec((N, EDGE), lambda i: (0, 1)),
            pl.BlockSpec((N, EDGE), lambda i: (0, 2)),
            smem_grid,
            whole((1, 6, H)),
        ],
        out_specs=[whole((6 * H, EDGE)), whole((2, 2 * EDGE))],
        out_shape=[jax.ShapeDtypeStruct((6 * H, EDGE), BF16), jax.ShapeDtypeStruct((2, 2 * EDGE), F32)],
    )(start, stiffness, stiffness, orders, in_rows)
    basis_rows = jnp.pad(basis, ((0, 128 - NV), (0, 0)))
    arrived = exchange(own_x, own_c, own_y)
    residual, rounded, rows = pl.pallas_call(
        residual_kernel,
        in_specs=vmem(9) + [smem] + vmem(1),
        out_specs=vmem(3),
        out_shape=[
            jax.ShapeDtypeStruct((2, N), F32),
            jax.ShapeDtypeStruct((2, N), BF16),
            jax.ShapeDtypeStruct((PLANE, 128), F32),
        ],
    )(edge, rest, *arrived, spread, rhs, orders, basis_rows)
    rows = lax.all_to_all(rows.reshape(PLANE, 1, 128), ("y", "c", "x"), 0, 0).reshape(PLANE, 128)
    local = pl.pallas_call(
        local_kernel,
        in_specs=vmem(2),
        out_specs=vmem(1)[0],
        out_shape=jax.ShapeDtypeStruct((2, N), F32),
    )(rounded, local_inverse)
    gathered = pl.pallas_call(
        repack_kernel,
        in_specs=vmem(1),
        out_specs=vmem(1)[0],
        out_shape=jax.ShapeDtypeStruct((Z, 2 * 12, 128), F32),
        scratch_shapes=[pltpu.VMEM((2 * 12, 128), F32)],
    )(rows)
    gathered = lax.all_to_all(gathered, "z", 0, 0)
    correction, own_x, own_c, own_y = pl.pallas_call(
        coarse_kernel,
        in_specs=vmem(4) + [smem] + vmem(2),
        out_specs=vmem(4),
        out_shape=[jax.ShapeDtypeStruct((2, N), F32)] + message_shapes(),
    )(gathered, coarse_inverse, basis, weights.reshape(1, N), orders, local, select)
    arrived = exchange(own_x, own_c, own_y)
    solved = pl.pallas_call(
        last_kernel,
        in_specs=vmem(1) + [smem] + vmem(7),
        out_specs=vmem(1)[0],
        out_shape=jax.ShapeDtypeStruct((2, N), F32),
    )(start, orders, correction, *arrived, spread)
    return solved, residual


def solution(mesh):
    fine = Mesh(mesh.devices.reshape(Z, Y, C, X), ALL)
    return jax.shard_map(
        per_device,
        mesh=fine,
        in_specs=(
            P(None, ALL),
            P(None, ALL),
            P(ALL, None),
            P(ALL, None),
            P(None, ALL),
            P(ALL),
            P(ALL, None),
            P(ALL),
            P(ALL, None, None),
            P(ALL, None),
            P(ALL, None, None),
        ),
        out_specs=(P(None, ALL), P(None, ALL)),
        check_vma=False,
    )
```

time: 213 us -> 98.8 us (0.46)
  the two profiles are of different devices: /device:TPU:66 before, /device:TPU:2 now
where the time goes in v1:
time: 98.8 us; the launch traced here: 98 us
  starting transfers between devices  43.5 us (44%)
  blocking collectives  16 us (16%)
  Pallas kernels  14.7 us (15%)
  waiting for transfers between devices  14.5 us (15%)
  local copies, waits for them, and re-layouts  7.74 us (8%)
  between operations  1.5 us (2%)
    all_to_all x1, blocking collectives, per_device(): lax.all_to_all(rows.reshape(PLANE, 1, 128), ('y', 'c', 'x'), 0, 0)  16 us
    all_to_all x1, starting transfers between devices, per_device(): gathered = lax.all_to_all(gathered, 'z', 0, 0)  12.8 us
    ppermute x2, starting transfers between devices, exchange(): ya = lax.ppermute(ya, CHIPS, even_chips)  10.8 us
    ppermute x2, starting transfers between devices, exchange(): xa = lax.ppermute(own_x[0], 'x', even_x)  10.6 us
    all_to_all x1, waiting for transfers between devices, per_device(): gathered = lax.all_to_all(gathered, 'z', 0, 0)  9.93 us
    ppermute x2, starting transfers between devices, exchange(): xb = lax.ppermute(own_x[1], 'x', odd_x)  4.19 us
    ppermute x2, starting transfers between devices, exchange(): pair = lax.ppermute(own_c, 'c', pairs_c)  3.82 us
    unnamed x30, local copies, waits for them, and re-layouts  3.72 us
  transfers between devices with their start and end apart: 11, of which 5 were waited for; matrix products, arithmetic and copies ran while one was open for 5% of the time, Pallas kernels for 4%

profile of v1, /device:TPU:2, one launch (start us, length us, event | category | flops | bytes accessed | tf_op | source)
XLA Modules:
  0.0 98.0 jit_solution(14311809328300466382)
XLA Ops:
  0.6 0.0 copy-start.5
  1.3 1.3 %copy.15.out_rows = s32[1,6,128]{2,1,0:T(8,128)} copy(s32[1,6,128]{2,0,1:T(1,128)} %param.19) | data formatting | bytes 6144 | tf_op args[8]
  2.6 2.0 %shard_map.122 = (bf16[256,768]{1,0:T(8,128)(2,1)}, f32[2,256]{1,0:T(2,128)}, f32[2,2,128]{2,1,0:T(2,128)}, f32[2,256]{1,0:T(2,128)}, f32[2,2,128]{2,1,0:T(2,128)}) custom-call(f32[2,768]{1,0:T(2,128)} %start.5, bf16[768,768]{1,0:T(8,128)(2,1)} %stiff_c.1, s32[1,1]{1,0:T(1,128)} %bitcast.21.orders, s32[1,6,128]{2,1,0:T(8,128)} %copy.15.out_rows, s32[1,6]{1,0:T(1,128)} %counts.1), custom_call_target="tpu_custom_call" | custom-call | tf_op jit(solution)/shard_map/pallas_call | solution.py:199
  4.6 1.9 %collective-permute-start.2 = (f32[2,256]{1,0:T(2,128)}, f32[2,256]{1,0:T(2,128)S(1)}, u32[]{:S(2)}, u32[]{:S(2)}) collective-permute-start(f32[2,256]{1,0:T(2,128)} %get-tuple-element.19), channel_id=1, source_target_pairs={{0,4},{4,0},{1,5},{5,1},{2,6},{6,2},{3,7},{7,3},{8,12},{12,8},{9,1... | collective-permute-start | bytes 6152 | tf_op jit(solution)/shard_map/ppermute | solution.py:180
  6.5 0.7 slice_bitcast_fusion.4
  7.2 0.7 collective-permute-done.2.pair
  7.8 0.0 copy-start.2
  7.9 0.7 collective-permute-start.4
  8.5 6.3 %collective-permute-start.3 = (f32[2,256]{1,0:T(2,128)S(1)}, f32[2,256]{1,0:T(2,128)S(1)}, u32[]{:S(2)}, u32[]{:S(2)}) collective-permute-start(f32[2,256]{1,0:T(2,128)S(1)} %pad_maximum_fusion), channel_id=1, source_target_pairs={{0,8},{4,12},{8,0},{12,4},{16,24},{20,28},{24,16},{28,20},{32,40},... | collective-permute-start | bytes 6152 | tf_op jit(solution)/shard_map/ppermute | solution.py:187
  14.9 0.7 slice_bitcast_fusion.6
  15.6 7.0 %collective-permute-start = (f32[2,128]{1,0:T(2,128)S(1)}, f32[2,128]{1,0:T(2,128)S(1)}, u32[]{:S(2)}, u32[]{:S(2)}) collective-permute-start(f32[2,128]{1,0:T(2,128)S(1)} %get-tuple-element.41), channel_id=1, source_target_pairs={{0,1},{1,0},{2,3},{3,2},{4,5},{5,4},{6,7},{7,6},{8,9},{9,8},{10,11... | collective-permute-start | bytes 3080 | tf_op jit(solution)/shard_map/ppermute | solution.py:181
  22.6 1.9 %collective-permute-start.1 = (f32[2,128]{1,0:T(2,128)S(1)}, f32[2,128]{1,0:T(2,128)S(1)}, u32[]{:S(2)}, u32[]{:S(2)}) collective-permute-start(f32[2,128]{1,0:T(2,128)S(1)} %get-tuple-element.40), channel_id=1, source_target_pairs={{1,2},{2,1},{5,6},{6,5},{9,10},{10,9},{13,14},{14,13},{17,18},{18,... | collective-permute-start | bytes 3080 | tf_op jit(solution)/shard_map/ppermute | solution.py:182
  24.5 0.0 copy-done.5
  24.5 0.6 copy.16.in_rows
  25.1 0.0 copy-start.1
  25.1 2.1 %shard_map.123 = (bf16[768,256]{1,0:T(8,128)(2,1)}, f32[2,512]{1,0:T(2,128)}) custom-call(f32[2,768]{1,0:T(2,128)} %start.5, bf16[768,768]{1,0:T(8,128)(2,1)} %stiff_c.1, bf16[768,768]{1,0:T(8,128)(2,1)} %stiff_c.1, s32[1,1]{1,0:T(1,128)} %bitcast.22.orders, s32[1,6,128]{2,1,0:T(8,128)} %copy.16.in_rows), custom_call_target="tpu_custom_call" | custom-call | tf_op jit(solution)/shard_map/pallas_call | solution.py:207
  27.2 0.0 copy-done.2
  27.2 0.0 copy-done.1
  27.2 0.0 copy-start.4
  27.3 0.7 pad.4.basis
  28.0 0.0 collective-permute-done.xa
  28.0 0.0 copy-start.10
  28.0 0.1 collective-permute-done.1.xb
  28.1 0.0 copy-start.11
  28.1 0.0 collective-permute-done.4.yb
  28.1 0.0 copy-start.6
  28.1 0.0 collective-permute-done.3.ya
  28.1 0.0 copy-start.7
  28.1 0.5 copy-done.10
  28.5 0.1 copy-done.11
  28.6 0.0 copy-done.6
  28.7 0.0 copy-done.7
  28.7 2.3 %shard_map.124 = (f32[2,768]{1,0:T(2,128)}, bf16[2,768]{1,0:T(2,128)(2,1)}, f32[64,128]{1,0:T(8,128)}) custom-call(f32[2,256]{1,0:T(2,128)} %get-tuple-element.16.edge, f32[2,512]{1,0:T(2,128)} %get-tuple-element.17.rest, f32[2,128]{1,0:T(2,128)} %copy-done.10, f32[2,128]{1,0:T(2,128)} %copy-done.11, f32[2,256]{1,0:T(2,128)} %copy-done.2, ...), custom_call_target="tpu_custom_call" | custom-call | tf_op jit(solution)/shard_map/pallas_call | solution.py:222
  30.9 16.0 %all_to_all.10 = f32[64,1,128]{2,1,0:T(1,128)} all-to-all(f32[64,1,128]{2,1,0:T(1,128)} %bitcast.27), channel_id=1, replica_groups=mesh['z'=12,'y'=8,'c'=2,'x'=4] {'y','c','x'}, dimensions={0} | all-to-all | bytes 65536 | tf_op jit(solution)/shard_map/all_to_all | solution.py:232
  46.9 1.5 %shard_map.125 = f32[12,24,128]{2,1,0:T(8,128)} custom-call(f32[64,128]{1,0:T(8,128)} %bitcast.26), custom_call_target="tpu_custom_call" | custom-call | tf_op jit(solution)/shard_map/pallas_call | solution.py:239
  48.4 12.8 %all-to-all-start.1 = ((f32[12,24,128]{2,1,0:T(8,128)}), f32[12,24,128]{2,1,0:T(8,128)S(1)}, u32[]{:S(2)}, u32[]{:S(2)}) async-start(f32[12,24,128]{2,1,0:T(8,128)} %shard_map.125), calls=%async_computation.1 | async-start | bytes 294912 | tf_op jit(solution)/shard_map/all_to_all | solution.py:246
  61.2 0.0 copy-done.4
  61.2 0.6 reshape.19.weights
  61.8 2.2 %shard_map.126.local = f32[2,768]{1,0:T(2,128)} custom-call(bf16[2,768]{1,0:T(2,128)(2,1)} %get-tuple-element.23.rounded, bf16[768,768]{1,0:T(8,128)(2,1)} %inverse.2), custom_call_target="tpu_custom_call" | custom-call | tf_op jit(solution)/shard_map/pallas_call | solution.py:233
  64.0 9.9 %all-to-all-done.1.gathered = f32[12,24,128]{2,1,0:T(8,128)S(1)} async-done(((f32[12,24,128]{2,1,0:T(8,128)}), f32[12,24,128]{2,1,0:T(8,128)S(1)}, u32[]{:S(2)}, u32[]{:S(2)}) %all-to-all-start.1) | async-done | bytes 147488 | tf_op jit(solution)/shard_map/all_to_all | solution.py:246
  73.9 0.0 copy-start
  73.9 0.7 copy-done
  74.6 2.8 %shard_map.127 = (f32[2,768]{1,0:T(2,128)}, f32[2,2,128]{2,1,0:T(2,128)}, f32[2,256]{1,0:T(2,128)}, f32[2,2,128]{2,1,0:T(2,128)}) custom-call(f32[12,24,128]{2,1,0:T(8,128)} %copy-done, f32[24,18432]{1,0:T(8,128)} %inverse.3, bf16[24,768]{1,0:T(8,128)(2,1)} %basis.1, f32[1,768]{1,0:T(1,128)} %reshape.19.weights, s32[1,1]{1,0:T(1,128)} %bitcast.24.orders, ...), custom_call_target="tpu_custom_call" | custom-call | tf_op jit(solution)/shard_map/pallas_call | solution.py:247
  77.4 1.9 %collective-permute-start.7 = (f32[2,256]{1,0:T(2,128)}, f32[2,256]{1,0:T(2,128)S(1)}, u32[]{:S(2)}, u32[]{:S(2)}) collective-permute-start(f32[2,256]{1,0:T(2,128)} %get-tuple-element.27), channel_id=1, source_target_pairs={{0,4},{4,0},{1,5},{5,1},{2,6},{6,2},{3,7},{7,3},{8,12},{12,8},{9,1... | collective-permute-start | bytes 6152 | tf_op jit(solution)/shard_map/ppermute | solution.py:180
  79.3 0.7 slice_bitcast_fusion
  80.0 0.7 collective-permute-done.7.pair
  80.6 0.0 copy-start.3
  80.6 0.7 collective-permute-start.9
  81.3 4.5 %collective-permute-start.8 = (f32[2,256]{1,0:T(2,128)S(1)}, f32[2,256]{1,0:T(2,128)S(1)}, u32[]{:S(2)}, u32[]{:S(2)}) collective-permute-start(f32[2,256]{1,0:T(2,128)S(1)} %pad_maximum_fusion.2), channel_id=1, source_target_pairs={{0,8},{4,12},{8,0},{12,4},{16,24},{20,28},{24,16},{28,20},{32,40},... | collective-permute-start | bytes 6152 | tf_op jit(solution)/shard_map/ppermute | solution.py:187
  85.8 0.7 slice_bitcast_fusion.2
  86.5 3.5 %collective-permute-start.5 = (f32[2,128]{1,0:T(2,128)S(1)}, f32[2,128]{1,0:T(2,128)S(1)}, u32[]{:S(2)}, u32[]{:S(2)}) collective-permute-start(f32[2,128]{1,0:T(2,128)S(1)} %get-tuple-element.35), channel_id=1, source_target_pairs={{0,1},{1,0},{2,3},{3,2},{4,5},{5,4},{6,7},{7,6},{8,9},{9,8},{10,11... | collective-permute-start | bytes 3080 | tf_op jit(solution)/shard_map/ppermute | solution.py:181
  90.1 2.3 %collective-permute-start.6 = (f32[2,128]{1,0:T(2,128)S(1)}, f32[2,128]{1,0:T(2,128)S(1)}, u32[]{:S(2)}, u32[]{:S(2)}) collective-permute-start(f32[2,128]{1,0:T(2,128)S(1)} %get-tuple-element.34), channel_id=1, source_target_pairs={{1,2},{2,1},{5,6},{6,5},{9,10},{10,9},{13,14},{14,13},{17,18},{18,... | collective-permute-start | bytes 3080 | tf_op jit(solution)/shard_map/ppermute | solution.py:182
  92.3 0.0 collective-permute-done.5.xa
  92.3 0.0 copy-start.12
  92.4 3.2 %collective-permute-done.6.xb = f32[2,128]{1,0:T(2,128)S(1)} collective-permute-done((f32[2,128]{1,0:T(2,128)S(1)}, f32[2,128]{1,0:T(2,128)S(1)}, u32[]{:S(2)}, u32[]{:S(2)}) %collective-permute-start.6) | collective-permute-done | bytes 1056 | tf_op jit(solution)/shard_map/ppermute | solution.py:182
  95.5 0.0 collective-permute-done.9.yb
  95.5 0.0 collective-permute-done.8.ya
  95.5 0.0 copy-start.9
  95.5 0.0 copy-done.3
  95.6 0.0 copy-done.12
  95.6 0.5 copy-done.13
  96.1 0.0 copy-done.8
  96.1 0.0 copy-done.9
  96.1 1.8 %shard_map.128 = f32[2,768]{1,0:T(2,128)} custom-call(f32[2,768]{1,0:T(2,128)} %start.5, s32[1,1]{1,0:T(1,128)} %bitcast.25.orders, f32[2,768]{1,0:T(2,128)} %get-tuple-element.25.correction, f32[2,128]{1,0:T(2,128)} %copy-done.12, f32[2,128]{1,0:T(2,128)} %copy-done.13, f32[2,256]{1,0:T(2,128)} %copy-done.3, f32[2,256]{1,0:T(2,128)} %copy-done.9, ...), custom_call_target="tpu_custom_call" | custom-call | tf_op jit(solution)/shard_map/pallas_call | solution.py:254
  (8 shorter events, 0.0 us)
Async XLA Ops:
  0.6 23.9 %copy-start.5 = (s32[1,6,128]{2,0,1:T(1,128)S(1)}, s32[1,6,128]{2,0,1:T(1,128)}, u32[]{:S(2)}) copy-start(s32[1,6,128]{2,0,1:T(1,128)} %param.21) | copy-start | bytes 9220
  4.6 3.3 %collective-permute-start.2 = (f32[2,256]{1,0:T(2,128)}, f32[2,256]{1,0:T(2,128)S(1)}, u32[]{:S(2)}, u32[]{:S(2)}) collective-permute-start(f32[2,256]{1,0:T(2,128)} %get-tuple-element.19), channel_id=1, source_target_pairs={{0,4},{4,0},{1,5},{5,1},{2,6},{6,2},{3,7},{7,3},{8,12},{12,8},{9,1... | collective-permute-start | bytes 6152 | tf_op jit(solution)/shard_map/ppermute | solution.py:180
  7.8 19.4 %copy-start.2 = (f32[2,256]{1,0:T(2,128)}, f32[2,256]{1,0:T(2,128)S(1)}, u32[]{:S(2)}) copy-start(f32[2,256]{1,0:T(2,128)S(1)} %collective-permute-done.2.pair) | copy-start | bytes 6148
  7.9 20.2 %collective-permute-start.4 = (f32[2,256]{1,0:T(2,128)S(1)}, f32[2,256]{1,0:T(2,128)S(1)}, u32[]{:S(2)}, u32[]{:S(2)}) collective-permute-start(f32[2,256]{1,0:T(2,128)S(1)} %pad_maximum_fusion.1), channel_id=1, source_target_pairs={{8,16},{16,8},{12,20},{20,12},{24,32},{32,24},{28,36},{36,28},{40,... | collective-permute-start | bytes 6152 | tf_op jit(solution)/shard_map/ppermute | solution.py:188
  8.5 19.5 %collective-permute-start.3 = (f32[2,256]{1,0:T(2,128)S(1)}, f32[2,256]{1,0:T(2,128)S(1)}, u32[]{:S(2)}, u32[]{:S(2)}) collective-permute-start(f32[2,256]{1,0:T(2,128)S(1)} %pad_maximum_fusion), channel_id=1, source_target_pairs={{0,8},{4,12},{8,0},{12,4},{16,24},{20,28},{24,16},{28,20},{32,40},... | collective-permute-start | bytes 6152 | tf_op jit(solution)/shard_map/ppermute | solution.py:187
  15.6 12.4 %collective-permute-start = (f32[2,128]{1,0:T(2,128)S(1)}, f32[2,128]{1,0:T(2,128)S(1)}, u32[]{:S(2)}, u32[]{:S(2)}) collective-permute-start(f32[2,128]{1,0:T(2,128)S(1)} %get-tuple-element.41), channel_id=1, source_target_pairs={{0,1},{1,0},{2,3},{3,2},{4,5},{5,4},{6,7},{7,6},{8,9},{9,8},{10,11... | collective-permute-start | bytes 3080 | tf_op jit(solution)/shard_map/ppermute | solution.py:181
  22.6 5.5 %collective-permute-start.1 = (f32[2,128]{1,0:T(2,128)S(1)}, f32[2,128]{1,0:T(2,128)S(1)}, u32[]{:S(2)}, u32[]{:S(2)}) collective-permute-start(f32[2,128]{1,0:T(2,128)S(1)} %get-tuple-element.40), channel_id=1, source_target_pairs={{1,2},{2,1},{5,6},{6,5},{9,10},{10,9},{13,14},{14,13},{17,18},{18,... | collective-permute-start | bytes 3080 | tf_op jit(solution)/shard_map/ppermute | solution.py:182
  25.1 2.1 %copy-start.1 = (bf16[24,768]{1,0:T(8,128)(2,1)S(1)}, bf16[24,768]{1,0:T(8,128)(2,1)}, u32[]{:S(2)}) copy-start(bf16[24,768]{1,0:T(8,128)(2,1)} %basis.1) | copy-start | bytes 110596
  27.2 34.0 %copy-start.4 = (f32[768]{0:T(1024)S(1)}, f32[768]{0:T(1024)}, u32[]{:S(2)}) copy-start(f32[768]{0:T(1024)} %param.16) | copy-start | bytes 9220
  28.0 0.6 copy-start.10
  28.1 0.6 copy-start.11
  28.1 0.6 copy-start.6
  28.1 0.6 copy-start.7
  48.4 25.5 %all-to-all-start.1 = ((f32[12,24,128]{2,1,0:T(8,128)}), f32[12,24,128]{2,1,0:T(8,128)S(1)}, u32[]{:S(2)}, u32[]{:S(2)}) async-start(f32[12,24,128]{2,1,0:T(8,128)} %shard_map.125), calls=%async_computation.1 | async-start | bytes 294912 | tf_op jit(solution)/shard_map/all_to_all | solution.py:246
  73.9 0.7 copy-start
  77.4 3.3 %collective-permute-start.7 = (f32[2,256]{1,0:T(2,128)}, f32[2,256]{1,0:T(2,128)S(1)}, u32[]{:S(2)}, u32[]{:S(2)}) collective-permute-start(f32[2,256]{1,0:T(2,128)} %get-tuple-element.27), channel_id=1, source_target_pairs={{0,4},{4,0},{1,5},{5,1},{2,6},{6,2},{3,7},{7,3},{8,12},{12,8},{9,1... | collective-permute-start | bytes 6152 | tf_op jit(solution)/shard_map/ppermute | solution.py:180
  80.6 14.9 %copy-start.3 = (f32[2,256]{1,0:T(2,128)}, f32[2,256]{1,0:T(2,128)S(1)}, u32[]{:S(2)}) copy-start(f32[2,256]{1,0:T(2,128)S(1)} %collective-permute-done.7.pair) | copy-start | bytes 6148
  80.6 14.9 %collective-permute-start.9 = (f32[2,256]{1,0:T(2,128)S(1)}, f32[2,256]{1,0:T(2,128)S(1)}, u32[]{:S(2)}, u32[]{:S(2)}) collective-permute-start(f32[2,256]{1,0:T(2,128)S(1)} %pad_maximum_fusion.3), channel_id=1, source_target_pairs={{8,16},{16,8},{12,20},{20,12},{24,32},{32,24},{28,36},{36,28},{40,... | collective-permute-start | bytes 6152 | tf_op jit(solution)/shard_map/ppermute | solution.py:188
  81.3 14.2 %collective-permute-start.8 = (f32[2,256]{1,0:T(2,128)S(1)}, f32[2,256]{1,0:T(2,128)S(1)}, u32[]{:S(2)}, u32[]{:S(2)}) collective-permute-start(f32[2,256]{1,0:T(2,128)S(1)} %pad_maximum_fusion.2), channel_id=1, source_target_pairs={{0,8},{4,12},{8,0},{12,4},{16,24},{20,28},{24,16},{28,20},{32,40},... | collective-permute-start | bytes 6152 | tf_op jit(solution)/shard_map/ppermute | solution.py:187
  86.5 5.8 %collective-permute-start.5 = (f32[2,128]{1,0:T(2,128)S(1)}, f32[2,128]{1,0:T(2,128)S(1)}, u32[]{:S(2)}, u32[]{:S(2)}) collective-permute-start(f32[2,128]{1,0:T(2,128)S(1)} %get-tuple-element.35), channel_id=1, source_target_pairs={{0,1},{1,0},{2,3},{3,2},{4,5},{5,4},{6,7},{7,6},{8,9},{9,8},{10,11... | collective-permute-start | bytes 3080 | tf_op jit(solution)/shard_map/ppermute | solution.py:181
  90.1 5.5 %collective-permute-start.6 = (f32[2,128]{1,0:T(2,128)S(1)}, f32[2,128]{1,0:T(2,128)S(1)}, u32[]{:S(2)}, u32[]{:S(2)}) collective-permute-start(f32[2,128]{1,0:T(2,128)S(1)} %get-tuple-element.34), channel_id=1, source_target_pairs={{1,2},{2,1},{5,6},{6,5},{9,10},{10,9},{13,14},{14,13},{17,18},{18,... | collective-permute-start | bytes 3080 | tf_op jit(solution)/shard_map/ppermute | solution.py:182
  92.3 3.2 %copy-start.12 = (f32[2,128]{1,0:T(2,128)}, f32[2,128]{1,0:T(2,128)S(1)}, u32[]{:S(2)}) copy-start(f32[2,128]{1,0:T(2,128)S(1)} %collective-permute-done.5.xa) | copy-start | bytes 3076
  95.5 0.6 copy-start.13
  95.5 0.6 copy-start.8
  95.5 0.6 copy-start.9

commit v2 on v1

v2 whole, which is shorter than its diff:
```python
import jax
import jax.numpy as jnp
from jax import lax
from jax.experimental import pallas as pl
from jax.experimental.pallas import tpu as pltpu
from jax.sharding import Mesh
from jax.sharding import PartitionSpec as P

Z, Y, C, X = 12, 8, 2, 4
PLANE = Y * C * X
N = 768
NV = 24
H = 128
EDGE = 256
F32, BF16 = jnp.float32, jnp.bfloat16
ALL = ("z", "y", "c", "x")
CHIPS = ("z", "y", "c")
LEAN = pltpu.CompilerParams(vmem_limit_bytes=8 << 20)


def on_chip(kernel, out_shape, args, scalars=(), far=(), scratch=()):
    def space(i):
        return pltpu.SMEM if i in scalars else pltpu.HBM if i in far else pltpu.VMEM

    specs = [pl.BlockSpec(memory_space=space(i)) for i in range(len(args))]
    args = [a if i in scalars else pltpu.with_memory_space_constraint(a, space(i)) for i, a in enumerate(args)]
    return pl.pallas_call(
        kernel,
        in_specs=specs,
        out_specs=[pl.BlockSpec(memory_space=pltpu.VMEM)] * len(out_shape),
        out_shape=[pltpu.VMEM(shape, dtype) for shape, dtype in out_shape],
        scratch_shapes=list(scratch),
        compiler_params=LEAN,
    )(*args)


def thirds(value):
    high = value.astype(BF16)
    rest = value - high.astype(F32)
    middle = rest.astype(BF16)
    low = (rest - middle.astype(F32)).astype(BF16)
    return jnp.concatenate([high, middle, low], axis=0)


def times_selection(value, selection):
    parts = jnp.dot(thirds(value), selection, preferred_element_type=F32)
    return parts[0:2] + parts[2:4] + parts[4:6]


def parities():
    chip = lax.axis_index("z") * Y + lax.axis_index("y")
    return lax.axis_index("x") % 2 == 0, chip % 2 == 0, lax.axis_index("c") == 0


def mask_of(orders_ref, width=N, first=0):
    return lax.broadcasted_iota(jnp.int32, (1, width), 1) + first < orders_ref[0, 0]


def send_messages(field, select, own_xa, own_xb, own_c, own_ya, own_yb):
    picked = times_selection(field, select)
    way = [picked[:, j * H : (j + 1) * H] for j in range(6)]
    even_x, even_chip, _ = parities()
    own_xa[...] = jnp.where(even_x, way[0], way[1])
    own_xb[...] = jnp.where(even_x, way[1], way[0])
    own_c[...] = picked[:, 2 * H : 4 * H]
    own_ya[...] = jnp.where(even_chip, way[4], way[5])
    own_yb[...] = jnp.where(even_chip, way[5], way[4])


def arrivals(xa, xb, pair, ya, yb):
    even_x, even_chip, first_core = parities()
    xa, xb, pair = xa[...], xb[...], pair[...]
    below = jnp.where(even_chip, yb[...], ya[...])
    above = jnp.where(even_chip, ya[...], yb[...])
    return jnp.concatenate(
        [
            jnp.where(even_x, xb, xa),
            jnp.where(even_x, xa, xb),
            jnp.where(first_core, below[:, H:], pair[:, :H]),
            jnp.where(first_core, pair[:, H:], above[:, H:]),
            below[:, :H],
            above[:, :H],
        ],
        axis=1,
    )


def first_kernel(start, stiff, orders, out_rows, counts, select, edge, own_xa, own_xb, own_c, own_ya, own_yb, columns, fields, listing, done):
    copies = [
        pltpu.make_async_copy(out_rows, listing, done.at[0]),
        pltpu.make_async_copy(start, fields, done.at[1]),
        pltpu.make_async_copy(stiff.at[:, pl.ds(0, EDGE)], columns, done.at[2]),
    ]
    for copy in copies:
        copy.start()
    copies[0].wait()
    rows = lax.broadcasted_iota(jnp.int32, (EDGE, H), 0)
    slots = lax.broadcasted_iota(jnp.int32, (1, H), 1)
    for j in range(6):
        listed = jnp.where(slots < counts[0, j], listing[j], -1)
        select[:, j * H : (j + 1) * H] = (rows == listed).astype(F32).astype(BF16)
    copies[1].wait()
    iterate = jnp.where(mask_of(orders), fields[...], 0.0).astype(BF16)
    copies[2].wait()
    product = jnp.dot(iterate, columns[...], preferred_element_type=F32)
    edge[...] = product
    send_messages(product, select[...], own_xa, own_xb, own_c, own_ya, own_yb)


def rest_kernel(start, stiff, orders, in_rows, spread, rest, columns, fields, listing, done):
    copies = [
        pltpu.make_async_copy(in_rows, listing, done.at[0]),
        pltpu.make_async_copy(start, fields, done.at[1]),
        pltpu.make_async_copy(stiff.at[:, pl.ds(EDGE, N - EDGE)], columns, done.at[2]),
    ]
    for copy in copies:
        copy.start()
    copies[0].wait()
    rows = lax.broadcasted_iota(jnp.int32, (EDGE, H), 0)
    for j in range(6):
        hit = (rows == listing[j]).astype(F32)
        spread[j * H : (j + 1) * H, :] = hit.T.astype(BF16)
    copies[1].wait()
    iterate = jnp.where(mask_of(orders), fields[...], 0.0).astype(BF16)
    copies[2].wait()
    rest[...] = jnp.dot(iterate, columns[...], preferred_element_type=F32)


def residual_kernel(edge, rest, xa, xb, pair, ya, yb, spread, rhs, orders, basis, inverse, _, residual, local, rows, held, done):
    copy = pltpu.make_async_copy(inverse, held, done)
    copy.start()
    summed = edge[...] + times_selection(arrivals(xa, xb, pair, ya, yb), spread[...])
    total = jnp.concatenate([summed, rest[...]], axis=1)
    value = jnp.where(mask_of(orders), rhs[...] - total, 0.0)
    residual[...] = value
    padded = jnp.concatenate([value, jnp.zeros((6, N), F32)], axis=0).astype(BF16)
    coarse = lax.dot_general(padded, basis[...], (((1,), (1,)), ((), ())), preferred_element_type=F32)
    coarse = jnp.concatenate([coarse, jnp.zeros((8, 128 - NV), F32)], axis=1)
    place = lax.axis_index("y") * (C * X) + lax.axis_index("c") * X + lax.axis_index("x")
    shift = (24 * place) % 128
    turned = pltpu.roll(coarse, shift, 1)
    turned_far = pltpu.roll(turned, 64, 1)
    rows[...] = jnp.broadcast_to(turned[0:1] + turned_far[1:2], (PLANE, 128))
    copy.wait()
    local[...] = jnp.dot(value.astype(BF16), held[...], preferred_element_type=F32)


def repack_kernel(rows, out, packed):
    taken = rows[...]
    far = pltpu.roll(taken, 64, 1)
    place = lax.broadcasted_iota(jnp.int32, (PLANE, 128), 0)
    lane = lax.broadcasted_iota(jnp.int32, (PLANE, 128), 1)
    within = (lane - NV * place + NV * PLANE) & 127
    row = jnp.where(within < NV, (NV * (place & 15) + within) >> 7, -1)
    for load, field in enumerate((taken, far)):
        for r in range(3):
            kept = jnp.where(row == r, field, 0.0)
            for group in range(4):
                packed[load * 12 + group * 3 + r : load * 12 + group * 3 + r + 1, :] = jnp.sum(
                    kept[group * 16 : (group + 1) * 16], axis=0, keepdims=True
                )
    whole = packed[...]
    for z in range(Z):
        out[z] = whole


def coarse_kernel(gathered, inverse, basis, weights, orders, local, select, correction, *own):
    sums = [[jnp.zeros((NV, 128), F32) for _ in range(2)] for _ in range(2)]
    for t in range(Z * 12):
        z, r = divmod(t, 12)
        block = inverse[:, t * 128 : (t + 1) * 128]
        for load in range(2):
            sums[load][t % 2] += block * gathered[z, load * 12 + r : load * 12 + r + 1, :]
    vectors = basis[...].astype(F32)
    fixes = []
    for load in range(2):
        coarse = jnp.sum(sums[load][0] + sums[load][1], axis=1, keepdims=True)
        coarse = coarse.astype(BF16).astype(F32)
        fixes.append(jnp.sum(vectors * coarse, axis=0, keepdims=True))
    fix = jnp.concatenate(fixes, axis=0)
    weight_row = jnp.concatenate([weights[j : j + 1, :] for j in range(6)], axis=1)
    value = jnp.where(mask_of(orders), weight_row * (local[...] + fix), 0.0)
    correction[...] = value
    send_messages(value[:, :EDGE], select[...], *own)


def last_kernel(start, orders, correction, xa, xb, pair, ya, yb, spread, solved):
    arrived = times_selection(arrivals(xa, xb, pair, ya, yb), spread[...])
    value = jnp.where(mask_of(orders), start[...], 0.0) + correction[...]
    solved[...] = value
    solved[:, :EDGE] = value[:, :EDGE] + arrived


MESSAGES = [((2, H), F32), ((2, H), F32), ((2, 2 * H), F32), ((2, H), F32), ((2, H), F32)]


def exchange(own_xa, own_xb, own_c, own_ya, own_yb):
    chips = Z * Y
    pairs_c = [(d, d ^ 1) for d in range(C)]
    even_x = [(d, d ^ 1) for d in range(X)]
    odd_x = [(1, 2), (2, 1)]
    even_chips = [(2 * q + c, 2 * (q ^ 1) + c) for q in range(chips) for c in range(C)]
    odd_chips = []
    for q in range(1, chips - 1, 2):
        for c in range(C):
            odd_chips += [(2 * q + c, 2 * q + 2 + c), (2 * q + 2 + c, 2 * q + c)]
    pair = lax.ppermute(own_c, "c", pairs_c)
    xa = lax.ppermute(own_xa, "x", even_x)
    xb = lax.ppermute(own_xb, "x", odd_x)
    even_chip = parities()[1]
    up, down = pair[:, :H], pair[:, H:]
    ya = jnp.concatenate([own_ya, jnp.where(even_chip, up, down)], axis=1)
    yb = jnp.concatenate([own_yb, jnp.where(even_chip, down, up)], axis=1)
    ya = lax.ppermute(ya, CHIPS, even_chips)
    yb = lax.ppermute(yb, CHIPS, odd_chips)
    return xa, xb, pair, ya, yb


def per_device(
    rhs, start, stiffness, local_inverse, basis, weights, coarse_inverse, orders, out_rows, out_counts, in_rows
):
    orders = orders.reshape(1, 1)
    out_rows = out_rows.reshape(6, 1, H)
    in_rows = in_rows.reshape(6, 1, H)
    arriving = [pltpu.VMEM((2, N), F32), pltpu.VMEM((6, 1, H), jnp.int32), pltpu.SemaphoreType.DMA((3,))]
    select, edge, *own = on_chip(
        first_kernel,
        [((EDGE, 6 * H), BF16), ((2, EDGE), F32)] + MESSAGES,
        [start, stiffness, orders, out_rows, out_counts],
        scalars=(2, 4),
        far=(0, 1, 3),
        scratch=[pltpu.VMEM((N, EDGE), BF16)] + arriving,
    )
    spread, rest = on_chip(
        rest_kernel,
        [((6 * H, EDGE), BF16), ((2, N - EDGE), F32)],
        [start, stiffness, orders, in_rows],
        scalars=(2,),
        far=(0, 1, 3),
        scratch=[pltpu.VMEM((N, N - EDGE), BF16)] + arriving,
    )
    arrived = exchange(*own)
    residual, local, rows = on_chip(
        residual_kernel,
        [((2, N), F32), ((2, N), F32), ((PLANE, 128), F32)],
        [edge, rest, *arrived, spread, rhs, orders, basis, local_inverse, coarse_inverse],
        scalars=(9,),
        far=(11,),
        scratch=[pltpu.VMEM((N, N), BF16), pltpu.SemaphoreType.DMA],
    )
    rows = lax.all_to_all(rows.reshape(PLANE, 1, 128), ("y", "c", "x"), 0, 0).reshape(PLANE, 128)
    (gathered,) = on_chip(
        repack_kernel, [((Z, 2 * 12, 128), F32)], [rows], scratch=[pltpu.VMEM((2 * 12, 128), F32)]
    )
    gathered = lax.all_to_all(gathered, "z", 0, 0)
    correction, *own = on_chip(
        coarse_kernel,
        [((2, N), F32)] + MESSAGES,
        [gathered, coarse_inverse, basis, weights.reshape(6, 128), orders, local, select],
        scalars=(4,),
    )
    arrived = exchange(*own)
    (solved,) = on_chip(last_kernel, [((2, N), F32)], [start, orders, correction, *arrived, spread], scalars=(1,))
    return solved, residual


def solution(mesh):
    fine = Mesh(mesh.devices.reshape(Z, Y, C, X), ALL)
    return jax.shard_map(
        per_device,
        mesh=fine,
        in_specs=(
            P(None, ALL),
            P(None, ALL),
            P(ALL, None),
            P(ALL, None),
            P(None, ALL),
            P(ALL),
            P(ALL, None),
            P(ALL),
            P(ALL, None, None),
            P(ALL, None),
            P(ALL, None, None),
        ),
        out_specs=(P(None, ALL), P(None, ALL)),
        check_vma=False,
    )
```

time: 98.8 us -> 88 us (0.89)
  the two profiles are of different devices: /device:TPU:2 before, /device:TPU:58 now
where the time goes in v2:
time: 88 us; the launch traced here: 87.5 us
  blocking collectives  42.5 us (48%)
  starting transfers between devices  30.7 us (35%)
  Pallas kernels  6 us (7%)
  waiting for transfers between devices  4.84 us (6%)
  local copies, waits for them, and re-layouts  1.9 us (2%)
  between operations  1.47 us (2%)
    all_to_all x1, blocking collectives, per_device(): gathered = lax.all_to_all(gathered, 'z', 0, 0)  24.5 us
    all_to_all x1, blocking collectives, per_device(): lax.all_to_all(rows.reshape(PLANE, 1, 128), ('y', 'c', 'x'), 0, 0)  18 us
    ppermute x2, starting transfers between devices, exchange(): yb = lax.ppermute(yb, CHIPS, odd_chips)  8.77 us
    ppermute x2, starting transfers between devices, exchange(): xb = lax.ppermute(own_xb, 'x', odd_x)  6.44 us
    pallas_call x6, Pallas kernels, on_chip(): pl.pallas_call(kernel, in_specs=specs, out_specs=[pl.BlockSpec(memory_spa...  6 us
    ppermute x2, starting transfers between devices, exchange(): ya = lax.ppermute(ya, CHIPS, even_chips)  5.82 us
    ppermute x2, starting transfers between devices, exchange(): xa = lax.ppermute(own_xa, 'x', even_x)  5.81 us
    ppermute x2, starting transfers between devices, exchange(): pair = lax.ppermute(own_c, 'c', pairs_c)  3.85 us
  transfers between devices with their start and end apart: 10, of which 4 were waited for; matrix products, arithmetic and copies ran while one was open for 1% of the time, Pallas kernels for 2%

profile of v2, /device:TPU:58, one launch (start us, length us, event | category | flops | bytes accessed | tf_op | source)
XLA Modules:
  0.0 87.5 jit_solution(1624421154611582415)
XLA Ops:
  1.3 0.0 copy-start.5
  1.3 0.6 copy-done.5
  1.9 0.0 copy-start
  1.9 0.0 copy-start.1
  1.9 0.0 copy-start.3
  1.9 2.0 %shard_map.122 = (bf16[256,768]{1,0:T(8,128)(2,1)S(1)}, f32[2,256]{1,0:T(2,128)S(1)}, f32[2,128]{1,0:T(2,128)S(1)}, f32[2,128]{1,0:T(2,128)S(1)}, f32[2,256]{1,0...) custom-call(f32[2,768]{1,0:T(2,128)} %start.5, bf16[768,768]{1,0:T(8,128)(2,1)} %stiff.3, ...), custom_call_target="tpu_custom_call" | custom-call | tf_op jit(solution)/shard_map/pallas_call | solution.py:27
  4.0 1.9 %collective-permute-start.2 = (f32[2,256]{1,0:T(2,128)S(1)}, f32[2,256]{1,0:T(2,128)S(1)}, u32[]{:S(2)}, u32[]{:S(2)}) collective-permute-start(f32[2,256]{1,0:T(2,128)S(1)} %get-tuple-element.24), channel_id=1, source_target_pairs={{0,4},{4,0},{1,5},{5,1},{2,6},{6,2},{3,7},{7,3},{8,12},{12,8},{9,1... | collective-permute-start | bytes 6152 | tf_op jit(solution)/shard_map/ppermute | solution.py:207
  5.9 1.1 %collective-permute-done.2.pair = f32[2,256]{1,0:T(2,128)S(1)} collective-permute-done((f32[2,256]{1,0:T(2,128)S(1)}, f32[2,256]{1,0:T(2,128)S(1)}, u32[]{:S(2)}, u32[]{:S(2)}) %collective-permute-start.2) | collective-permute-done | bytes 2080 | tf_op jit(solution)/shard_map/ppermute | solution.py:207
  7.0 3.3 %collective-permute-start.3 = (f32[2,256]{1,0:T(2,128)S(1)}, f32[2,256]{1,0:T(2,128)S(1)}, u32[]{:S(2)}, u32[]{:S(2)}) collective-permute-start(f32[2,256]{1,0:T(2,128)S(1)} %pad_maximum_fusion), channel_id=1, source_target_pairs={{0,8},{4,12},{8,0},{12,4},{16,24},{20,28},{24,16},{28,20},{32,40},... | collective-permute-start | bytes 6152 | tf_op jit(solution)/shard_map/ppermute | solution.py:214
  10.3 3.7 %collective-permute-start.4 = (f32[2,256]{1,0:T(2,128)S(1)}, f32[2,256]{1,0:T(2,128)S(1)}, u32[]{:S(2)}, u32[]{:S(2)}) collective-permute-start(f32[2,256]{1,0:T(2,128)S(1)} %pad_maximum_fusion.1), channel_id=1, source_target_pairs={{8,16},{16,8},{12,20},{20,12},{24,32},{32,24},{28,36},{36,28},{40,... | collective-permute-start | bytes 6152 | tf_op jit(solution)/shard_map/ppermute | solution.py:215
  14.0 2.4 %collective-permute-start = (f32[2,128]{1,0:T(2,128)S(1)}, f32[2,128]{1,0:T(2,128)S(1)}, u32[]{:S(2)}, u32[]{:S(2)}) collective-permute-start(f32[2,128]{1,0:T(2,128)S(1)} %get-tuple-element.22), channel_id=1, source_target_pairs={{0,1},{1,0},{2,3},{3,2},{4,5},{5,4},{6,7},{7,6},{8,9},{9,8},{10,11... | collective-permute-start | bytes 3080 | tf_op jit(solution)/shard_map/ppermute | solution.py:208
  16.5 4.1 %collective-permute-start.1 = (f32[2,128]{1,0:T(2,128)S(1)}, f32[2,128]{1,0:T(2,128)S(1)}, u32[]{:S(2)}, u32[]{:S(2)}) collective-permute-start(f32[2,128]{1,0:T(2,128)S(1)} %get-tuple-element.23), channel_id=1, source_target_pairs={{1,2},{2,1},{5,6},{6,5},{9,10},{10,9},{13,14},{14,13},{17,18},{18,... | collective-permute-start | bytes 3080 | tf_op jit(solution)/shard_map/ppermute | solution.py:209
  20.6 1.4 %shard_map.123 = (bf16[768,256]{1,0:T(8,128)(2,1)S(1)}, f32[2,512]{1,0:T(2,128)S(1)}) custom-call(f32[2,768]{1,0:T(2,128)} %start.5, bf16[768,768]{1,0:T(8,128)(2,1)} %stiff.3, s32[1,1]{1,0:T(1,128)} %bitcast.9.orders, s32[6,1,128]{2,1,0:T(1,128)} %bitcast.17), custom_call_target="tpu_custom_call" | custom-call | tf_op jit(solution)/shard_map/pallas_call | solution.py:27
  22.0 0.0 collective-permute-done.xa
  22.0 0.1 collective-permute-done.1.xb
  22.1 0.0 collective-permute-done.3.ya
  22.1 0.0 collective-permute-done.4.yb
  22.1 0.0 copy-done
  22.1 0.0 copy-done.1
  22.1 0.0 copy-done.3
  22.1 0.0 copy-start.4
  22.1 1.6 %shard_map.124 = (f32[2,768]{1,0:T(2,128)S(1)}, f32[2,768]{1,0:T(2,128)S(1)}, f32[64,128]{1,0:T(8,128)S(1)}) custom-call(f32[2,256]{1,0:T(2,128)S(1)} %get-tuple-element.20.edge, f32[2,512]{1,0:T(2,128)S(1)} %get-tuple-element.21.rest, f32[2,128]{1,0:T(2,128)S(1)} %collective-permute-done.xa, f32[2,128]{1,0:T(2,128)S(1)} %collective-permute-done.1.xb, ...), custom_call_target="tpu_custom_call" | custom-call | tf_op jit(solution)/shard_map/pallas_call | solution.py:27
  23.8 18.0 %all_to_all.10 = f32[64,1,128]{2,1,0:T(1,128)S(1)} all-to-all(f32[64,1,128]{2,1,0:T(1,128)S(1)} %bitcast.14), channel_id=1, replica_groups=mesh['z'=12,'y'=8,'c'=2,'x'=4] {'y','c','x'}, dimensions={0} | all-to-all | bytes 65536 | tf_op jit(solution)/shard_map/all_to_all | solution.py:251
  41.8 0.1 shard_map.125
  41.9 24.5 %all_to_all.11.gathered = f32[12,24,128]{2,1,0:T(8,128)S(1)} all-to-all(f32[12,24,128]{2,1,0:T(8,128)S(1)} %shard_map.125), channel_id=1, replica_groups=mesh['z'=12,'y'=8,'c'=2,'x'=4] {'z'}, dimensions={0} | all-to-all | bytes 294912 | tf_op jit(solution)/shard_map/all_to_all | solution.py:255
  66.4 0.0 copy-done.4
  66.4 0.0 copy-start.2
  66.4 0.7 shard_map.126
  67.1 1.9 %collective-permute-start.7 = (f32[2,256]{1,0:T(2,128)S(1)}, f32[2,256]{1,0:T(2,128)S(1)}, u32[]{:S(2)}, u32[]{:S(2)}) collective-permute-start(f32[2,256]{1,0:T(2,128)S(1)} %get-tuple-element.34), channel_id=1, source_target_pairs={{0,4},{4,0},{1,5},{5,1},{2,6},{6,2},{3,7},{7,3},{8,12},{12,8},{9,1... | collective-permute-start | bytes 6152 | tf_op jit(solution)/shard_map/ppermute | solution.py:207
  69.0 1.1 %collective-permute-done.7.pair = f32[2,256]{1,0:T(2,128)S(1)} collective-permute-done((f32[2,256]{1,0:T(2,128)S(1)}, f32[2,256]{1,0:T(2,128)S(1)}, u32[]{:S(2)}, u32[]{:S(2)}) %collective-permute-start.7) | collective-permute-done | bytes 2080 | tf_op jit(solution)/shard_map/ppermute | solution.py:207
  70.2 2.6 %collective-permute-start.8 = (f32[2,256]{1,0:T(2,128)S(1)}, f32[2,256]{1,0:T(2,128)S(1)}, u32[]{:S(2)}, u32[]{:S(2)}) collective-permute-start(f32[2,256]{1,0:T(2,128)S(1)} %pad_maximum_fusion.2), channel_id=1, source_target_pairs={{0,8},{4,12},{8,0},{12,4},{16,24},{20,28},{24,16},{28,20},{32,40},... | collective-permute-start | bytes 6152 | tf_op jit(solution)/shard_map/ppermute | solution.py:214
  72.8 5.1 %collective-permute-start.9 = (f32[2,256]{1,0:T(2,128)S(1)}, f32[2,256]{1,0:T(2,128)S(1)}, u32[]{:S(2)}, u32[]{:S(2)}) collective-permute-start(f32[2,256]{1,0:T(2,128)S(1)} %pad_maximum_fusion.3), channel_id=1, source_target_pairs={{8,16},{16,8},{12,20},{20,12},{24,32},{32,24},{28,36},{36,28},{40,... | collective-permute-start | bytes 6152 | tf_op jit(solution)/shard_map/ppermute | solution.py:215
  77.8 3.4 %collective-permute-start.5 = (f32[2,128]{1,0:T(2,128)S(1)}, f32[2,128]{1,0:T(2,128)S(1)}, u32[]{:S(2)}, u32[]{:S(2)}) collective-permute-start(f32[2,128]{1,0:T(2,128)S(1)} %get-tuple-element.32), channel_id=1, source_target_pairs={{0,1},{1,0},{2,3},{3,2},{4,5},{5,4},{6,7},{7,6},{8,9},{9,8},{10,11... | collective-permute-start | bytes 3080 | tf_op jit(solution)/shard_map/ppermute | solution.py:208
  81.2 2.4 %collective-permute-start.6 = (f32[2,128]{1,0:T(2,128)S(1)}, f32[2,128]{1,0:T(2,128)S(1)}, u32[]{:S(2)}, u32[]{:S(2)}) collective-permute-start(f32[2,128]{1,0:T(2,128)S(1)} %get-tuple-element.33), channel_id=1, source_target_pairs={{1,2},{2,1},{5,6},{6,5},{9,10},{10,9},{13,14},{14,13},{17,18},{18,... | collective-permute-start | bytes 3080 | tf_op jit(solution)/shard_map/ppermute | solution.py:209
  83.6 0.6 copy.15
  84.2 0.0 collective-permute-done.5.xa
  84.2 2.5 %collective-permute-done.6.xb = f32[2,128]{1,0:T(2,128)S(1)} collective-permute-done((f32[2,128]{1,0:T(2,128)S(1)}, f32[2,128]{1,0:T(2,128)S(1)}, u32[]{:S(2)}, u32[]{:S(2)}) %collective-permute-start.6) | collective-permute-done | bytes 1056 | tf_op jit(solution)/shard_map/ppermute | solution.py:209
  86.7 0.0 collective-permute-done.8.ya
  86.7 0.0 collective-permute-done.9.yb
  86.7 0.0 copy-done.2
  86.7 0.2 shard_map.127
  86.8 0.6 copy.14
  (6 shorter events, 0.0 us)
Async XLA Ops:
  1.3 0.7 copy-start.5
  1.9 20.2 %copy-start = (f32[24,18432]{1,0:T(8,128)S(1)}, f32[24,18432]{1,0:T(8,128)}, u32[]{:S(2)}) copy-start(f32[24,18432]{1,0:T(8,128)} %inverse.3) | copy-start | bytes 5308420
  1.9 20.2 %copy-start.1 = (bf16[24,768]{1,0:T(8,128)(2,1)S(1)}, bf16[24,768]{1,0:T(8,128)(2,1)}, u32[]{:S(2)}) copy-start(bf16[24,768]{1,0:T(8,128)(2,1)} %basis.3) | copy-start | bytes 110596
  1.9 20.2 %copy-start.3 = (f32[2,768]{1,0:T(2,128)S(1)}, f32[2,768]{1,0:T(2,128)}, u32[]{:S(2)}) copy-start(f32[2,768]{1,0:T(2,128)} %rhs.1) | copy-start | bytes 18436
  4.0 3.1 %collective-permute-start.2 = (f32[2,256]{1,0:T(2,128)S(1)}, f32[2,256]{1,0:T(2,128)S(1)}, u32[]{:S(2)}, u32[]{:S(2)}) collective-permute-start(f32[2,256]{1,0:T(2,128)S(1)} %get-tuple-element.24), channel_id=1, source_target_pairs={{0,4},{4,0},{1,5},{5,1},{2,6},{6,2},{3,7},{7,3},{8,12},{12,8},{9,1... | collective-permute-start | bytes 6152 | tf_op jit(solution)/shard_map/ppermute | solution.py:207
  7.0 15.1 %collective-permute-start.3 = (f32[2,256]{1,0:T(2,128)S(1)}, f32[2,256]{1,0:T(2,128)S(1)}, u32[]{:S(2)}, u32[]{:S(2)}) collective-permute-start(f32[2,256]{1,0:T(2,128)S(1)} %pad_maximum_fusion), channel_id=1, source_target_pairs={{0,8},{4,12},{8,0},{12,4},{16,24},{20,28},{24,16},{28,20},{32,40},... | collective-permute-start | bytes 6152 | tf_op jit(solution)/shard_map/ppermute | solution.py:214
  10.3 11.8 %collective-permute-start.4 = (f32[2,256]{1,0:T(2,128)S(1)}, f32[2,256]{1,0:T(2,128)S(1)}, u32[]{:S(2)}, u32[]{:S(2)}) collective-permute-start(f32[2,256]{1,0:T(2,128)S(1)} %pad_maximum_fusion.1), channel_id=1, source_target_pairs={{8,16},{16,8},{12,20},{20,12},{24,32},{32,24},{28,36},{36,28},{40,... | collective-permute-start | bytes 6152 | tf_op jit(solution)/shard_map/ppermute | solution.py:215
  14.0 7.9 %collective-permute-start = (f32[2,128]{1,0:T(2,128)S(1)}, f32[2,128]{1,0:T(2,128)S(1)}, u32[]{:S(2)}, u32[]{:S(2)}) collective-permute-start(f32[2,128]{1,0:T(2,128)S(1)} %get-tuple-element.22), channel_id=1, source_target_pairs={{0,1},{1,0},{2,3},{3,2},{4,5},{5,4},{6,7},{7,6},{8,9},{9,8},{10,11... | collective-permute-start | bytes 3080 | tf_op jit(solution)/shard_map/ppermute | solution.py:208
  16.5 5.6 %collective-permute-start.1 = (f32[2,128]{1,0:T(2,128)S(1)}, f32[2,128]{1,0:T(2,128)S(1)}, u32[]{:S(2)}, u32[]{:S(2)}) collective-permute-start(f32[2,128]{1,0:T(2,128)S(1)} %get-tuple-element.23), channel_id=1, source_target_pairs={{1,2},{2,1},{5,6},{6,5},{9,10},{10,9},{13,14},{14,13},{17,18},{18,... | collective-permute-start | bytes 3080 | tf_op jit(solution)/shard_map/ppermute | solution.py:209
  22.1 44.3 %copy-start.4 = (f32[768]{0:T(1024)S(1)}, f32[768]{0:T(1024)}, u32[]{:S(2)}) copy-start(f32[768]{0:T(1024)} %param.16) | copy-start | bytes 9220
  66.4 20.3 %copy-start.2 = (f32[2,768]{1,0:T(2,128)S(1)}, f32[2,768]{1,0:T(2,128)}, u32[]{:S(2)}) copy-start(f32[2,768]{1,0:T(2,128)} %start.5) | copy-start | bytes 18436
  67.1 3.1 %collective-permute-start.7 = (f32[2,256]{1,0:T(2,128)S(1)}, f32[2,256]{1,0:T(2,128)S(1)}, u32[]{:S(2)}, u32[]{:S(2)}) collective-permute-start(f32[2,256]{1,0:T(2,128)S(1)} %get-tuple-element.34), channel_id=1, source_target_pairs={{0,4},{4,0},{1,5},{5,1},{2,6},{6,2},{3,7},{7,3},{8,12},{12,8},{9,1... | collective-permute-start | bytes 6152 | tf_op jit(solution)/shard_map/ppermute | solution.py:207
  70.2 16.5 %collective-permute-start.8 = (f32[2,256]{1,0:T(2,128)S(1)}, f32[2,256]{1,0:T(2,128)S(1)}, u32[]{:S(2)}, u32[]{:S(2)}) collective-permute-start(f32[2,256]{1,0:T(2,128)S(1)} %pad_maximum_fusion.2), channel_id=1, source_target_pairs={{0,8},{4,12},{8,0},{12,4},{16,24},{20,28},{24,16},{28,20},{32,40},... | collective-permute-start | bytes 6152 | tf_op jit(solution)/shard_map/ppermute | solution.py:214
  72.8 13.9 %collective-permute-start.9 = (f32[2,256]{1,0:T(2,128)S(1)}, f32[2,256]{1,0:T(2,128)S(1)}, u32[]{:S(2)}, u32[]{:S(2)}) collective-permute-start(f32[2,256]{1,0:T(2,128)S(1)} %pad_maximum_fusion.3), channel_id=1, source_target_pairs={{8,16},{16,8},{12,20},{20,12},{24,32},{32,24},{28,36},{36,28},{40,... | collective-permute-start | bytes 6152 | tf_op jit(solution)/shard_map/ppermute | solution.py:215
  77.8 6.4 %collective-permute-start.5 = (f32[2,128]{1,0:T(2,128)S(1)}, f32[2,128]{1,0:T(2,128)S(1)}, u32[]{:S(2)}, u32[]{:S(2)}) collective-permute-start(f32[2,128]{1,0:T(2,128)S(1)} %get-tuple-element.32), channel_id=1, source_target_pairs={{0,1},{1,0},{2,3},{3,2},{4,5},{5,4},{6,7},{7,6},{8,9},{9,8},{10,11... | collective-permute-start | bytes 3080 | tf_op jit(solution)/shard_map/ppermute | solution.py:208
  81.2 5.5 %collective-permute-start.6 = (f32[2,128]{1,0:T(2,128)S(1)}, f32[2,128]{1,0:T(2,128)S(1)}, u32[]{:S(2)}, u32[]{:S(2)}) collective-permute-start(f32[2,128]{1,0:T(2,128)S(1)} %get-tuple-element.33), channel_id=1, source_target_pairs={{1,2},{2,1},{5,6},{6,5},{9,10},{10,9},{13,14},{14,13},{17,18},{18,... | collective-permute-start | bytes 3080 | tf_op jit(solution)/shard_map/ppermute | solution.py:209

commit v3 on v2

v3 whole, which is shorter than its diff:
```python
import jax
import jax.numpy as jnp
from jax import lax
from jax.experimental import pallas as pl
from jax.experimental.pallas import tpu as pltpu
from jax.sharding import Mesh
from jax.sharding import PartitionSpec as P

Z, Y, C, X = 12, 8, 2, 4
PLANE = Y * C * X
N = 768
NV = 24
H = 128
EDGE = 256
F32, BF16 = jnp.float32, jnp.bfloat16
ALL = ("z", "y", "c", "x")
CHIPS = ("z", "y", "c")
LEAN = pltpu.CompilerParams(vmem_limit_bytes=8 << 20)


def on_chip(kernel, out_shape, args, far=(), scratch=(), scalars=()):
    spaces = [pltpu.SMEM if i in scalars else pltpu.HBM if i in far else pltpu.VMEM for i in range(len(args))]
    args = [a if i in scalars else pltpu.with_memory_space_constraint(a, spaces[i]) for i, a in enumerate(args)]
    return pl.pallas_call(
        kernel,
        in_specs=[pl.BlockSpec(memory_space=space) for space in spaces],
        out_specs=[pl.BlockSpec(memory_space=pltpu.VMEM)] * len(out_shape),
        out_shape=[pltpu.VMEM(shape, dtype) for shape, dtype in out_shape],
        scratch_shapes=list(scratch),
        compiler_params=LEAN,
    )(*args)


def thirds(value):
    high = value.astype(BF16)
    rest = value - high.astype(F32)
    middle = rest.astype(BF16)
    low = (rest - middle.astype(F32)).astype(BF16)
    return jnp.concatenate([high, middle, low], axis=0)


def times_selection(value, selection):
    parts = jnp.dot(thirds(value), selection, preferred_element_type=F32)
    return parts[0:2] + parts[2:4] + parts[4:6]


def write_slots(field, select, own):
    picked = times_selection(field, select)
    for j in range(6):
        own[j] = picked[:, j * H : (j + 1) * H]


def arrivals(both, moved):
    first = lax.axis_index("c") == 0
    up, down = 0, 5
    return jnp.concatenate(
        [
            jnp.where(first, moved[up + 3], moved[up + 4]),
            jnp.where(first, moved[down + 3], moved[down + 4]),
            jnp.where(first, moved[up + 2], both[2]),
            jnp.where(first, both[6 + 3], moved[down + 2]),
            jnp.where(first, moved[up], moved[up + 1]),
            jnp.where(first, moved[down], moved[down + 1]),
        ],
        axis=1,
    )


def exchange(own):
    chips = Z * Y
    both = lax.all_gather(own, "c", axis=0, tiled=True)
    first = lax.axis_index("c") == 0
    along_x = jnp.where(first, jnp.stack([both[0], both[6]]), jnp.stack([both[1], both[7]]))
    along_y = jnp.where(first, jnp.stack([both[4], both[10], both[8]]), jnp.stack([both[5], both[11], both[3]]))
    route_y = [(2 * q, 2 * q + 2) for q in range(chips - 1)] + [(2 * q + 1, 2 * q - 1) for q in range(1, chips)]
    route_x = [(d, d + 1) for d in range(X - 1)] + [(X + d, X + d - 1) for d in range(1, X)]
    got_y = lax.ppermute(along_y, CHIPS, route_y)
    got_x = lax.ppermute(along_x, ("c", "x"), route_x)
    moved = lax.all_gather(jnp.concatenate([got_y, got_x]), "c", axis=0, tiled=True)
    return both, moved


def first_kernel(start, stiff, orders, out_rows, counts, select, edge, mask, iterate, own, columns, fields, listing, count, done):
    copies = [
        pltpu.make_async_copy(counts, count, done.at[0]),
        pltpu.make_async_copy(out_rows, listing, done.at[1]),
        pltpu.make_async_copy(start, fields, done.at[2]),
        pltpu.make_async_copy(stiff.at[:, pl.ds(0, EDGE)], columns, done.at[3]),
    ]
    for copy in copies:
        copy.start()
    rows = lax.broadcasted_iota(jnp.int32, (EDGE, H), 0)
    slots = lax.broadcasted_iota(jnp.int32, (1, H), 1)
    copies[0].wait()
    copies[1].wait()
    for j in range(6):
        listed = jnp.where(slots < count[0, j], listing[j], -1)
        select[:, j * H : (j + 1) * H] = (rows == listed).astype(F32).astype(BF16)
    kept = lax.broadcasted_iota(jnp.int32, (1, N), 1) < orders[0]
    mask[...] = kept.astype(F32)
    copies[2].wait()
    masked = jnp.where(kept, fields[...], 0.0)
    iterate[...] = masked
    copies[3].wait()
    product = jnp.dot(masked.astype(BF16), columns[...], preferred_element_type=F32)
    edge[...] = product
    write_slots(product, select[...], own)


def rest_kernel(iterate, stiff, in_rows, inverse, spread, rest, held, columns, listing, done):
    copies = [
        pltpu.make_async_copy(in_rows, listing, done.at[0]),
        pltpu.make_async_copy(stiff.at[:, pl.ds(EDGE, N - EDGE)], columns, done.at[1]),
        pltpu.make_async_copy(inverse, held, done.at[2]),
    ]
    for copy in copies:
        copy.start()
    rows = lax.broadcasted_iota(jnp.int32, (EDGE, H), 0)
    copies[0].wait()
    for j in range(6):
        hit = (rows == listing[j]).astype(F32)
        spread[j * H : (j + 1) * H, :] = hit.T.astype(BF16)
    copies[1].wait()
    rest[...] = jnp.dot(iterate[...].astype(BF16), columns[...], preferred_element_type=F32)
    copies[2].wait()


def residual_kernel(edge, rest, both, moved, spread, rhs, mask, basis, _, residual, rounded, rows):
    summed = edge[...] + times_selection(arrivals(both, moved), spread[...])
    total = jnp.concatenate([summed, rest[...]], axis=1)
    value = jnp.where(mask[...] > 0.0, rhs[...] - total, 0.0)
    residual[...] = value
    rounded[...] = value.astype(BF16)
    padded = jnp.concatenate([value, jnp.zeros((6, N), F32)], axis=0).astype(BF16)
    coarse = lax.dot_general(padded, basis[...], (((1,), (1,)), ((), ())), preferred_element_type=F32)
    coarse = jnp.concatenate([coarse, jnp.zeros((8, 128 - NV), F32)], axis=1)
    place = lax.axis_index("y") * (C * X) + lax.axis_index("c") * X + lax.axis_index("x")
    shift = (24 * place) % 128
    turned = pltpu.roll(coarse, shift, 1)
    turned_far = pltpu.roll(turned, 64, 1)
    rows[...] = jnp.broadcast_to(turned[0:1] + turned_far[1:2], (PLANE, 128))


def repack_kernel(rows, out, packed):
    taken = rows[...]
    far = pltpu.roll(taken, 64, 1)
    place = lax.broadcasted_iota(jnp.int32, (PLANE, 128), 0)
    lane = lax.broadcasted_iota(jnp.int32, (PLANE, 128), 1)
    within = (lane - NV * place + NV * PLANE) & 127
    row = jnp.where(within < NV, (NV * (place & 15) + within) >> 7, -1)
    for load, field in enumerate((taken, far)):
        for r in range(3):
            kept = jnp.where(row == r, field, 0.0)
            for group in range(4):
                packed[load * 12 + group * 3 + r : load * 12 + group * 3 + r + 1, :] = jnp.sum(
                    kept[group * 16 : (group + 1) * 16], axis=0, keepdims=True
                )
    whole = packed[...]
    for z in range(Z):
        out[z] = whole


def coarse_kernel(gathered, inverse, basis, weights, mask, rounded, held, select, correction, own):
    sums = [[jnp.zeros((NV, 128), F32) for _ in range(2)] for _ in range(2)]
    for t in range(Z * 12):
        z, r = divmod(t, 12)
        block = inverse[:, t * 128 : (t + 1) * 128]
        for load in range(2):
            sums[load][t % 2] += block * gathered[z, load * 12 + r : load * 12 + r + 1, :]
    vectors = basis[...].astype(F32)
    fixes = []
    for load in range(2):
        coarse = jnp.sum(sums[load][0] + sums[load][1], axis=1, keepdims=True)
        coarse = coarse.astype(BF16).astype(F32)
        fixes.append(jnp.sum(vectors * coarse, axis=0, keepdims=True))
    fix = jnp.concatenate(fixes, axis=0)
    local = jnp.dot(rounded[...], held[...], preferred_element_type=F32)
    weight_row = jnp.concatenate([weights[j : j + 1, :] for j in range(6)], axis=1)
    value = weight_row * mask[...] * (local + fix)
    correction[...] = value
    write_slots(value[:, :EDGE], select[...], own)


def last_kernel(iterate, correction, both, moved, spread, solved):
    arrived = times_selection(arrivals(both, moved), spread[...])
    value = iterate[...] + correction[...]
    solved[...] = value
    solved[:, :EDGE] = value[:, :EDGE] + arrived


def per_device(
    rhs, start, stiffness, local_inverse, basis, weights, coarse_inverse, orders, out_rows, out_counts, in_rows
):
    out_rows = out_rows.reshape(6, 1, H)
    in_rows = in_rows.reshape(6, 1, H)
    slots = ((6, 2, H), F32)
    listing = pltpu.VMEM((6, 1, H), jnp.int32)
    select, edge, mask, iterate, own = on_chip(
        first_kernel,
        [((EDGE, 6 * H), BF16), ((2, EDGE), F32), ((1, N), F32), ((2, N), F32), slots],
        [start, stiffness, orders, out_rows, out_counts],
        far=(0, 1, 3, 4),
        scalars=(2,),
        scratch=[
            pltpu.VMEM((N, EDGE), BF16),
            pltpu.VMEM((2, N), F32),
            listing,
            pltpu.SMEM((1, 6), jnp.int32),
            pltpu.SemaphoreType.DMA((4,)),
        ],
    )
    spread, rest, held = on_chip(
        rest_kernel,
        [((6 * H, EDGE), BF16), ((2, N - EDGE), F32), ((N, N), BF16)],
        [iterate, stiffness, in_rows, local_inverse],
        far=(1, 2, 3),
        scratch=[pltpu.VMEM((N, N - EDGE), BF16), listing, pltpu.SemaphoreType.DMA((3,))],
    )
    both, moved = exchange(own)
    residual, rounded, rows = on_chip(
        residual_kernel,
        [((2, N), F32), ((2, N), BF16), ((PLANE, 128), F32)],
        [edge, rest, both, moved, spread, rhs, mask, basis, coarse_inverse],
    )
    rows = lax.all_to_all(rows.reshape(PLANE, 1, 128), ("y", "c", "x"), 0, 0).reshape(PLANE, 128)
    (gathered,) = on_chip(
        repack_kernel, [((Z, 2 * 12, 128), F32)], [rows], scratch=[pltpu.VMEM((2 * 12, 128), F32)]
    )
    gathered = lax.all_to_all(gathered, "z", 0, 0)
    correction, own = on_chip(
        coarse_kernel,
        [((2, N), F32), slots],
        [gathered, coarse_inverse, basis, weights.reshape(6, 128), mask, rounded, held, select],
    )
    both, moved = exchange(own)
    (solved,) = on_chip(last_kernel, [((2, N), F32)], [iterate, correction, both, moved, spread])
    return solved, residual


def solution(mesh):
    fine = Mesh(mesh.devices.reshape(Z, Y, C, X), ALL)
    return jax.shard_map(
        per_device,
        mesh=fine,
        in_specs=(
            P(None, ALL),
            P(None, ALL),
            P(ALL, None),
            P(ALL, None),
            P(None, ALL),
            P(ALL),
            P(ALL, None),
            P(ALL),
            P(ALL, None, None),
            P(ALL, None),
            P(ALL, None, None),
        ),
        out_specs=(P(None, ALL), P(None, ALL)),
        check_vma=False,
    )
```

time: 88 us -> 75.9 us (0.86)
  the two profiles are of different devices: /device:TPU:58 before, /device:TPU:1 now
where the time goes in v3:
time: 75.9 us; the launch traced here: 75.6 us
  blocking collectives  59.3 us (78%)
  starting transfers between devices  5.17 us (7%)
  Pallas kernels  4.67 us (6%)
  waiting for transfers between devices  3.75 us (5%)
  between operations  1.41 us (2%)
  local copies, waits for them, and re-layouts  1.27 us (2%)
    all_to_all x1, blocking collectives, per_device(): gathered = lax.all_to_all(gathered, 'z', 0, 0)  24.6 us
    all_gather x2, blocking collectives, exchange(): both = lax.all_gather(own, 'c', axis=0, tiled=True)  16.3 us
    all_to_all x1, blocking collectives, per_device(): lax.all_to_all(rows.reshape(PLANE, 1, 128), ('y', 'c', 'x'), 0, 0)  13.8 us
    pallas_call x6, Pallas kernels, on_chip(): pl.pallas_call(kernel, in_specs=[pl.BlockSpec(memory_space=space) for spa...  4.67 us
    all_gather x2, blocking collectives, exchange(): lax.all_gather(jnp.concatenate([got_y, got_x]), 'c', axis=0, tiled=True)  4.47 us
    ppermute x2, waiting for transfers between devices, exchange(): got_x = lax.ppermute(along_x, ('c', 'x'), route_x)  3.74 us
    ppermute x2, starting transfers between devices, exchange(): got_x = lax.ppermute(along_x, ('c', 'x'), route_x)  2.58 us
    ppermute x2, starting transfers between devices, exchange(): got_y = lax.ppermute(along_y, CHIPS, route_y)  2.58 us
  transfers between devices with their start and end apart: 4, of which 2 were waited for; matrix products, arithmetic and copies ran while one was open for 1% of the time, Pallas kernels for 2%

profile of v3, /device:TPU:1, one launch (start us, length us, event | category | flops | bytes accessed | tf_op | source)
XLA Modules:
  0.0 75.6 jit_solution(6870753979402005924)
XLA Ops:
  1.3 1.5 %shard_map.122 = (bf16[256,768]{1,0:T(8,128)(2,1)S(1)}, f32[2,256]{1,0:T(2,128)S(1)}, f32[1,768]{1,0:T(1,128)S(1)}, f32[2,768]{1,0:T(2,128)S(1)}, f32[6,2,128]{2,1,0:T(2,128)S(1)}) custom-call(f32[2,768]{1,0:T(2,128)} %start.1, bf16[768,768]{1,0:T(8,128)(2,1)} %stiff.3, s32[1]{0:T(128)S(6)} %copy.16.orders, s32[6,1,128]{2,1,0:T(1,128)} %bitcast.10, ...), custom_call_target="tpu_custom_call" | custom-call | tf_op jit(solution)/shard_map/pallas_call | solution.py:24
  2.8 11.9 %all_gather.12.both = f32[12,2,128]{2,1,0:T(2,128)S(1)} all-gather(f32[6,2,128]{2,1,0:T(2,128)S(1)} %get-tuple-element.18), channel_id=1, replica_groups=mesh['z'=12,'y'=8,'c'=2,'x'=4] {'c'}, dimensions={0}, use_global_device_ids=true | all-gather | bytes 18432 | tf_op jit(solution)/shard_map/all_gather | solution.py:71
  14.7 1.3 %collective-permute-start = (f32[3,2,128]{2,1,0:T(2,128)S(1)}, f32[3,2,128]{2,1,0:T(2,128)S(1)}, u32[]{:S(2)}, u32[]{:S(2)}) collective-permute-start(f32[3,2,128]{2,1,0:T(2,128)S(1)} %maximum_select_fusion), channel_id=1, source_target_pairs={{0,8},{8,16},{16,24},{24,32},{32,40},{40,48},{48,56},{56,64},{64,7... | collective-permute-start | bytes 9224 | tf_op jit(solution)/shard_map/ppermute | solution.py:77
  16.0 1.3 %collective-permute-start.1 = (f32[2,2,128]{2,1,0:T(2,128)S(1)}, f32[2,2,128]{2,1,0:T(2,128)S(1)}, u32[]{:S(2)}, u32[]{:S(2)}) collective-permute-start(f32[2,2,128]{2,1,0:T(2,128)S(1)} %maximum_select_fusion.2), channel_id=1, source_target_pairs={{0,1},{1,2},{2,3},{5,4},{6,5},{7,6},{8,9},{9,10},{10,11},{13,12},{... | collective-permute-start | bytes 6152 | tf_op jit(solution)/shard_map/ppermute | solution.py:78
  17.3 0.0 copy-start
  17.4 0.0 copy-start.1
  17.4 0.0 copy-start.2
  17.4 1.7 %shard_map.123 = (bf16[768,256]{1,0:T(8,128)(2,1)S(1)}, f32[2,512]{1,0:T(2,128)S(1)}, bf16[768,768]{1,0:T(8,128)(2,1)S(1)}) custom-call(f32[2,768]{1,0:T(2,128)S(1)} %get-tuple-element.15.iterate, bf16[768,768]{1,0:T(8,128)(2,1)} %stiff.3, s32[6,1,128]{2,1,0:T(1,128)} %bitcast.11, bf16[768,768]{1,0:T(8,128)(2,1)} %inverse.2), custom_call_target="tpu_custom_call" | custom-call | tf_op jit(solution)/shard_map/pallas_call | solution.py:24
  19.1 1.3 %collective-permute-done.1 = f32[2,2,128]{2,1,0:T(2,128)S(1)} collective-permute-done((f32[2,2,128]{2,1,0:T(2,128)S(1)}, f32[2,2,128]{2,1,0:T(2,128)S(1)}, u32[]{:S(2)}, u32[]{:S(2)}) %collective-permute-start.1) | collective-permute-done | bytes 2080 | tf_op jit(solution)/shard_map/ppermute | solution.py:78
  20.4 0.0 collective-permute-done
  20.4 1.8 %all_gather.13.moved = f32[10,2,128]{2,1,0:T(2,128)S(1)} all-gather(f32[5,2,128]{2,1,0:T(2,128)S(1)} %pad_maximum_fusion), channel_id=1, replica_groups=mesh['z'=12,'y'=8,'c'=2,'x'=4] {'c'}, dimensions={0}, use_global_device_ids=true | all-gather | bytes 15360 | tf_op jit(solution)/shard_map/all_gather | solution.py:79
  22.2 0.0 copy-done
  22.2 0.0 copy-done.1
  22.2 0.0 copy-done.2
  22.2 0.0 copy-start.3
  22.2 0.5 shard_map.124
  22.7 13.8 %all_to_all.10 = f32[64,1,128]{2,1,0:T(1,128)S(1)} all-to-all(f32[64,1,128]{2,1,0:T(1,128)S(1)} %bitcast.8), channel_id=1, replica_groups=mesh['z'=12,'y'=8,'c'=2,'x'=4] {'y','c','x'}, dimensions={0} | all-to-all | bytes 65536 | tf_op jit(solution)/shard_map/all_to_all | solution.py:225
  36.5 0.1 shard_map.125
  36.6 24.6 %all_to_all.11.gathered = f32[12,24,128]{2,1,0:T(8,128)S(1)} all-to-all(f32[12,24,128]{2,1,0:T(8,128)S(1)} %shard_map.125), channel_id=1, replica_groups=mesh['z'=12,'y'=8,'c'=2,'x'=4] {'z'}, dimensions={0} | all-to-all | bytes 294912 | tf_op jit(solution)/shard_map/all_to_all | solution.py:229
  61.3 0.0 copy-done.3
  61.3 0.8 %shard_map.126 = (f32[2,768]{1,0:T(2,128)S(1)}, f32[6,2,128]{2,1,0:T(2,128)S(1)}) custom-call(f32[12,24,128]{2,1,0:T(8,128)S(1)} %all_to_all.11.gathered, f32[24,18432]{1,0:T(8,128)S(1)} %copy-done, bf16[24,768]{1,0:T(8,128)(2,1)S(1)} %copy-done.1, f32[6,128]{1,0:T(8,128)S(1)} %bitcast.9, f32[1,768]{1,0:T(1,128)S(1)} %get-tuple-element.20.mask, ...), custom_call_target="tpu_custom_call" | custom-call | tf_op jit(solution)/shard_map/pallas_call | solution.py:24
  62.1 4.4 %all_gather.14.both = f32[12,2,128]{2,1,0:T(2,128)S(1)} all-gather(f32[6,2,128]{2,1,0:T(2,128)S(1)} %get-tuple-element.26), channel_id=1, replica_groups=mesh['z'=12,'y'=8,'c'=2,'x'=4] {'c'}, dimensions={0}, use_global_device_ids=true | all-gather | bytes 18432 | tf_op jit(solution)/shard_map/all_gather | solution.py:71
  66.5 1.3 %collective-permute-start.2 = (f32[3,2,128]{2,1,0:T(2,128)S(1)}, f32[3,2,128]{2,1,0:T(2,128)S(1)}, u32[]{:S(2)}, u32[]{:S(2)}) collective-permute-start(f32[3,2,128]{2,1,0:T(2,128)S(1)} %maximum_select_fusion.1), channel_id=1, source_target_pairs={{0,8},{8,16},{16,24},{24,32},{32,40},{40,48},{48,56},{56,64},{64,7... | collective-permute-start | bytes 9224 | tf_op jit(solution)/shard_map/ppermute | solution.py:77
  67.8 1.3 %collective-permute-start.3 = (f32[2,2,128]{2,1,0:T(2,128)S(1)}, f32[2,2,128]{2,1,0:T(2,128)S(1)}, u32[]{:S(2)}, u32[]{:S(2)}) collective-permute-start(f32[2,2,128]{2,1,0:T(2,128)S(1)} %maximum_select_fusion.3), channel_id=1, source_target_pairs={{0,1},{1,2},{2,3},{5,4},{6,5},{7,6},{8,9},{9,10},{10,11},{13,12},{... | collective-permute-start | bytes 6152 | tf_op jit(solution)/shard_map/ppermute | solution.py:78
  69.1 0.6 copy.15
  69.7 2.4 %collective-permute-done.3 = f32[2,2,128]{2,1,0:T(2,128)S(1)} collective-permute-done((f32[2,2,128]{2,1,0:T(2,128)S(1)}, f32[2,2,128]{2,1,0:T(2,128)S(1)}, u32[]{:S(2)}, u32[]{:S(2)}) %collective-permute-start.3) | collective-permute-done | bytes 2080 | tf_op jit(solution)/shard_map/ppermute | solution.py:78
  72.1 0.0 collective-permute-done.2
  72.2 2.7 %all_gather.15.moved = f32[10,2,128]{2,1,0:T(2,128)S(1)} all-gather(f32[5,2,128]{2,1,0:T(2,128)S(1)} %pad_maximum_fusion.1), channel_id=1, replica_groups=mesh['z'=12,'y'=8,'c'=2,'x'=4] {'c'}, dimensions={0}, use_global_device_ids=true | all-gather | bytes 15360 | tf_op jit(solution)/shard_map/all_gather | solution.py:79
  74.8 0.1 shard_map.127
  75.0 0.6 copy.14
  (8 shorter events, 0.0 us)
Async XLA Ops:
  14.7 5.6 %collective-permute-start = (f32[3,2,128]{2,1,0:T(2,128)S(1)}, f32[3,2,128]{2,1,0:T(2,128)S(1)}, u32[]{:S(2)}, u32[]{:S(2)}) collective-permute-start(f32[3,2,128]{2,1,0:T(2,128)S(1)} %maximum_select_fusion), channel_id=1, source_target_pairs={{0,8},{8,16},{16,24},{24,32},{32,40},{40,48},{48,56},{56,64},{64,7... | collective-permute-start | bytes 9224 | tf_op jit(solution)/shard_map/ppermute | solution.py:77
  16.0 4.3 %collective-permute-start.1 = (f32[2,2,128]{2,1,0:T(2,128)S(1)}, f32[2,2,128]{2,1,0:T(2,128)S(1)}, u32[]{:S(2)}, u32[]{:S(2)}) collective-permute-start(f32[2,2,128]{2,1,0:T(2,128)S(1)} %maximum_select_fusion.2), channel_id=1, source_target_pairs={{0,1},{1,2},{2,3},{5,4},{6,5},{7,6},{8,9},{9,10},{10,11},{13,12},{... | collective-permute-start | bytes 6152 | tf_op jit(solution)/shard_map/ppermute | solution.py:78
  17.3 4.9 %copy-start = (f32[24,18432]{1,0:T(8,128)S(1)}, f32[24,18432]{1,0:T(8,128)}, u32[]{:S(2)}) copy-start(f32[24,18432]{1,0:T(8,128)} %inverse.3) | copy-start | bytes 5308420
  17.4 4.9 %copy-start.1 = (bf16[24,768]{1,0:T(8,128)(2,1)S(1)}, bf16[24,768]{1,0:T(8,128)(2,1)}, u32[]{:S(2)}) copy-start(bf16[24,768]{1,0:T(8,128)(2,1)} %basis.3) | copy-start | bytes 110596
  17.4 4.9 %copy-start.2 = (f32[2,768]{1,0:T(2,128)S(1)}, f32[2,768]{1,0:T(2,128)}, u32[]{:S(2)}) copy-start(f32[2,768]{1,0:T(2,128)} %rhs.1) | copy-start | bytes 18436
  22.2 39.1 %copy-start.3 = (f32[768]{0:T(1024)S(1)}, f32[768]{0:T(1024)}, u32[]{:S(2)}) copy-start(f32[768]{0:T(1024)} %param.16) | copy-start | bytes 9220
  66.5 5.6 %collective-permute-start.2 = (f32[3,2,128]{2,1,0:T(2,128)S(1)}, f32[3,2,128]{2,1,0:T(2,128)S(1)}, u32[]{:S(2)}, u32[]{:S(2)}) collective-permute-start(f32[3,2,128]{2,1,0:T(2,128)S(1)} %maximum_select_fusion.1), channel_id=1, source_target_pairs={{0,8},{8,16},{16,24},{24,32},{32,40},{40,48},{48,56},{56,64},{64,7... | collective-permute-start | bytes 9224 | tf_op jit(solution)/shard_map/ppermute | solution.py:77
  67.8 4.3 %collective-permute-start.3 = (f32[2,2,128]{2,1,0:T(2,128)S(1)}, f32[2,2,128]{2,1,0:T(2,128)S(1)}, u32[]{:S(2)}, u32[]{:S(2)}) collective-permute-start(f32[2,2,128]{2,1,0:T(2,128)S(1)} %maximum_select_fusion.3), channel_id=1, source_target_pairs={{0,1},{1,2},{2,3},{5,4},{6,5},{7,6},{8,9},{9,10},{10,11},{13,12},{... | collective-permute-start | bytes 6152 | tf_op jit(solution)/shard_map/ppermute | solution.py:78

commit v4 on v3

--- a/solution.py
+++ b/solution.py
@@ -18,9 +18,9 @@
 LEAN = pltpu.CompilerParams(vmem_limit_bytes=8 << 20)
 
 
-def on_chip(kernel, out_shape, args, far=(), scratch=(), scalars=()):
-    spaces = [pltpu.SMEM if i in scalars else pltpu.HBM if i in far else pltpu.VMEM for i in range(len(args))]
-    args = [a if i in scalars else pltpu.with_memory_space_constraint(a, spaces[i]) for i, a in enumerate(args)]
+def on_chip(kernel, out_shape, args, far=(), scratch=(), loose=()):
+    spaces = [pl.ANY if i in loose else pltpu.HBM if i in far else pltpu.VMEM for i in range(len(args))]
+    args = [a if i in loose else pltpu.with_memory_space_constraint(a, spaces[i]) for i, a in enumerate(args)]
     return pl.pallas_call(
         kernel,
         in_specs=[pl.BlockSpec(memory_space=space) for space in spaces],
@@ -80,12 +80,17 @@
     return both, moved
 
 
-def first_kernel(start, stiff, orders, out_rows, counts, select, edge, mask, iterate, own, columns, fields, listing, count, done):
+def first_kernel(
+    start, stiff, orders, out_rows, counts, in_rows, select, edge, mask, iterate, own, beyond, arriving, columns, fields, listing, order, count, done
+):
     copies = [
         pltpu.make_async_copy(counts, count, done.at[0]),
         pltpu.make_async_copy(out_rows, listing, done.at[1]),
-        pltpu.make_async_copy(start, fields, done.at[2]),
-        pltpu.make_async_copy(stiff.at[:, pl.ds(0, EDGE)], columns, done.at[3]),
+        pltpu.make_async_copy(orders, order, done.at[2]),
+        pltpu.make_async_copy(start, fields, done.at[3]),
+        pltpu.make_async_copy(stiff.at[:, pl.ds(0, EDGE)], columns, done.at[4]),
+        pltpu.make_async_copy(in_rows, arriving, done.at[5]),
+        pltpu.make_async_copy(stiff.at[:, pl.ds(EDGE, N - EDGE)], beyond, done.at[6]),
     ]
     for copy in copies:
         copy.start()
@@ -96,33 +101,26 @@
     for j in range(6):
         listed = jnp.where(slots < count[0, j], listing[j], -1)
         select[:, j * H : (j + 1) * H] = (rows == listed).astype(F32).astype(BF16)
-    kept = lax.broadcasted_iota(jnp.int32, (1, N), 1) < orders[0]
+    copies[2].wait()
+    kept = lax.broadcasted_iota(jnp.int32, (1, N), 1) < order[0]
     mask[...] = kept.astype(F32)
-    copies[2].wait()
+    copies[3].wait()
     masked = jnp.where(kept, fields[...], 0.0)
     iterate[...] = masked
-    copies[3].wait()
+    copies[4].wait()
     product = jnp.dot(masked.astype(BF16), columns[...], preferred_element_type=F32)
     edge[...] = product
     write_slots(product, select[...], own)
-
-
-def rest_kernel(iterate, stiff, in_rows, inverse, spread, rest, held, columns, listing, done):
-    copies = [
-        pltpu.make_async_copy(in_rows, listing, done.at[0]),
-        pltpu.make_async_copy(stiff.at[:, pl.ds(EDGE, N - EDGE)], columns, done.at[1]),
-        pltpu.make_async_copy(inverse, held, done.at[2]),
-    ]
-    for copy in copies:
-        copy.start()
+    copies[5].wait()
+    copies[6].wait()
+
+
+def rest_kernel(iterate, beyond, arriving, spread, rest):
     rows = lax.broadcasted_iota(jnp.int32, (EDGE, H), 0)
-    copies[0].wait()
     for j in range(6):
-        hit = (rows == listing[j]).astype(F32)
+        hit = (rows == arriving[j]).astype(F32)
         spread[j * H : (j + 1) * H, :] = hit.T.astype(BF16)
-    copies[1].wait()
-    rest[...] = jnp.dot(iterate[...].astype(BF16), columns[...], preferred_element_type=F32)
-    copies[2].wait()
+    rest[...] = jnp.dot(iterate[...].astype(BF16), beyond[...], preferred_element_type=F32)
 
 
 def residual_kernel(edge, rest, both, moved, spread, rhs, mask, basis, _, residual, rounded, rows):
@@ -194,27 +192,32 @@
     out_rows = out_rows.reshape(6, 1, H)
     in_rows = in_rows.reshape(6, 1, H)
     slots = ((6, 2, H), F32)
-    listing = pltpu.VMEM((6, 1, H), jnp.int32)
-    select, edge, mask, iterate, own = on_chip(
+    select, edge, mask, iterate, own, beyond, arriving = on_chip(
         first_kernel,
-        [((EDGE, 6 * H), BF16), ((2, EDGE), F32), ((1, N), F32), ((2, N), F32), slots],
-        [start, stiffness, orders, out_rows, out_counts],
-        far=(0, 1, 3, 4),
-        scalars=(2,),
+        [
+            ((EDGE, 6 * H), BF16),
+            ((2, EDGE), F32),
+            ((1, N), F32),
+            ((2, N), F32),
+            slots,
+            ((N, N - EDGE), BF16),
+            ((6, 1, H), jnp.int32),
+        ],
+        [start, stiffness, orders, out_rows, out_counts, in_rows],
+        far=(0, 1, 3, 4, 5),
+        loose=(2,),
         scratch=[
             pltpu.VMEM((N, EDGE), BF16),
             pltpu.VMEM((2, N), F32),
-            listing,
+            pltpu.VMEM((6, 1, H), jnp.int32),
+            pltpu.SMEM((1,), jnp.int32),
             pltpu.SMEM((1, 6), jnp.int32),
-            pltpu.SemaphoreType.DMA((4,)),
+            pltpu.SemaphoreType.DMA((7,)),
         ],
     )
-    spread, rest, held = on_chip(
-        rest_kernel,
-        [((6 * H, EDGE), BF16), ((2, N - EDGE), F32), ((N, N), BF16)],
-        [iterate, stiffness, in_rows, local_inverse],
-        far=(1, 2, 3),
-        scratch=[pltpu.VMEM((N, N - EDGE), BF16), listing, pltpu.SemaphoreType.DMA((3,))],
+    coarse_inverse, own = lax.optimization_barrier((coarse_inverse, own))
+    spread, rest = on_chip(
+        rest_kernel, [((6 * H, EDGE), BF16), ((2, N - EDGE), F32)], [iterate, beyond, arriving]
     )
     both, moved = exchange(own)
     residual, rounded, rows = on_chip(
@@ -230,7 +233,7 @@
     correction, own = on_chip(
         coarse_kernel,
         [((2, N), F32), slots],
-        [gathered, coarse_inverse, basis, weights.reshape(6, 128), mask, rounded, held, select],
+        [gathered, coarse_inverse, basis, weights.reshape(6, 128), mask, rounded, local_inverse, select],
     )
     both, moved = exchange(own)
     (solved,) = on_chip(last_kernel, [((2, N), F32)], [iterate, correction, both, moved, spread])

time: 75.9 us -> 76.1 us (level)
  waiting for transfers between devices: 3.75 us -> 5.25 us
  Pallas kernels: 4.67 us -> 3.22 us
    ppermute x2, waiting for transfers between devices: 3.74 us -> 5.24 us  [exchange(): got_x = lax.ppermute(along_x, ('c', 'x'), route_x)]
    pallas_call x6, Pallas kernels: 4.67 us -> 3.22 us  [on_chip(): pl.pallas_call(kernel, in_specs=[pl.BlockSpec(memory_space=space) for spa...]
  transfers between devices with their start and end apart: 4 -> 4, of which waited for: 2 -> 2; matrix products, arithmetic and copies ran while one was open for 1% -> 1% of each run, Pallas kernels for 2% -> 0%
where the time goes in v4:
time: 76.1 us; the launch traced here: 75.8 us
  blocking collectives  59.3 us (78%)
  waiting for transfers between devices  5.25 us (7%)
  starting transfers between devices  5.17 us (7%)
  Pallas kernels  3.22 us (4%)
  between operations  1.54 us (2%)
  local copies, waits for them, and re-layouts  1.27 us (2%)
    all_to_all x1, blocking collectives, per_device(): gathered = lax.all_to_all(gathered, 'z', 0, 0)  25.2 us
    all_gather x2, blocking collectives, exchange(): both = lax.all_gather(own, 'c', axis=0, tiled=True)  16.3 us
    all_to_all x1, blocking collectives, per_device(): lax.all_to_all(rows.reshape(PLANE, 1, 128), ('y', 'c', 'x'), 0, 0)  13.3 us
    ppermute x2, waiting for transfers between devices, exchange(): got_x = lax.ppermute(along_x, ('c', 'x'), route_x)  5.24 us
    all_gather x2, blocking collectives, exchange(): lax.all_gather(jnp.concatenate([got_y, got_x]), 'c', axis=0, tiled=True)  4.47 us
    pallas_call x6, Pallas kernels, on_chip(): pl.pallas_call(kernel, in_specs=[pl.BlockSpec(memory_space=space) for spa...  3.22 us
    ppermute x2, starting transfers between devices, exchange(): got_x = lax.ppermute(along_x, ('c', 'x'), route_x)  2.58 us
    ppermute x2, starting transfers between devices, exchange(): got_y = lax.ppermute(along_y, CHIPS, route_y)  2.58 us
  transfers between devices with their start and end apart: 4, of which 2 were waited for; matrix products, arithmetic and copies ran while one was open for 1% of the time, Pallas kernels for 0%

profile of v4, /device:TPU:1, one launch (start us, length us, event | category | flops | bytes accessed | tf_op | source)
XLA Modules:
  0.0 75.8 jit_solution(4841716013751920648)
XLA Ops:
  0.6 0.0 copy-start
  0.6 0.0 copy-start.3
  0.7 0.0 copy-start.2
  1.4 1.5 %shard_map.122 = (bf16[256,768]{1,0:T(8,128)(2,1)S(1)}, f32[2,256]{1,0:T(2,128)S(1)}, f32[1,768]{1,0:T(1,128)S(1)}, f32[2,768]{1,0:T(2,128)S(1)}, f32[6,2,128]{2...) custom-call(f32[2,768]{1,0:T(2,128)} %start.1, bf16[768,768]{1,0:T(8,128)(2,1)} %stiff.1, ...), custom_call_target="tpu_custom_call" | custom-call | tf_op jit(solution)/shard_map/pallas_call | solution.py:24
  3.0 11.9 %all_gather.12.both = f32[12,2,128]{2,1,0:T(2,128)S(1)} all-gather(f32[6,2,128]{2,1,0:T(2,128)S(1)} %get-tuple-element.24), channel_id=1, replica_groups=mesh['z'=12,'y'=8,'c'=2,'x'=4] {'c'}, dimensions={0}, use_global_device_ids=true | all-gather | bytes 18432 | tf_op jit(solution)/shard_map/all_gather | solution.py:71
  14.9 1.3 %collective-permute-start = (f32[3,2,128]{2,1,0:T(2,128)S(1)}, f32[3,2,128]{2,1,0:T(2,128)S(1)}, u32[]{:S(2)}, u32[]{:S(2)}) collective-permute-start(f32[3,2,128]{2,1,0:T(2,128)S(1)} %maximum_select_fusion), channel_id=1, source_target_pairs={{0,8},{8,16},{16,24},{24,32},{32,40},{40,48},{48,56},{56,64},{64,7... | collective-permute-start | bytes 9224 | tf_op jit(solution)/shard_map/ppermute | solution.py:77
  16.2 1.3 %collective-permute-start.1 = (f32[2,2,128]{2,1,0:T(2,128)S(1)}, f32[2,2,128]{2,1,0:T(2,128)S(1)}, u32[]{:S(2)}, u32[]{:S(2)}) collective-permute-start(f32[2,2,128]{2,1,0:T(2,128)S(1)} %maximum_select_fusion.2), channel_id=1, source_target_pairs={{0,1},{1,2},{2,3},{5,4},{6,5},{7,6},{8,9},{9,10},{10,11},{13,12},{... | collective-permute-start | bytes 6152 | tf_op jit(solution)/shard_map/ppermute | solution.py:78
  17.5 0.2 shard_map.123
  17.7 2.8 %collective-permute-done.1 = f32[2,2,128]{2,1,0:T(2,128)S(1)} collective-permute-done((f32[2,2,128]{2,1,0:T(2,128)S(1)}, f32[2,2,128]{2,1,0:T(2,128)S(1)}, u32[]{:S(2)}, u32[]{:S(2)}) %collective-permute-start.1) | collective-permute-done | bytes 2080 | tf_op jit(solution)/shard_map/ppermute | solution.py:78
  20.6 0.0 collective-permute-done
  20.6 1.8 %all_gather.13.moved = f32[10,2,128]{2,1,0:T(2,128)S(1)} all-gather(f32[5,2,128]{2,1,0:T(2,128)S(1)} %pad_maximum_fusion), channel_id=1, replica_groups=mesh['z'=12,'y'=8,'c'=2,'x'=4] {'c'}, dimensions={0}, use_global_device_ids=true | all-gather | bytes 15360 | tf_op jit(solution)/shard_map/all_gather | solution.py:79
  22.4 0.0 copy-done
  22.4 0.0 copy-done.3
  22.4 0.0 copy-done.2
  22.4 0.0 copy-start.1
  22.4 0.0 copy-start.4
  22.4 0.5 shard_map.124
  22.9 13.3 %all_to_all.10 = f32[64,1,128]{2,1,0:T(1,128)S(1)} all-to-all(f32[64,1,128]{2,1,0:T(1,128)S(1)} %bitcast.8), channel_id=1, replica_groups=mesh['z'=12,'y'=8,'c'=2,'x'=4] {'y','c','x'}, dimensions={0} | all-to-all | bytes 65536 | tf_op jit(solution)/shard_map/all_to_all | solution.py:228
  36.2 0.1 shard_map.125
  36.3 25.2 %all_to_all.11.gathered = f32[12,24,128]{2,1,0:T(8,128)S(1)} all-to-all(f32[12,24,128]{2,1,0:T(8,128)S(1)} %shard_map.125), channel_id=1, replica_groups=mesh['z'=12,'y'=8,'c'=2,'x'=4] {'z'}, dimensions={0} | all-to-all | bytes 294912 | tf_op jit(solution)/shard_map/all_to_all | solution.py:232
  61.5 0.0 copy-done.1
  61.5 0.0 copy-done.4
  61.5 0.8 %shard_map.126 = (f32[2,768]{1,0:T(2,128)S(1)}, f32[6,2,128]{2,1,0:T(2,128)S(1)}) custom-call(f32[12,24,128]{2,1,0:T(8,128)S(1)} %all_to_all.11.gathered, f32[24,18432]{1,0:T(8,128)S(1)} %copy-done, bf16[24,768]{1,0:T(8,128)(2,1)S(1)} %copy-done.2, f32[6,128]{1,0:T(8,128)S(1)} %bitcast.9, f32[1,768]{1,0:T(1,128)S(1)} %get-tuple-element.26.mask, ...), custom_call_target="tpu_custom_call" | custom-call | tf_op jit(solution)/shard_map/pallas_call | solution.py:24
  62.3 4.4 %all_gather.14.both = f32[12,2,128]{2,1,0:T(2,128)S(1)} all-gather(f32[6,2,128]{2,1,0:T(2,128)S(1)} %get-tuple-element.32), channel_id=1, replica_groups=mesh['z'=12,'y'=8,'c'=2,'x'=4] {'c'}, dimensions={0}, use_global_device_ids=true | all-gather | bytes 18432 | tf_op jit(solution)/shard_map/all_gather | solution.py:71
  66.7 1.3 %collective-permute-start.2 = (f32[3,2,128]{2,1,0:T(2,128)S(1)}, f32[3,2,128]{2,1,0:T(2,128)S(1)}, u32[]{:S(2)}, u32[]{:S(2)}) collective-permute-start(f32[3,2,128]{2,1,0:T(2,128)S(1)} %maximum_select_fusion.1), channel_id=1, source_target_pairs={{0,8},{8,16},{16,24},{24,32},{32,40},{40,48},{48,56},{56,64},{64,7... | collective-permute-start | bytes 9224 | tf_op jit(solution)/shard_map/ppermute | solution.py:77
  68.0 1.3 %collective-permute-start.3 = (f32[2,2,128]{2,1,0:T(2,128)S(1)}, f32[2,2,128]{2,1,0:T(2,128)S(1)}, u32[]{:S(2)}, u32[]{:S(2)}) collective-permute-start(f32[2,2,128]{2,1,0:T(2,128)S(1)} %maximum_select_fusion.3), channel_id=1, source_target_pairs={{0,1},{1,2},{2,3},{5,4},{6,5},{7,6},{8,9},{9,10},{10,11},{13,12},{... | collective-permute-start | bytes 6152 | tf_op jit(solution)/shard_map/ppermute | solution.py:78
  69.3 0.6 copy.15
  69.9 2.4 %collective-permute-done.3 = f32[2,2,128]{2,1,0:T(2,128)S(1)} collective-permute-done((f32[2,2,128]{2,1,0:T(2,128)S(1)}, f32[2,2,128]{2,1,0:T(2,128)S(1)}, u32[]{:S(2)}, u32[]{:S(2)}) %collective-permute-start.3) | collective-permute-done | bytes 2080 | tf_op jit(solution)/shard_map/ppermute | solution.py:78
  72.3 0.0 collective-permute-done.2
  72.3 2.7 %all_gather.15.moved = f32[10,2,128]{2,1,0:T(2,128)S(1)} all-gather(f32[5,2,128]{2,1,0:T(2,128)S(1)} %pad_maximum_fusion.1), channel_id=1, replica_groups=mesh['z'=12,'y'=8,'c'=2,'x'=4] {'c'}, dimensions={0}, use_global_device_ids=true | all-gather | bytes 15360 | tf_op jit(solution)/shard_map/all_gather | solution.py:79
  75.0 0.1 shard_map.127
  75.1 0.6 copy.14
  (8 shorter events, 0.0 us)
Async XLA Ops:
  0.6 21.8 %copy-start = (f32[24,18432]{1,0:T(8,128)S(1)}, f32[24,18432]{1,0:T(8,128)}, u32[]{:S(2)}) copy-start(f32[24,18432]{1,0:T(8,128)} %inverse) | copy-start | bytes 5308420
  0.6 21.8 %copy-start.3 = (f32[2,768]{1,0:T(2,128)S(1)}, f32[2,768]{1,0:T(2,128)}, u32[]{:S(2)}) copy-start(f32[2,768]{1,0:T(2,128)} %rhs.1) | copy-start | bytes 18436
  0.7 21.8 %copy-start.2 = (bf16[24,768]{1,0:T(8,128)(2,1)S(1)}, bf16[24,768]{1,0:T(8,128)(2,1)}, u32[]{:S(2)}) copy-start(bf16[24,768]{1,0:T(8,128)(2,1)} %basis.3) | copy-start | bytes 110596
  14.9 5.6 %collective-permute-start = (f32[3,2,128]{2,1,0:T(2,128)S(1)}, f32[3,2,128]{2,1,0:T(2,128)S(1)}, u32[]{:S(2)}, u32[]{:S(2)}) collective-permute-start(f32[3,2,128]{2,1,0:T(2,128)S(1)} %maximum_select_fusion), channel_id=1, source_target_pairs={{0,8},{8,16},{16,24},{24,32},{32,40},{40,48},{48,56},{56,64},{64,7... | collective-permute-start | bytes 9224 | tf_op jit(solution)/shard_map/ppermute | solution.py:77
  16.2 4.3 %collective-permute-start.1 = (f32[2,2,128]{2,1,0:T(2,128)S(1)}, f32[2,2,128]{2,1,0:T(2,128)S(1)}, u32[]{:S(2)}, u32[]{:S(2)}) collective-permute-start(f32[2,2,128]{2,1,0:T(2,128)S(1)} %maximum_select_fusion.2), channel_id=1, source_target_pairs={{0,1},{1,2},{2,3},{5,4},{6,5},{7,6},{8,9},{9,10},{10,11},{13,12},{... | collective-permute-start | bytes 6152 | tf_op jit(solution)/shard_map/ppermute | solution.py:78
  22.4 39.1 %copy-start.1 = (bf16[768,768]{1,0:T(8,128)(2,1)S(1)}, bf16[768,768]{1,0:T(8,128)(2,1)}, u32[]{:S(2)}) copy-start(bf16[768,768]{1,0:T(8,128)(2,1)} %held.1) | copy-start | bytes 3538948
  22.4 39.1 %copy-start.4 = (f32[768]{0:T(1024)S(1)}, f32[768]{0:T(1024)}, u32[]{:S(2)}) copy-start(f32[768]{0:T(1024)} %param.16) | copy-start | bytes 9220
  66.7 5.6 %collective-permute-start.2 = (f32[3,2,128]{2,1,0:T(2,128)S(1)}, f32[3,2,128]{2,1,0:T(2,128)S(1)}, u32[]{:S(2)}, u32[]{:S(2)}) collective-permute-start(f32[3,2,128]{2,1,0:T(2,128)S(1)} %maximum_select_fusion.1), channel_id=1, source_target_pairs={{0,8},{8,16},{16,24},{24,32},{32,40},{40,48},{48,56},{56,64},{64,7... | collective-permute-start | bytes 9224 | tf_op jit(solution)/shard_map/ppermute | solution.py:77
  68.0 4.3 %collective-permute-start.3 = (f32[2,2,128]{2,1,0:T(2,128)S(1)}, f32[2,2,128]{2,1,0:T(2,128)S(1)}, u32[]{:S(2)}, u32[]{:S(2)}) collective-permute-start(f32[2,2,128]{2,1,0:T(2,128)S(1)} %maximum_select_fusion.3), channel_id=1, source_target_pairs={{0,1},{1,2},{2,3},{5,4},{6,5},{7,6},{8,9},{9,10},{10,11},{13,12},{... | collective-permute-start | bytes 6152 | tf_op jit(solution)/shard_map/ppermute | solution.py:78

commit v5 on v4

v5 whole, which is shorter than its diff:
```python
import jax
import jax.numpy as jnp
from jax import lax
from jax.experimental import pallas as pl
from jax.experimental.pallas import tpu as pltpu
from jax.sharding import Mesh
from jax.sharding import PartitionSpec as P

Z, Y, C, X = 12, 8, 2, 4
LAYER = Y * X
HALF = Z * LAYER * 24
N = 768
NV = 24
H = 128
EDGE = 256
F32, BF16 = jnp.float32, jnp.bfloat16
ALL = ("z", "y", "c", "x")
CHIPS = ("z", "y", "c")
LEAN = pltpu.CompilerParams(vmem_limit_bytes=8 << 20)


def on_chip(kernel, out_shape, args, far=(), scratch=(), loose=()):
    spaces = [pl.ANY if i in loose else pltpu.HBM if i in far else pltpu.VMEM for i in range(len(args))]
    args = [a if i in loose else pltpu.with_memory_space_constraint(a, spaces[i]) for i, a in enumerate(args)]
    return pl.pallas_call(
        kernel,
        in_specs=[pl.BlockSpec(memory_space=space) for space in spaces],
        out_specs=[pl.BlockSpec(memory_space=pltpu.VMEM)] * len(out_shape),
        out_shape=[pltpu.VMEM(shape, dtype) for shape, dtype in out_shape],
        scratch_shapes=list(scratch),
        compiler_params=LEAN,
    )(*args)


def thirds(value):
    high = value.astype(BF16)
    rest = value - high.astype(F32)
    middle = rest.astype(BF16)
    low = (rest - middle.astype(F32)).astype(BF16)
    return jnp.concatenate([high, middle, low], axis=0)


def times_selection(value, selection):
    parts = jnp.dot(thirds(value), selection, preferred_element_type=F32)
    return parts[0:2] + parts[2:4] + parts[4:6]


def selection_of(listed):
    rows = lax.broadcasted_iota(jnp.int32, (EDGE, H), 0)
    return [(rows == one).astype(F32).astype(BF16) for one in listed]


def spread_of(arriving):
    rows = lax.broadcasted_iota(jnp.int32, (EDGE, H), 0)
    return jnp.concatenate([(rows == arriving[j]).astype(F32).T.astype(BF16) for j in range(6)], axis=0)


def arrivals(both, moved):
    first = lax.axis_index("c") == 0
    up, down, second = 0, moved.shape[0] // 2, both.shape[0] // 2
    return jnp.concatenate(
        [
            jnp.where(first, moved[up + 3], moved[up + 4]),
            jnp.where(first, moved[down + 3], moved[down + 4]),
            jnp.where(first, moved[up + 2], both[2]),
            jnp.where(first, both[second + 3], moved[down + 2]),
            jnp.where(first, moved[up], moved[up + 1]),
            jnp.where(first, moved[down], moved[down + 1]),
        ],
        axis=1,
    )


def across(both):
    chips = Z * Y
    first = lax.axis_index("c") == 0
    own, other = both[: both.shape[0] // 2], both[both.shape[0] // 2 :]
    along_x = jnp.where(first, jnp.stack([own[0], other[0]]), jnp.stack([own[1], other[1]]))
    along_y = jnp.where(first, jnp.stack([own[4], other[4], other[2]]), jnp.stack([own[5], other[5], own[3]]))
    route_y = [(2 * q, 2 * q + 2) for q in range(chips - 1)] + [(2 * q + 1, 2 * q - 1) for q in range(1, chips)]
    route_x = [(d, d + 1) for d in range(X - 1)] + [(X + d, X + d - 1) for d in range(1, X)]
    got_y = lax.ppermute(along_y, CHIPS, route_y)
    got_x = lax.ppermute(along_x, ("c", "x"), route_x)
    return [got_y, got_x]


def in_pair(value):
    return lax.all_gather(value, "c", axis=0, tiled=True)


def first_kernel(
    start, stiff, orders, out_rows, counts, in_rows, inverse, edge, mask, iterate, own, beyond, arriving, near, columns, fields, listing, order, count, done
):
    copies = [
        pltpu.make_async_copy(counts, count, done.at[0]),
        pltpu.make_async_copy(out_rows, listing, done.at[1]),
        pltpu.make_async_copy(orders, order, done.at[2]),
        pltpu.make_async_copy(start, fields, done.at[3]),
        pltpu.make_async_copy(stiff.at[:, pl.ds(0, EDGE)], columns, done.at[4]),
        pltpu.make_async_copy(in_rows, arriving, done.at[5]),
        pltpu.make_async_copy(stiff.at[:, pl.ds(EDGE, N - EDGE)], beyond, done.at[6]),
        pltpu.make_async_copy(inverse, near, done.at[7]),
    ]
    for copy in copies:
        copy.start()
    slots = lax.broadcasted_iota(jnp.int32, (1, H), 1)
    copies[0].wait()
    copies[1].wait()
    listed = [jnp.where(slots < count[0, j], listing[j], -1) for j in range(6)]
    select = selection_of(listed)
    for j in range(6):
        own[6 + j // 2, j % 2 : j % 2 + 1, :] = listed[j].astype(F32)
    copies[2].wait()
    kept = lax.broadcasted_iota(jnp.int32, (1, N), 1) < order[0]
    mask[...] = kept.astype(F32)
    copies[3].wait()
    masked = jnp.where(kept, fields[...], 0.0)
    iterate[...] = masked
    copies[4].wait()
    product = jnp.dot(masked.astype(BF16), columns[...], preferred_element_type=F32)
    edge[...] = product
    picked = times_selection(product, jnp.concatenate(select, axis=1))
    for j in range(6):
        own[j] = picked[:, j * H : (j + 1) * H]
    copies[5].wait()
    copies[6].wait()
    copies[7].wait()


def weight_row(weights):
    return jnp.concatenate([weights[j : j + 1, :] for j in range(6)], axis=1)


def rest_kernel(iterate, beyond, mask, weights, basis, inverse, rest, edges, mine, theirs):
    first = lax.axis_index("c") == 0
    rest[...] = jnp.dot(iterate[...].astype(BF16), beyond[...], preferred_element_type=F32)
    weighted = basis[...].astype(F32) * (weight_row(weights) * mask[...])
    for half in range(2):
        for row in range(0, NV, 2):
            edges[half * 12 + row // 2] = weighted[row : row + 2, half * H : (half + 1) * H]
    for group in range(HALF // 384):
        block = inverse[:, group * 768 : (group + 1) * 768]
        low = jnp.concatenate([block[:, k * 192 : k * 192 + 96] for k in range(4)], axis=1)
        high = jnp.concatenate([block[:, k * 192 + 96 : k * 192 + 192] for k in range(4)], axis=1)
        mine[:, group * 384 : (group + 1) * 384] = jnp.where(first, low, high)
        theirs[:, group * 384 : (group + 1) * 384] = jnp.where(first, high, low)


def residual_kernel(edge, rest, both, moved, arriving, rhs, mask, basis, residual, rounded, rows):
    summed = edge[...] + times_selection(arrivals(both, moved), spread_of(arriving))
    total = jnp.concatenate([summed, rest[...]], axis=1)
    value = jnp.where(mask[...] > 0.0, rhs[...] - total, 0.0)
    residual[...] = value
    rounded[...] = value.astype(BF16)
    padded = jnp.concatenate([value, jnp.zeros((6, N), F32)], axis=0).astype(BF16)
    coarse = lax.dot_general(padded, basis[...], (((1,), (1,)), ((), ())), preferred_element_type=F32)
    coarse = jnp.concatenate([coarse, jnp.zeros((8, 128 - NV), F32)], axis=1)
    place = lax.axis_index("y") * X + lax.axis_index("x")
    shift = (24 * place) % 128
    turned = pltpu.roll(coarse, shift, 1)
    turned_far = pltpu.roll(turned, 64, 1)
    rows[...] = jnp.broadcast_to(turned[0:1] + turned_far[1:2], (LAYER, 128))


def repack_kernel(rows, out, packed):
    taken = rows[...]
    far = pltpu.roll(taken, 64, 1)
    place = lax.broadcasted_iota(jnp.int32, (LAYER, 128), 0)
    lane = lax.broadcasted_iota(jnp.int32, (LAYER, 128), 1)
    within = (lane - NV * place + NV * LAYER) & 127
    row = jnp.where(within < NV, (NV * (place & 15) + within) >> 7, -1)
    for load, field in enumerate((taken, far)):
        for r in range(3):
            kept = jnp.where(row == r, field, 0.0)
            for group in range(2):
                packed[load * 6 + group * 3 + r : load * 6 + group * 3 + r + 1, :] = jnp.sum(
                    kept[group * 16 : (group + 1) * 16], axis=0, keepdims=True
                )
    whole = packed[...]
    for z in range(Z):
        out[z] = whole


def partial_kernel(gathered, mine, given, rounded, held, weights, mask, shared, local):
    first = lax.axis_index("c") == 0
    sums = [[[jnp.zeros((NV, 128), F32) for _ in range(2)] for _ in range(2)] for _ in range(2)]
    for t in range(HALF // 128):
        z, r = divmod(t, 6)
        blocks = [rows[:, t * 128 : (t + 1) * 128] for rows in (mine, given)]
        for load in range(2):
            factor = gathered[z, load * 6 + r : load * 6 + r + 1, :]
            for owner in range(2):
                sums[owner][load][t % 2] += blocks[owner] * factor
    lane = lax.broadcasted_iota(jnp.int32, (NV, 128), 1)
    tile = jnp.zeros((NV, 128), F32)
    for owner in range(2):
        at = jnp.where(first, 2 * owner, 2 - 2 * owner)
        for load in range(2):
            part = jnp.sum(sums[owner][load][0] + sums[owner][load][1], axis=1, keepdims=True)
            tile = jnp.where(lane == at + load, part, tile)
    shared[:NV] = tile
    weighted = weight_row(weights) * mask[...] * jnp.dot(rounded[...], held[...], preferred_element_type=F32)
    local[...] = weighted
    for load in range(2):
        for half in range(2):
            at = NV + 2 * load + half
            shared[at : at + 1, :] = weighted[load : load + 1, half * H : (half + 1) * H]
    shared[NV + 4 :] = jnp.zeros((4, 128), F32)


def coarse_kernel(shared, local, basis, weights, mask, moved, before, correction, both):
    first = lax.axis_index("c") == 0
    total = shared[:NV] + shared[32 : 32 + NV]
    total = total.astype(BF16).astype(F32)
    vectors = basis[...].astype(F32)
    partner_local = jnp.where(first, shared[56:60], shared[24:28])
    fixes, partner = [], []
    for load in range(2):
        pair = [total[:, load : load + 1], total[:, 2 + load : 3 + load]]
        coarse = jnp.where(first, pair[0], pair[1])
        fixes.append(jnp.sum(vectors * coarse, axis=0, keepdims=True))
        coarse = jnp.where(first, pair[1], pair[0])
        halves = []
        for half in range(2):
            terms = jnp.zeros((2, H), F32)
            for row in range(0, NV, 2):
                at = 5 + half * 12 + row // 2
                terms += jnp.where(first, moved[5 + NV + at], moved[at]) * coarse[row : row + 2]
            halves.append(partner_local[2 * load + half : 2 * load + half + 1, :] + jnp.sum(terms, axis=0, keepdims=True))
        partner.append(jnp.concatenate(halves, axis=1))
    value = local[...] + weight_row(weights) * mask[...] * jnp.concatenate(fixes, axis=0)
    correction[...] = value
    low = [before[6 + j // 2, j % 2 : j % 2 + 1, :].astype(jnp.int32) for j in range(6)]
    high = [before[15 + j // 2, j % 2 : j % 2 + 1, :].astype(jnp.int32) for j in range(6)]
    select = selection_of([jnp.where(first, low[j], high[j]) for j in range(6)])
    partner_select = selection_of([jnp.where(first, high[j], low[j]) for j in range(6)])
    own = times_selection(value[:, :EDGE], jnp.concatenate(select, axis=1))
    other = times_selection(jnp.concatenate(partner, axis=0), jnp.concatenate(partner_select, axis=1))
    for j in range(6):
        mine, theirs = own[:, j * H : (j + 1) * H], other[:, j * H : (j + 1) * H]
        both[j] = jnp.where(first, mine, theirs)
        both[6 + j] = jnp.where(first, theirs, mine)


def last_kernel(iterate, correction, both, moved, arriving, solved):
    arrived = times_selection(arrivals(both, moved), spread_of(arriving))
    value = iterate[...] + correction[...]
    solved[...] = value
    solved[:, :EDGE] = value[:, :EDGE] + arrived


def per_device(
    rhs, start, stiffness, local_inverse, basis, weights, coarse_inverse, orders, out_rows, out_counts, in_rows
):
    out_rows = out_rows.reshape(6, 1, H)
    in_rows = in_rows.reshape(6, 1, H)
    weights = weights.reshape(6, 128)
    edge, mask, iterate, own, beyond, arriving, near = on_chip(
        first_kernel,
        [
            ((2, EDGE), F32),
            ((1, N), F32),
            ((2, N), F32),
            ((9, 2, H), F32),
            ((N, N - EDGE), BF16),
            ((6, 1, H), jnp.int32),
            ((NV, C * HALF), F32),
        ],
        [start, stiffness, orders, out_rows, out_counts, in_rows, coarse_inverse],
        far=(0, 1, 3, 4, 5, 6),
        loose=(2,),
        scratch=[
            pltpu.VMEM((N, EDGE), BF16),
            pltpu.VMEM((2, N), F32),
            pltpu.VMEM((6, 1, H), jnp.int32),
            pltpu.SMEM((1,), jnp.int32),
            pltpu.SMEM((1, 6), jnp.int32),
            pltpu.SemaphoreType.DMA((8,)),
        ],
    )
    both = in_pair(own)
    going = across(both)
    rest, edges, mine, theirs = on_chip(
        rest_kernel,
        [((2, N - EDGE), F32), ((NV, 2, H), F32), ((NV, HALF), F32), ((NV, HALF), F32)],
        [iterate, beyond, mask, weights, basis, near],
    )
    given = lax.ppermute(theirs, "c", [(0, 1), (1, 0)])
    before = both
    moved = in_pair(jnp.concatenate(going + [edges]))
    edges = moved
    residual, rounded, rows = on_chip(
        residual_kernel,
        [((2, N), F32), ((2, N), BF16), ((LAYER, 128), F32)],
        [edge, rest, both, moved, arriving, rhs, mask, basis],
    )
    rows = lax.all_to_all(rows.reshape(LAYER, 1, 128), ("y", "x"), 0, 0).reshape(LAYER, 128)
    (gathered,) = on_chip(repack_kernel, [((Z, 12, 128), F32)], [rows], scratch=[pltpu.VMEM((12, 128), F32)])
    gathered = lax.all_to_all(gathered, "z", 0, 0)
    shared, local = on_chip(
        partial_kernel,
        [((32, 128), F32), ((2, N), F32)],
        [gathered, mine, given, rounded, local_inverse, weights, mask],
    )
    correction, both = on_chip(
        coarse_kernel,
        [((2, N), F32), ((12, 2, H), F32)],
        [in_pair(shared), local, basis, weights, mask, edges, before],
    )
    moved = in_pair(jnp.concatenate(across(both)))
    (solved,) = on_chip(last_kernel, [((2, N), F32)], [iterate, correction, both, moved, arriving])
    return solved, residual


def solution(mesh):
    fine = Mesh(mesh.devices.reshape(Z, Y, C, X), ALL)
    return jax.shard_map(
        per_device,
        mesh=fine,
        in_specs=(
            P(None, ALL),
            P(None, ALL),
            P(ALL, None),
            P(ALL, None),
            P(None, ALL),
            P(ALL),
            P(ALL, None),
            P(ALL),
            P(ALL, None, None),
            P(ALL, None),
            P(ALL, None, None),
        ),
        out_specs=(P(None, ALL), P(None, ALL)),
        check_vma=False,
    )
```

time: 76.1 us -> 79.3 us (1.042)
  starting transfers between devices: 5.17 us -> 17.5 us
  blocking collectives: 59.3 us -> 47.7 us
  Pallas kernels: 3.22 us -> 5.52 us
    ppermute x4 -> x5, starting transfers between devices: 5.17 us -> 17.5 us  [the longest x1 12.4 us: per_device(): given = lax.ppermute(theirs, 'c', [(0, 1), (1, 0)])]
    all_gather x4, blocking collectives: 20.8 us -> 11.3 us  [in_pair(): return lax.all_gather(value, 'c', axis=0, tiled=True)]
    pallas_call x6 -> x7, Pallas kernels: 3.22 us -> 5.52 us  [on_chip(): pl.pallas_call(kernel, in_specs=[pl.BlockSpec(memory_space=space) for spa...]
    all_to_all x1, blocking collectives: 13.3 us -> 12.2 us  [per_device(): lax.all_to_all(rows.reshape(LAYER, 1, 128), ('y', 'x'), 0, 0)]
    all_to_all x1, blocking collectives: 25.2 us -> 24.2 us  [per_device(): gathered = lax.all_to_all(gathered, 'z', 0, 0)]
    ppermute x4 -> x5, waiting for transfers between devices: 5.25 us -> 5.47 us  [the longest x2 5.46 us: across(): got_x = lax.ppermute(along_x, ('c', 'x'), route_x)]
  transfers between devices with their start and end apart: 4 -> 5, of which waited for: 2 -> 2; matrix products, arithmetic and copies ran while one was open for 1% -> 1% of each run, Pallas kernels for 0% -> 1%
where the time goes in v5:
time: 79.3 us; the launch traced here: 78.9 us
  blocking collectives  47.7 us (60%)
  starting transfers between devices  17.5 us (22%)
  Pallas kernels  5.52 us (7%)
  waiting for transfers between devices  5.47 us (7%)
  between operations  1.44 us (2%)
  local copies, waits for them, and re-layouts  1.23 us (2%)
    all_to_all x1, blocking collectives, per_device(): gathered = lax.all_to_all(gathered, 'z', 0, 0)  24.2 us
    ppermute x1, starting transfers between devices, per_device(): given = lax.ppermute(theirs, 'c', [(0, 1), (1, 0)])  12.4 us
    all_to_all x1, blocking collectives, per_device(): lax.all_to_all(rows.reshape(LAYER, 1, 128), ('y', 'x'), 0, 0)  12.2 us
    all_gather x4, blocking collectives, in_pair(): return lax.all_gather(value, 'c', axis=0, tiled=True)  11.3 us
    pallas_call x7, Pallas kernels, on_chip(): pl.pallas_call(kernel, in_specs=[pl.BlockSpec(memory_space=space) for spa...  5.52 us
    ppermute x2, waiting for transfers between devices, across(): got_x = lax.ppermute(along_x, ('c', 'x'), route_x)  5.46 us
    ppermute x2, starting transfers between devices, across(): got_x = lax.ppermute(along_x, ('c', 'x'), route_x)  2.58 us
    ppermute x2, starting transfers between devices, across(): got_y = lax.ppermute(along_y, CHIPS, route_y)  2.58 us
  transfers between devices with their start and end apart: 5, of which 2 were waited for; matrix products, arithmetic and copies ran while one was open for 1% of the time, Pallas kernels for 1%

profile of v5, /device:TPU:1, one launch (start us, length us, event | category | flops | bytes accessed | tf_op | source)
XLA Modules:
  0.0 78.9 jit_solution(15472230840882589241)
XLA Ops:
  0.6 0.0 copy-start.2
  0.6 0.0 copy-start.1
  1.3 2.0 %shard_map.122 = (f32[2,256]{1,0:T(2,128)S(1)}, f32[1,768]{1,0:T(1,128)S(1)}, f32[2,768]{1,0:T(2,128)S(1)}, f32[9,2,128]{2,1,0:T(2,128)S(1)}, bf16[768,512]{1,0:...) custom-call(f32[2,768]{1,0:T(2,128)} %start.1, bf16[768,768]{1,0:T(8,128)(2,1)} %stiff.1, ...), custom_call_target="tpu_custom_call" | custom-call | tf_op jit(solution)/shard_map/pallas_call | solution.py:25
  3.3 0.0 copy-start.3
  3.3 0.0 copy-start
  3.3 0.0 copy-done.2
  3.3 0.0 copy-done.1
  3.3 1.6 %shard_map.123 = (f32[2,512]{1,0:T(2,128)S(1)}, f32[24,2,128]{2,1,0:T(2,128)S(1)}, f32[24,9216]{1,0:T(8,128)S(1)}, f32[24,9216]{1,0:T(8,128)}) custom-call(f32[2,768]{1,0:T(2,128)S(1)} %get-tuple-element.20.iterate, bf16[768,512]{1,0:T(8,128)(2,1)S(1)} %get-tuple-element.22.beyond, f32[1,768]{1,0:T(1,128)S(1)} %get-tuple-element.23.mask, ...), custom_call_target="tpu_custom_call" | custom-call | tf_op jit(solution)/shard_map/pallas_call | solution.py:25
  4.9 12.4 %collective-permute-start.2 = (f32[24,9216]{1,0:T(8,128)}, f32[24,9216]{1,0:T(8,128)S(1)}, u32[]{:S(2)}, u32[]{:S(2)}) collective-permute-start(f32[24,9216]{1,0:T(8,128)} %get-tuple-element.31), channel_id=1, source_target_pairs={{0,4},{4,0},{1,5},{5,1},{2,6},{6,2},{3,7},{7,3},{8,12},{12,8},{9,1... | collective-permute-start | bytes 2654216 | tf_op jit(solution)/shard_map/ppermute | solution.py:288
  17.3 2.2 %all_gather.12.both.before = f32[18,2,128]{2,1,0:T(2,128)S(1)} all-gather(f32[9,2,128]{2,1,0:T(2,128)S(1)} %get-tuple-element.26), channel_id=1, replica_groups=mesh['z'=12,'y'=8,'c'=2,'x'=4] {'c'}, dimensions={0}, use_global_device_ids=true | all-gather | bytes 27648 | tf_op jit(solution)/shard_map/all_gather | solution.py:88
  19.6 1.3 %collective-permute-start = (f32[3,2,128]{2,1,0:T(2,128)S(1)}, f32[3,2,128]{2,1,0:T(2,128)S(1)}, u32[]{:S(2)}, u32[]{:S(2)}) collective-permute-start(f32[3,2,128]{2,1,0:T(2,128)S(1)} %maximum_select_fusion), channel_id=1, source_target_pairs={{0,8},{8,16},{16,24},{24,32},{32,40},{40,48},{48,56},{56,64},{64,7... | collective-permute-start | bytes 9224 | tf_op jit(solution)/shard_map/ppermute | solution.py:82
  20.9 1.3 %collective-permute-start.1 = (f32[2,2,128]{2,1,0:T(2,128)S(1)}, f32[2,2,128]{2,1,0:T(2,128)S(1)}, u32[]{:S(2)}, u32[]{:S(2)}) collective-permute-start(f32[2,2,128]{2,1,0:T(2,128)S(1)} %maximum_select_fusion.2), channel_id=1, source_target_pairs={{0,1},{1,2},{2,3},{5,4},{6,5},{7,6},{8,9},{9,10},{10,11},{13,12},{... | collective-permute-start | bytes 6152 | tf_op jit(solution)/shard_map/ppermute | solution.py:83
  22.2 3.0 %collective-permute-done.1 = f32[2,2,128]{2,1,0:T(2,128)S(1)} collective-permute-done((f32[2,2,128]{2,1,0:T(2,128)S(1)}, f32[2,2,128]{2,1,0:T(2,128)S(1)}, u32[]{:S(2)}, u32[]{:S(2)}) %collective-permute-start.1) | collective-permute-done | bytes 2080 | tf_op jit(solution)/shard_map/ppermute | solution.py:83
  25.2 0.0 collective-permute-done
  25.3 1.8 %all_gather.13.moved = f32[58,2,128]{2,1,0:T(2,128)S(1)} all-gather(f32[29,2,128]{2,1,0:T(2,128)S(1)} %pad_maximum_fusion), channel_id=1, replica_groups=mesh['z'=12,'y'=8,'c'=2,'x'=4] {'c'}, dimensions={0}, use_global_device_ids=true | all-gather | bytes 89088 | tf_op jit(solution)/shard_map/all_gather | solution.py:88
  27.1 0.0 copy-done.3
  27.1 0.6 shard_map.124
  27.7 12.2 %all_to_all.10 = f32[32,1,128]{2,1,0:T(1,128)S(1)} all-to-all(f32[32,1,128]{2,1,0:T(1,128)S(1)} %bitcast.11), channel_id=1, replica_groups=mesh['z'=12,'y'=8,'c'=2,'x'=4] {'y','x'}, dimensions={0} | all-to-all | bytes 32768 | tf_op jit(solution)/shard_map/all_to_all | solution.py:297
  39.8 0.1 shard_map.125
  39.9 24.2 %all_to_all.11.gathered = f32[12,12,128]{2,1,0:T(8,128)S(1)} all-to-all(f32[12,12,128]{2,1,0:T(8,128)S(1)} %shard_map.125), channel_id=1, replica_groups=mesh['z'=12,'y'=8,'c'=2,'x'=4] {'z'}, dimensions={0} | all-to-all | bytes 147456 | tf_op jit(solution)/shard_map/all_to_all | solution.py:299
  64.1 0.0 collective-permute-done.2.given
  64.1 0.0 copy-done
  64.1 0.6 shard_map.126
  64.7 4.7 %all_gather.14.shared = f32[64,128]{1,0:T(8,128)S(1)} all-gather(f32[32,128]{1,0:T(8,128)S(1)} %get-tuple-element.33), channel_id=1, replica_groups=mesh['z'=12,'y'=8,'c'=2,'x'=4] {'c'}, dimensions={0}, use_global_device_ids=true | all-gather | bytes 49152 | tf_op jit(solution)/shard_map/all_gather | solution.py:88
  69.4 0.4 shard_map.127
  69.8 1.3 %collective-permute-start.3 = (f32[3,2,128]{2,1,0:T(2,128)S(1)}, f32[3,2,128]{2,1,0:T(2,128)S(1)}, u32[]{:S(2)}, u32[]{:S(2)}) collective-permute-start(f32[3,2,128]{2,1,0:T(2,128)S(1)} %maximum_select_fusion.1), channel_id=1, source_target_pairs={{0,8},{8,16},{16,24},{24,32},{32,40},{40,48},{48,56},{56,64},{64,7... | collective-permute-start | bytes 9224 | tf_op jit(solution)/shard_map/ppermute | solution.py:82
  71.1 1.3 %collective-permute-start.4 = (f32[2,2,128]{2,1,0:T(2,128)S(1)}, f32[2,2,128]{2,1,0:T(2,128)S(1)}, u32[]{:S(2)}, u32[]{:S(2)}) collective-permute-start(f32[2,2,128]{2,1,0:T(2,128)S(1)} %maximum_select_fusion.3), channel_id=1, source_target_pairs={{0,1},{1,2},{2,3},{5,4},{6,5},{7,6},{8,9},{9,10},{10,11},{13,12},{... | collective-permute-start | bytes 6152 | tf_op jit(solution)/shard_map/ppermute | solution.py:83
  72.4 0.6 copy.15
  73.0 2.4 %collective-permute-done.4 = f32[2,2,128]{2,1,0:T(2,128)S(1)} collective-permute-done((f32[2,2,128]{2,1,0:T(2,128)S(1)}, f32[2,2,128]{2,1,0:T(2,128)S(1)}, u32[]{:S(2)}, u32[]{:S(2)}) %collective-permute-start.4) | collective-permute-done | bytes 2080 | tf_op jit(solution)/shard_map/ppermute | solution.py:83
  75.5 0.0 collective-permute-done.3
  75.5 2.5 %all_gather.15.moved = f32[10,2,128]{2,1,0:T(2,128)S(1)} all-gather(f32[5,2,128]{2,1,0:T(2,128)S(1)} %pad_maximum_fusion.1), channel_id=1, replica_groups=mesh['z'=12,'y'=8,'c'=2,'x'=4] {'c'}, dimensions={0}, use_global_device_ids=true | all-gather | bytes 15360 | tf_op jit(solution)/shard_map/all_gather | solution.py:88
  78.0 0.3 shard_map.128
  78.3 0.6 copy.14
  (8 shorter events, 0.1 us)
Async XLA Ops:
  0.6 2.7 %copy-start.2 = (f32[768]{0:T(1024)S(1)}, f32[768]{0:T(1024)}, u32[]{:S(2)}) copy-start(f32[768]{0:T(1024)} %param.16) | copy-start | bytes 9220
  0.6 2.7 %copy-start.1 = (bf16[24,768]{1,0:T(8,128)(2,1)S(1)}, bf16[24,768]{1,0:T(8,128)(2,1)}, u32[]{:S(2)}) copy-start(bf16[24,768]{1,0:T(8,128)(2,1)} %basis.5) | copy-start | bytes 110596
  3.3 23.8 %copy-start.3 = (f32[2,768]{1,0:T(2,128)S(1)}, f32[2,768]{1,0:T(2,128)}, u32[]{:S(2)}) copy-start(f32[2,768]{1,0:T(2,128)} %rhs.1) | copy-start | bytes 18436
  3.3 60.8 %copy-start = (bf16[768,768]{1,0:T(8,128)(2,1)S(1)}, bf16[768,768]{1,0:T(8,128)(2,1)}, u32[]{:S(2)}) copy-start(bf16[768,768]{1,0:T(8,128)(2,1)} %held.1) | copy-start | bytes 3538948
  4.9 59.2 %collective-permute-start.2 = (f32[24,9216]{1,0:T(8,128)}, f32[24,9216]{1,0:T(8,128)S(1)}, u32[]{:S(2)}, u32[]{:S(2)}) collective-permute-start(f32[24,9216]{1,0:T(8,128)} %get-tuple-element.31), channel_id=1, source_target_pairs={{0,4},{4,0},{1,5},{5,1},{2,6},{6,2},{3,7},{7,3},{8,12},{12,8},{9,1... | collective-permute-start | bytes 2654216 | tf_op jit(solution)/shard_map/ppermute | solution.py:288
  19.6 5.6 %collective-permute-start = (f32[3,2,128]{2,1,0:T(2,128)S(1)}, f32[3,2,128]{2,1,0:T(2,128)S(1)}, u32[]{:S(2)}, u32[]{:S(2)}) collective-permute-start(f32[3,2,128]{2,1,0:T(2,128)S(1)} %maximum_select_fusion), channel_id=1, source_target_pairs={{0,8},{8,16},{16,24},{24,32},{32,40},{40,48},{48,56},{56,64},{64,7... | collective-permute-start | bytes 9224 | tf_op jit(solution)/shard_map/ppermute | solution.py:82
  20.9 4.3 %collective-permute-start.1 = (f32[2,2,128]{2,1,0:T(2,128)S(1)}, f32[2,2,128]{2,1,0:T(2,128)S(1)}, u32[]{:S(2)}, u32[]{:S(2)}) collective-permute-start(f32[2,2,128]{2,1,0:T(2,128)S(1)} %maximum_select_fusion.2), channel_id=1, source_target_pairs={{0,1},{1,2},{2,3},{5,4},{6,5},{7,6},{8,9},{9,10},{10,11},{13,12},{... | collective-permute-start | bytes 6152 | tf_op jit(solution)/shard_map/ppermute | solution.py:83
  69.8 5.6 %collective-permute-start.3 = (f32[3,2,128]{2,1,0:T(2,128)S(1)}, f32[3,2,128]{2,1,0:T(2,128)S(1)}, u32[]{:S(2)}, u32[]{:S(2)}) collective-permute-start(f32[3,2,128]{2,1,0:T(2,128)S(1)} %maximum_select_fusion.1), channel_id=1, source_target_pairs={{0,8},{8,16},{16,24},{24,32},{32,40},{40,48},{48,56},{56,64},{64,7... | collective-permute-start | bytes 9224 | tf_op jit(solution)/shard_map/ppermute | solution.py:82
  71.1 4.3 %collective-permute-start.4 = (f32[2,2,128]{2,1,0:T(2,128)S(1)}, f32[2,2,128]{2,1,0:T(2,128)S(1)}, u32[]{:S(2)}, u32[]{:S(2)}) collective-permute-start(f32[2,2,128]{2,1,0:T(2,128)S(1)} %maximum_select_fusion.3), channel_id=1, source_target_pairs={{0,1},{1,2},{2,3},{5,4},{6,5},{7,6},{8,9},{9,10},{10,11},{13,12},{... | collective-permute-start | bytes 6152 | tf_op jit(solution)/shard_map/ppermute | solution.py:83

commit v6 on v5

--- a/solution.py
+++ b/solution.py
@@ -19,7 +19,7 @@
 LEAN = pltpu.CompilerParams(vmem_limit_bytes=8 << 20)
 
 
-def on_chip(kernel, out_shape, args, far=(), scratch=(), loose=()):
+def on_chip(kernel, out_shape, args, far=(), scratch=(), loose=(), work=None):
     spaces = [pl.ANY if i in loose else pltpu.HBM if i in far else pltpu.VMEM for i in range(len(args))]
     args = [a if i in loose else pltpu.with_memory_space_constraint(a, spaces[i]) for i, a in enumerate(args)]
     return pl.pallas_call(
@@ -29,6 +29,7 @@
         out_shape=[pltpu.VMEM(shape, dtype) for shape, dtype in out_shape],
         scratch_shapes=list(scratch),
         compiler_params=LEAN,
+        cost_estimate=work,
     )(*args)
 
 
@@ -89,7 +90,7 @@
 
 
 def first_kernel(
-    start, stiff, orders, out_rows, counts, in_rows, inverse, edge, mask, iterate, own, beyond, arriving, near, columns, fields, listing, order, count, done
+    start, stiff, orders, out_rows, counts, in_rows, edge, mask, iterate, own, beyond, arriving, columns, fields, listing, order, count, done
 ):
     copies = [
         pltpu.make_async_copy(counts, count, done.at[0]),
@@ -99,7 +100,6 @@
         pltpu.make_async_copy(stiff.at[:, pl.ds(0, EDGE)], columns, done.at[4]),
         pltpu.make_async_copy(in_rows, arriving, done.at[5]),
         pltpu.make_async_copy(stiff.at[:, pl.ds(EDGE, N - EDGE)], beyond, done.at[6]),
-        pltpu.make_async_copy(inverse, near, done.at[7]),
     ]
     for copy in copies:
         copy.start()
@@ -124,15 +124,15 @@
         own[j] = picked[:, j * H : (j + 1) * H]
     copies[5].wait()
     copies[6].wait()
-    copies[7].wait()
 
 
 def weight_row(weights):
     return jnp.concatenate([weights[j : j + 1, :] for j in range(6)], axis=1)
 
 
-def rest_kernel(iterate, beyond, mask, weights, basis, inverse, rest, edges, mine, theirs):
-    first = lax.axis_index("c") == 0
+def rest_kernel(iterate, beyond, mask, weights, basis, inverse, arriving, spread, rest, edges, mine, theirs):
+    first = lax.axis_index("c") == 0
+    spread[...] = spread_of(arriving)
     rest[...] = jnp.dot(iterate[...].astype(BF16), beyond[...], preferred_element_type=F32)
     weighted = basis[...].astype(F32) * (weight_row(weights) * mask[...])
     for half in range(2):
@@ -146,8 +146,8 @@
         theirs[:, group * 384 : (group + 1) * 384] = jnp.where(first, high, low)
 
 
-def residual_kernel(edge, rest, both, moved, arriving, rhs, mask, basis, residual, rounded, rows):
-    summed = edge[...] + times_selection(arrivals(both, moved), spread_of(arriving))
+def residual_kernel(edge, rest, both, moved, spread, rhs, mask, basis, residual, rounded, rows):
+    summed = edge[...] + times_selection(arrivals(both, moved), spread[...])
     total = jnp.concatenate([summed, rest[...]], axis=1)
     value = jnp.where(mask[...] > 0.0, rhs[...] - total, 0.0)
     residual[...] = value
@@ -242,8 +242,8 @@
         both[6 + j] = jnp.where(first, theirs, mine)
 
 
-def last_kernel(iterate, correction, both, moved, arriving, solved):
-    arrived = times_selection(arrivals(both, moved), spread_of(arriving))
+def last_kernel(iterate, correction, both, moved, spread, solved):
+    arrived = times_selection(arrivals(both, moved), spread[...])
     value = iterate[...] + correction[...]
     solved[...] = value
     solved[:, :EDGE] = value[:, :EDGE] + arrived
@@ -255,7 +255,7 @@
     out_rows = out_rows.reshape(6, 1, H)
     in_rows = in_rows.reshape(6, 1, H)
     weights = weights.reshape(6, 128)
-    edge, mask, iterate, own, beyond, arriving, near = on_chip(
+    edge, mask, iterate, own, beyond, arriving = on_chip(
         first_kernel,
         [
             ((2, EDGE), F32),
@@ -264,10 +264,10 @@
             ((9, 2, H), F32),
             ((N, N - EDGE), BF16),
             ((6, 1, H), jnp.int32),
-            ((NV, C * HALF), F32),
         ],
-        [start, stiffness, orders, out_rows, out_counts, in_rows, coarse_inverse],
-        far=(0, 1, 3, 4, 5, 6),
+        [start, stiffness, orders, out_rows, out_counts, in_rows],
+        far=(0, 1, 3, 4, 5),
+        work=pl.CostEstimate(flops=2 * 10**9, transcendentals=0, bytes_accessed=1 << 21),
         loose=(2,),
         scratch=[
             pltpu.VMEM((N, EDGE), BF16),
@@ -275,15 +275,15 @@
             pltpu.VMEM((6, 1, H), jnp.int32),
             pltpu.SMEM((1,), jnp.int32),
             pltpu.SMEM((1, 6), jnp.int32),
-            pltpu.SemaphoreType.DMA((8,)),
+            pltpu.SemaphoreType.DMA((7,)),
         ],
     )
     both = in_pair(own)
     going = across(both)
-    rest, edges, mine, theirs = on_chip(
+    spread, rest, edges, mine, theirs = on_chip(
         rest_kernel,
-        [((2, N - EDGE), F32), ((NV, 2, H), F32), ((NV, HALF), F32), ((NV, HALF), F32)],
-        [iterate, beyond, mask, weights, basis, near],
+        [((6 * H, EDGE), BF16), ((2, N - EDGE), F32), ((NV, 2, H), F32), ((NV, HALF), F32), ((NV, HALF), F32)],
+        [iterate, beyond, mask, weights, basis, coarse_inverse, arriving],
     )
     given = lax.ppermute(theirs, "c", [(0, 1), (1, 0)])
     before = both
@@ -292,7 +292,7 @@
     residual, rounded, rows = on_chip(
         residual_kernel,
         [((2, N), F32), ((2, N), BF16), ((LAYER, 128), F32)],
-        [edge, rest, both, moved, arriving, rhs, mask, basis],
+        [edge, rest, both, moved, spread, rhs, mask, basis],
     )
     rows = lax.all_to_all(rows.reshape(LAYER, 1, 128), ("y", "x"), 0, 0).reshape(LAYER, 128)
     (gathered,) = on_chip(repack_kernel, [((Z, 12, 128), F32)], [rows], scratch=[pltpu.VMEM((12, 128), F32)])
@@ -308,7 +308,7 @@
         [in_pair(shared), local, basis, weights, mask, edges, before],
     )
     moved = in_pair(jnp.concatenate(across(both)))
-    (solved,) = on_chip(last_kernel, [((2, N), F32)], [iterate, correction, both, moved, arriving])
+    (solved,) = on_chip(last_kernel, [((2, N), F32)], [iterate, correction, both, moved, spread])
     return solved, residual
 
 

time: 79.3 us -> 79 us (level)
  no operation moved by 1% of the time
where the time goes in v6:
time: 79 us; the launch traced here: 78.6 us
  blocking collectives  47.7 us (60%)
  starting transfers between devices  17.5 us (22%)
  waiting for transfers between devices  5.47 us (7%)
  Pallas kernels  4.99 us (6%)
  local copies, waits for them, and re-layouts  1.48 us (2%)
  between operations  1.41 us (2%)
    all_to_all x1, blocking collectives, per_device(): gathered = lax.all_to_all(gathered, 'z', 0, 0)  24.2 us
    ppermute x1, starting transfers between devices, per_device(): given = lax.ppermute(theirs, 'c', [(0, 1), (1, 0)])  12.4 us
    all_to_all x1, blocking collectives, per_device(): lax.all_to_all(rows.reshape(LAYER, 1, 128), ('y', 'x'), 0, 0)  12.2 us
    all_gather x4, blocking collectives, in_pair(): return lax.all_gather(value, 'c', axis=0, tiled=True)  11.3 us
    ppermute x2, waiting for transfers between devices, across(): got_x = lax.ppermute(along_x, ('c', 'x'), route_x)  5.46 us
    pallas_call x7, Pallas kernels, on_chip(): pl.pallas_call(kernel, in_specs=[pl.BlockSpec(memory_space=space) for spa...  4.99 us
    ppermute x2, starting transfers between devices, across(): got_x = lax.ppermute(along_x, ('c', 'x'), route_x)  2.58 us
    ppermute x2, starting transfers between devices, across(): got_y = lax.ppermute(along_y, CHIPS, route_y)  2.58 us
  transfers between devices with their start and end apart: 5, of which 2 were waited for; matrix products, arithmetic and copies ran while one was open for 1% of the time, Pallas kernels for 1%

profile of v6, /device:TPU:1, one launch (start us, length us, event | category | flops | bytes accessed | tf_op | source)
XLA Modules:
  0.0 78.6 jit_solution(755505277107612613)
XLA Ops:
  1.3 0.0 copy-start
  1.3 0.0 copy-start.2
  1.3 0.0 copy-start.3
  1.3 1.6 %shard_map.122 = (f32[2,256]{1,0:T(2,128)S(1)}, f32[1,768]{1,0:T(1,128)S(1)}, f32[2,768]{1,0:T(2,128)S(1)}, f32[9,2,128]{2,1,0:T(2,128)S(1)}, bf16[768,512]{1,0:T(8,128)(2,1)S(1)}, /*index=5*/s32[6,1,128]{2,1,0:T(1,128)S(1)}) custom-call(f32[2,768]{1,0:T(2,128)} %start.1, bf16[768,768]{1,0:T(8,128)(2,1)} %stiff.1, s32[1]{0:T(128)S(6)} %copy.16.orders, ...), custom_call_target="tpu_custom_call" | custom-call | flops 2000000000 | bytes 2097152 | tf_op jit(solution)/shard_map/pallas_call | solution.py:25
  2.9 0.2 copy-done
  3.2 0.0 copy-done.2
  3.2 0.0 copy-done.3
  3.2 0.0 copy-start.4
  3.2 0.0 copy-start.1
  3.2 1.7 %shard_map.123 = (bf16[768,256]{1,0:T(8,128)(2,1)S(1)}, f32[2,512]{1,0:T(2,128)S(1)}, f32[24,2,128]{2,1,0:T(2,128)S(1)}, f32[24,9216]{1,0:T(8,128)S(1)}, f32[24,9216]{1,0:T(8,128)}) custom-call(f32[2,768]{1,0:T(2,128)S(1)} %get-tuple-element.20.iterate, bf16[768,512]{1,0:T(8,128)(2,1)S(1)} %get-tuple-element.22.beyond, f32[1,768]{1,0:T(1,128)S(1)} %get-tuple-element.23.mask, ...), custom_call_target="tpu_custom_call" | custom-call | tf_op jit(solution)/shard_map/pallas_call | solution.py:25
  4.9 12.4 %collective-permute-start.2 = (f32[24,9216]{1,0:T(8,128)}, f32[24,9216]{1,0:T(8,128)S(1)}, u32[]{:S(2)}, u32[]{:S(2)}) collective-permute-start(f32[24,9216]{1,0:T(8,128)} %get-tuple-element.31), channel_id=1, source_target_pairs={{0,4},{4,0},{1,5},{5,1},{2,6},{6,2},{3,7},{7,3},{8,12},{12,8},{9,1... | collective-permute-start | bytes 2654216 | tf_op jit(solution)/shard_map/ppermute | solution.py:288
  17.3 2.2 %all_gather.12.both.before = f32[18,2,128]{2,1,0:T(2,128)S(1)} all-gather(f32[9,2,128]{2,1,0:T(2,128)S(1)} %get-tuple-element.26), channel_id=1, replica_groups=mesh['z'=12,'y'=8,'c'=2,'x'=4] {'c'}, dimensions={0}, use_global_device_ids=true | all-gather | bytes 27648 | tf_op jit(solution)/shard_map/all_gather | solution.py:89
  19.6 1.3 %collective-permute-start = (f32[3,2,128]{2,1,0:T(2,128)S(1)}, f32[3,2,128]{2,1,0:T(2,128)S(1)}, u32[]{:S(2)}, u32[]{:S(2)}) collective-permute-start(f32[3,2,128]{2,1,0:T(2,128)S(1)} %maximum_select_fusion), channel_id=1, source_target_pairs={{0,8},{8,16},{16,24},{24,32},{32,40},{40,48},{48,56},{56,64},{64,7... | collective-permute-start | bytes 9224 | tf_op jit(solution)/shard_map/ppermute | solution.py:83
  20.9 1.3 %collective-permute-start.1 = (f32[2,2,128]{2,1,0:T(2,128)S(1)}, f32[2,2,128]{2,1,0:T(2,128)S(1)}, u32[]{:S(2)}, u32[]{:S(2)}) collective-permute-start(f32[2,2,128]{2,1,0:T(2,128)S(1)} %maximum_select_fusion.2), channel_id=1, source_target_pairs={{0,1},{1,2},{2,3},{5,4},{6,5},{7,6},{8,9},{9,10},{10,11},{13,12},{... | collective-permute-start | bytes 6152 | tf_op jit(solution)/shard_map/ppermute | solution.py:84
  22.2 3.0 %collective-permute-done.1 = f32[2,2,128]{2,1,0:T(2,128)S(1)} collective-permute-done((f32[2,2,128]{2,1,0:T(2,128)S(1)}, f32[2,2,128]{2,1,0:T(2,128)S(1)}, u32[]{:S(2)}, u32[]{:S(2)}) %collective-permute-start.1) | collective-permute-done | bytes 2080 | tf_op jit(solution)/shard_map/ppermute | solution.py:84
  25.2 0.0 collective-permute-done
  25.2 1.8 %all_gather.13.moved = f32[58,2,128]{2,1,0:T(2,128)S(1)} all-gather(f32[29,2,128]{2,1,0:T(2,128)S(1)} %pad_maximum_fusion), channel_id=1, replica_groups=mesh['z'=12,'y'=8,'c'=2,'x'=4] {'c'}, dimensions={0}, use_global_device_ids=true | all-gather | bytes 89088 | tf_op jit(solution)/shard_map/all_gather | solution.py:89
  27.1 0.0 copy-done.4
  27.1 0.5 shard_map.124
  27.5 12.2 %all_to_all.10 = f32[32,1,128]{2,1,0:T(1,128)S(1)} all-to-all(f32[32,1,128]{2,1,0:T(1,128)S(1)} %bitcast.11), channel_id=1, replica_groups=mesh['z'=12,'y'=8,'c'=2,'x'=4] {'y','x'}, dimensions={0} | all-to-all | bytes 32768 | tf_op jit(solution)/shard_map/all_to_all | solution.py:297
  39.7 0.1 shard_map.125
  39.8 24.2 %all_to_all.11.gathered = f32[12,12,128]{2,1,0:T(8,128)S(1)} all-to-all(f32[12,12,128]{2,1,0:T(8,128)S(1)} %shard_map.125), channel_id=1, replica_groups=mesh['z'=12,'y'=8,'c'=2,'x'=4] {'z'}, dimensions={0} | all-to-all | bytes 147456 | tf_op jit(solution)/shard_map/all_to_all | solution.py:299
  64.0 0.0 collective-permute-done.2.given
  64.0 0.0 copy-done.1
  64.0 0.5 shard_map.126
  64.5 4.7 %all_gather.14.shared = f32[64,128]{1,0:T(8,128)S(1)} all-gather(f32[32,128]{1,0:T(8,128)S(1)} %get-tuple-element.33), channel_id=1, replica_groups=mesh['z'=12,'y'=8,'c'=2,'x'=4] {'c'}, dimensions={0}, use_global_device_ids=true | all-gather | bytes 49152 | tf_op jit(solution)/shard_map/all_gather | solution.py:89
  69.2 0.4 shard_map.127
  69.6 1.3 %collective-permute-start.3 = (f32[3,2,128]{2,1,0:T(2,128)S(1)}, f32[3,2,128]{2,1,0:T(2,128)S(1)}, u32[]{:S(2)}, u32[]{:S(2)}) collective-permute-start(f32[3,2,128]{2,1,0:T(2,128)S(1)} %maximum_select_fusion.1), channel_id=1, source_target_pairs={{0,8},{8,16},{16,24},{24,32},{32,40},{40,48},{48,56},{56,64},{64,7... | collective-permute-start | bytes 9224 | tf_op jit(solution)/shard_map/ppermute | solution.py:83
  71.0 1.3 %collective-permute-start.4 = (f32[2,2,128]{2,1,0:T(2,128)S(1)}, f32[2,2,128]{2,1,0:T(2,128)S(1)}, u32[]{:S(2)}, u32[]{:S(2)}) collective-permute-start(f32[2,2,128]{2,1,0:T(2,128)S(1)} %maximum_select_fusion.3), channel_id=1, source_target_pairs={{0,1},{1,2},{2,3},{5,4},{6,5},{7,6},{8,9},{9,10},{10,11},{13,12},{... | collective-permute-start | bytes 6152 | tf_op jit(solution)/shard_map/ppermute | solution.py:84
  72.2 0.6 copy.15
  72.8 2.4 %collective-permute-done.4 = f32[2,2,128]{2,1,0:T(2,128)S(1)} collective-permute-done((f32[2,2,128]{2,1,0:T(2,128)S(1)}, f32[2,2,128]{2,1,0:T(2,128)S(1)}, u32[]{:S(2)}, u32[]{:S(2)}) %collective-permute-start.4) | collective-permute-done | bytes 2080 | tf_op jit(solution)/shard_map/ppermute | solution.py:84
  75.3 0.0 collective-permute-done.3
  75.3 2.5 %all_gather.15.moved = f32[10,2,128]{2,1,0:T(2,128)S(1)} all-gather(f32[5,2,128]{2,1,0:T(2,128)S(1)} %pad_maximum_fusion.1), channel_id=1, replica_groups=mesh['z'=12,'y'=8,'c'=2,'x'=4] {'c'}, dimensions={0}, use_global_device_ids=true | all-gather | bytes 15360 | tf_op jit(solution)/shard_map/all_gather | solution.py:89
  77.8 0.1 shard_map.128
  78.0 0.6 copy.14
  (8 shorter events, 0.1 us)
Async XLA Ops:
  1.3 1.9 %copy-start = (f32[24,18432]{1,0:T(8,128)S(1)}, f32[24,18432]{1,0:T(8,128)}, u32[]{:S(2)}) copy-start(f32[24,18432]{1,0:T(8,128)} %inverse.1) | copy-start | bytes 5308420
  1.3 1.9 %copy-start.2 = (bf16[24,768]{1,0:T(8,128)(2,1)S(1)}, bf16[24,768]{1,0:T(8,128)(2,1)}, u32[]{:S(2)}) copy-start(bf16[24,768]{1,0:T(8,128)(2,1)} %basis.5) | copy-start | bytes 110596
  1.3 1.9 %copy-start.3 = (f32[768]{0:T(1024)S(1)}, f32[768]{0:T(1024)}, u32[]{:S(2)}) copy-start(f32[768]{0:T(1024)} %param.16) | copy-start | bytes 9220
  3.2 23.9 %copy-start.4 = (f32[2,768]{1,0:T(2,128)S(1)}, f32[2,768]{1,0:T(2,128)}, u32[]{:S(2)}) copy-start(f32[2,768]{1,0:T(2,128)} %rhs.1) | copy-start | bytes 18436
  3.2 60.8 %copy-start.1 = (bf16[768,768]{1,0:T(8,128)(2,1)S(1)}, bf16[768,768]{1,0:T(8,128)(2,1)}, u32[]{:S(2)}) copy-start(bf16[768,768]{1,0:T(8,128)(2,1)} %held.1) | copy-start | bytes 3538948
  4.9 59.1 %collective-permute-start.2 = (f32[24,9216]{1,0:T(8,128)}, f32[24,9216]{1,0:T(8,128)S(1)}, u32[]{:S(2)}, u32[]{:S(2)}) collective-permute-start(f32[24,9216]{1,0:T(8,128)} %get-tuple-element.31), channel_id=1, source_target_pairs={{0,4},{4,0},{1,5},{5,1},{2,6},{6,2},{3,7},{7,3},{8,12},{12,8},{9,1... | collective-permute-start | bytes 2654216 | tf_op jit(solution)/shard_map/ppermute | solution.py:288
  19.6 5.6 %collective-permute-start = (f32[3,2,128]{2,1,0:T(2,128)S(1)}, f32[3,2,128]{2,1,0:T(2,128)S(1)}, u32[]{:S(2)}, u32[]{:S(2)}) collective-permute-start(f32[3,2,128]{2,1,0:T(2,128)S(1)} %maximum_select_fusion), channel_id=1, source_target_pairs={{0,8},{8,16},{16,24},{24,32},{32,40},{40,48},{48,56},{56,64},{64,7... | collective-permute-start | bytes 9224 | tf_op jit(solution)/shard_map/ppermute | solution.py:83
  20.9 4.3 %collective-permute-start.1 = (f32[2,2,128]{2,1,0:T(2,128)S(1)}, f32[2,2,128]{2,1,0:T(2,128)S(1)}, u32[]{:S(2)}, u32[]{:S(2)}) collective-permute-start(f32[2,2,128]{2,1,0:T(2,128)S(1)} %maximum_select_fusion.2), channel_id=1, source_target_pairs={{0,1},{1,2},{2,3},{5,4},{6,5},{7,6},{8,9},{9,10},{10,11},{13,12},{... | collective-permute-start | bytes 6152 | tf_op jit(solution)/shard_map/ppermute | solution.py:84
  69.6 5.6 %collective-permute-start.3 = (f32[3,2,128]{2,1,0:T(2,128)S(1)}, f32[3,2,128]{2,1,0:T(2,128)S(1)}, u32[]{:S(2)}, u32[]{:S(2)}) collective-permute-start(f32[3,2,128]{2,1,0:T(2,128)S(1)} %maximum_select_fusion.1), channel_id=1, source_target_pairs={{0,8},{8,16},{16,24},{24,32},{32,40},{40,48},{48,56},{56,64},{64,7... | collective-permute-start | bytes 9224 | tf_op jit(solution)/shard_map/ppermute | solution.py:83
  71.0 4.3 %collective-permute-start.4 = (f32[2,2,128]{2,1,0:T(2,128)S(1)}, f32[2,2,128]{2,1,0:T(2,128)S(1)}, u32[]{:S(2)}, u32[]{:S(2)}) collective-permute-start(f32[2,2,128]{2,1,0:T(2,128)S(1)} %maximum_select_fusion.3), channel_id=1, source_target_pairs={{0,1},{1,2},{2,3},{5,4},{6,5},{7,6},{8,9},{9,10},{10,11},{13,12},{... | collective-permute-start | bytes 6152 | tf_op jit(solution)/shard_map/ppermute | solution.py:84

commit v7 on v6

--- a/solution.py
+++ b/solution.py
@@ -130,14 +130,12 @@
     return jnp.concatenate([weights[j : j + 1, :] for j in range(6)], axis=1)
 
 
-def rest_kernel(iterate, beyond, mask, weights, basis, inverse, arriving, spread, rest, edges, mine, theirs):
+def rest_kernel(iterate, beyond, mask, weights, basis, inverse, arriving, spread, rest, mine, theirs):
     first = lax.axis_index("c") == 0
     spread[...] = spread_of(arriving)
     rest[...] = jnp.dot(iterate[...].astype(BF16), beyond[...], preferred_element_type=F32)
     weighted = basis[...].astype(F32) * (weight_row(weights) * mask[...])
-    for half in range(2):
-        for row in range(0, NV, 2):
-            edges[half * 12 + row // 2] = weighted[row : row + 2, half * H : (half + 1) * H]
+    theirs[:, HALF:] = weighted[:, :EDGE]
     for group in range(HALF // 384):
         block = inverse[:, group * 768 : (group + 1) * 768]
         low = jnp.concatenate([block[:, k * 192 : k * 192 + 96] for k in range(4)], axis=1)
@@ -208,7 +206,7 @@
     shared[NV + 4 :] = jnp.zeros((4, 128), F32)
 
 
-def coarse_kernel(shared, local, basis, weights, mask, moved, before, correction, both):
+def coarse_kernel(shared, local, basis, weights, mask, given, before, correction, both):
     first = lax.axis_index("c") == 0
     total = shared[:NV] + shared[32 : 32 + NV]
     total = total.astype(BF16).astype(F32)
@@ -220,13 +218,11 @@
         coarse = jnp.where(first, pair[0], pair[1])
         fixes.append(jnp.sum(vectors * coarse, axis=0, keepdims=True))
         coarse = jnp.where(first, pair[1], pair[0])
-        halves = []
-        for half in range(2):
-            terms = jnp.zeros((2, H), F32)
-            for row in range(0, NV, 2):
-                at = 5 + half * 12 + row // 2
-                terms += jnp.where(first, moved[5 + NV + at], moved[at]) * coarse[row : row + 2]
-            halves.append(partner_local[2 * load + half : 2 * load + half + 1, :] + jnp.sum(terms, axis=0, keepdims=True))
+        term = jnp.sum(given[:, HALF:] * coarse, axis=0, keepdims=True)
+        halves = [
+            partner_local[2 * load + half : 2 * load + half + 1, :] + term[:, half * H : (half + 1) * H]
+            for half in range(2)
+        ]
         partner.append(jnp.concatenate(halves, axis=1))
     value = local[...] + weight_row(weights) * mask[...] * jnp.concatenate(fixes, axis=0)
     correction[...] = value
@@ -280,15 +276,14 @@
     )
     both = in_pair(own)
     going = across(both)
-    spread, rest, edges, mine, theirs = on_chip(
+    spread, rest, mine, theirs = on_chip(
         rest_kernel,
-        [((6 * H, EDGE), BF16), ((2, N - EDGE), F32), ((NV, 2, H), F32), ((NV, HALF), F32), ((NV, HALF), F32)],
+        [((6 * H, EDGE), BF16), ((2, N - EDGE), F32), ((NV, HALF), F32), ((NV, HALF + EDGE), F32)],
         [iterate, beyond, mask, weights, basis, coarse_inverse, arriving],
     )
     given = lax.ppermute(theirs, "c", [(0, 1), (1, 0)])
     before = both
-    moved = in_pair(jnp.concatenate(going + [edges]))
-    edges = moved
+    moved = in_pair(jnp.concatenate(going))
     residual, rounded, rows = on_chip(
         residual_kernel,
         [((2, N), F32), ((2, N), BF16), ((LAYER, 128), F32)],
@@ -305,7 +300,7 @@
     correction, both = on_chip(
         coarse_kernel,
         [((2, N), F32), ((12, 2, H), F32)],
-        [in_pair(shared), local, basis, weights, mask, edges, before],
+        [in_pair(shared), local, basis, weights, mask, given, before],
     )
     moved = in_pair(jnp.concatenate(across(both)))
     (solved,) = on_chip(last_kernel, [((2, N), F32)], [iterate, correction, both, moved, spread])

time: 79 us -> 79 us (level)
  no operation moved by 1% of the time
where the time goes in v7:
time: 79 us; the launch traced here: 78.6 us
  blocking collectives  47.7 us (60%)
  starting transfers between devices  17.5 us (22%)
  waiting for transfers between devices  5.47 us (7%)
  Pallas kernels  5.01 us (6%)
  local copies, waits for them, and re-layouts  1.48 us (2%)
  between operations  1.41 us (2%)
    all_to_all x1, blocking collectives, per_device(): gathered = lax.all_to_all(gathered, 'z', 0, 0)  24.2 us
    ppermute x1, starting transfers between devices, per_device(): given = lax.ppermute(theirs, 'c', [(0, 1), (1, 0)])  12.4 us
    all_to_all x1, blocking collectives, per_device(): lax.all_to_all(rows.reshape(LAYER, 1, 128), ('y', 'x'), 0, 0)  12.2 us
    all_gather x4, blocking collectives, in_pair(): return lax.all_gather(value, 'c', axis=0, tiled=True)  11.3 us
    ppermute x2, waiting for transfers between devices, across(): got_x = lax.ppermute(along_x, ('c', 'x'), route_x)  5.46 us
    pallas_call x7, Pallas kernels, on_chip(): pl.pallas_call(kernel, in_specs=[pl.BlockSpec(memory_space=space) for spa...  5.01 us
    ppermute x2, starting transfers between devices, across(): got_x = lax.ppermute(along_x, ('c', 'x'), route_x)  2.58 us
    ppermute x2, starting transfers between devices, across(): got_y = lax.ppermute(along_y, CHIPS, route_y)  2.58 us
  transfers between devices with their start and end apart: 5, of which 2 were waited for; matrix products, arithmetic and copies ran while one was open for 1% of the time, Pallas kernels for 1%

profile of v7, /device:TPU:1, one launch (start us, length us, event | category | flops | bytes accessed | tf_op | source)
XLA Modules:
  0.0 78.6 jit_solution(13571788818455431616)
XLA Ops:
  1.3 0.0 copy-start
  1.3 0.0 copy-start.2
  1.3 0.0 copy-start.3
  1.3 1.6 %shard_map.122 = (f32[2,256]{1,0:T(2,128)S(1)}, f32[1,768]{1,0:T(1,128)S(1)}, f32[2,768]{1,0:T(2,128)S(1)}, f32[9,2,128]{2,1,0:T(2,128)S(1)}, bf16[768,512]{1,0:T(8,128)(2,1)S(1)}, /*index=5*/s32[6,1,128]{2,1,0:T(1,128)S(1)}) custom-call(f32[2,768]{1,0:T(2,128)} %start.1, bf16[768,768]{1,0:T(8,128)(2,1)} %stiff.1, s32[1]{0:T(128)S(6)} %copy.16.orders, ...), custom_call_target="tpu_custom_call" | custom-call | flops 2000000000 | bytes 2097152 | tf_op jit(solution)/shard_map/pallas_call | solution.py:25
  2.9 0.2 copy-done
  3.2 0.0 copy-done.2
  3.2 0.0 copy-done.3
  3.2 0.0 copy-start.4
  3.2 0.0 copy-start.1
  3.2 1.7 %shard_map.123 = (bf16[768,256]{1,0:T(8,128)(2,1)S(1)}, f32[2,512]{1,0:T(2,128)S(1)}, f32[24,9216]{1,0:T(8,128)S(1)}, f32[24,9472]{1,0:T(8,128)}) custom-call(f32[2,768]{1,0:T(2,128)S(1)} %get-tuple-element.19.iterate, bf16[768,512]{1,0:T(8,128)(2,1)S(1)} %get-tuple-element.21.beyond, f32[1,768]{1,0:T(1,128)S(1)} %get-tuple-element.22.mask, ...), custom_call_target="tpu_custom_call" | custom-call | tf_op jit(solution)/shard_map/pallas_call | solution.py:25
  4.9 12.4 %collective-permute-start.2 = (f32[24,9472]{1,0:T(8,128)}, f32[24,9472]{1,0:T(8,128)S(1)}, u32[]{:S(2)}, u32[]{:S(2)}) collective-permute-start(f32[24,9472]{1,0:T(8,128)} %get-tuple-element.29), channel_id=1, source_target_pairs={{0,4},{4,0},{1,5},{5,1},{2,6},{6,2},{3,7},{7,3},{8,12},{12,8},{9,1... | collective-permute-start | bytes 2727944 | tf_op jit(solution)/shard_map/ppermute | solution.py:284
  17.3 2.3 %all_gather.12.both.before = f32[18,2,128]{2,1,0:T(2,128)S(1)} all-gather(f32[9,2,128]{2,1,0:T(2,128)S(1)} %get-tuple-element.25), channel_id=1, replica_groups=mesh['z'=12,'y'=8,'c'=2,'x'=4] {'c'}, dimensions={0}, use_global_device_ids=true | all-gather | bytes 27648 | tf_op jit(solution)/shard_map/all_gather | solution.py:89
  19.6 1.3 %collective-permute-start = (f32[3,2,128]{2,1,0:T(2,128)S(1)}, f32[3,2,128]{2,1,0:T(2,128)S(1)}, u32[]{:S(2)}, u32[]{:S(2)}) collective-permute-start(f32[3,2,128]{2,1,0:T(2,128)S(1)} %maximum_select_fusion), channel_id=1, source_target_pairs={{0,8},{8,16},{16,24},{24,32},{32,40},{40,48},{48,56},{56,64},{64,7... | collective-permute-start | bytes 9224 | tf_op jit(solution)/shard_map/ppermute | solution.py:83
  20.9 1.3 %collective-permute-start.1 = (f32[2,2,128]{2,1,0:T(2,128)S(1)}, f32[2,2,128]{2,1,0:T(2,128)S(1)}, u32[]{:S(2)}, u32[]{:S(2)}) collective-permute-start(f32[2,2,128]{2,1,0:T(2,128)S(1)} %maximum_select_fusion.2), channel_id=1, source_target_pairs={{0,1},{1,2},{2,3},{5,4},{6,5},{7,6},{8,9},{9,10},{10,11},{13,12},{... | collective-permute-start | bytes 6152 | tf_op jit(solution)/shard_map/ppermute | solution.py:84
  22.2 3.0 %collective-permute-done.1 = f32[2,2,128]{2,1,0:T(2,128)S(1)} collective-permute-done((f32[2,2,128]{2,1,0:T(2,128)S(1)}, f32[2,2,128]{2,1,0:T(2,128)S(1)}, u32[]{:S(2)}, u32[]{:S(2)}) %collective-permute-start.1) | collective-permute-done | bytes 2080 | tf_op jit(solution)/shard_map/ppermute | solution.py:84
  25.2 0.0 collective-permute-done
  25.3 1.8 %all_gather.13.moved = f32[10,2,128]{2,1,0:T(2,128)S(1)} all-gather(f32[5,2,128]{2,1,0:T(2,128)S(1)} %pad_maximum_fusion), channel_id=1, replica_groups=mesh['z'=12,'y'=8,'c'=2,'x'=4] {'c'}, dimensions={0}, use_global_device_ids=true | all-gather | bytes 15360 | tf_op jit(solution)/shard_map/all_gather | solution.py:89
  27.1 0.0 copy-done.4
  27.1 0.5 shard_map.124
  27.5 12.2 %all_to_all.10 = f32[32,1,128]{2,1,0:T(1,128)S(1)} all-to-all(f32[32,1,128]{2,1,0:T(1,128)S(1)} %bitcast.11), channel_id=1, replica_groups=mesh['z'=12,'y'=8,'c'=2,'x'=4] {'y','x'}, dimensions={0} | all-to-all | bytes 32768 | tf_op jit(solution)/shard_map/all_to_all | solution.py:292
  39.7 0.1 shard_map.125
  39.8 24.2 %all_to_all.11.gathered = f32[12,12,128]{2,1,0:T(8,128)S(1)} all-to-all(f32[12,12,128]{2,1,0:T(8,128)S(1)} %shard_map.125), channel_id=1, replica_groups=mesh['z'=12,'y'=8,'c'=2,'x'=4] {'z'}, dimensions={0} | all-to-all | bytes 147456 | tf_op jit(solution)/shard_map/all_to_all | solution.py:294
  64.0 0.0 collective-permute-done.2.given
  64.0 0.0 copy-done.1
  64.0 0.5 shard_map.126
  64.6 4.7 %all_gather.14.shared = f32[64,128]{1,0:T(8,128)S(1)} all-gather(f32[32,128]{1,0:T(8,128)S(1)} %get-tuple-element.31), channel_id=1, replica_groups=mesh['z'=12,'y'=8,'c'=2,'x'=4] {'c'}, dimensions={0}, use_global_device_ids=true | all-gather | bytes 49152 | tf_op jit(solution)/shard_map/all_gather | solution.py:89
  69.2 0.4 shard_map.127
  69.6 1.3 %collective-permute-start.3 = (f32[3,2,128]{2,1,0:T(2,128)S(1)}, f32[3,2,128]{2,1,0:T(2,128)S(1)}, u32[]{:S(2)}, u32[]{:S(2)}) collective-permute-start(f32[3,2,128]{2,1,0:T(2,128)S(1)} %maximum_select_fusion.1), channel_id=1, source_target_pairs={{0,8},{8,16},{16,24},{24,32},{32,40},{40,48},{48,56},{56,64},{64,7... | collective-permute-start | bytes 9224 | tf_op jit(solution)/shard_map/ppermute | solution.py:83
  71.0 1.3 %collective-permute-start.4 = (f32[2,2,128]{2,1,0:T(2,128)S(1)}, f32[2,2,128]{2,1,0:T(2,128)S(1)}, u32[]{:S(2)}, u32[]{:S(2)}) collective-permute-start(f32[2,2,128]{2,1,0:T(2,128)S(1)} %maximum_select_fusion.3), channel_id=1, source_target_pairs={{0,1},{1,2},{2,3},{5,4},{6,5},{7,6},{8,9},{9,10},{10,11},{13,12},{... | collective-permute-start | bytes 6152 | tf_op jit(solution)/shard_map/ppermute | solution.py:84
  72.3 0.6 copy.15
  72.9 2.4 %collective-permute-done.4 = f32[2,2,128]{2,1,0:T(2,128)S(1)} collective-permute-done((f32[2,2,128]{2,1,0:T(2,128)S(1)}, f32[2,2,128]{2,1,0:T(2,128)S(1)}, u32[]{:S(2)}, u32[]{:S(2)}) %collective-permute-start.4) | collective-permute-done | bytes 2080 | tf_op jit(solution)/shard_map/ppermute | solution.py:84
  75.3 0.0 collective-permute-done.3
  75.3 2.5 %all_gather.15.moved = f32[10,2,128]{2,1,0:T(2,128)S(1)} all-gather(f32[5,2,128]{2,1,0:T(2,128)S(1)} %pad_maximum_fusion.1), channel_id=1, replica_groups=mesh['z'=12,'y'=8,'c'=2,'x'=4] {'c'}, dimensions={0}, use_global_device_ids=true | all-gather | bytes 15360 | tf_op jit(solution)/shard_map/all_gather | solution.py:89
  77.8 0.1 shard_map.128
  78.0 0.6 copy.14
  (8 shorter events, 0.1 us)
Async XLA Ops:
  1.3 1.9 %copy-start = (f32[24,18432]{1,0:T(8,128)S(1)}, f32[24,18432]{1,0:T(8,128)}, u32[]{:S(2)}) copy-start(f32[24,18432]{1,0:T(8,128)} %inverse.1) | copy-start | bytes 5308420
  1.3 1.9 %copy-start.2 = (bf16[24,768]{1,0:T(8,128)(2,1)S(1)}, bf16[24,768]{1,0:T(8,128)(2,1)}, u32[]{:S(2)}) copy-start(bf16[24,768]{1,0:T(8,128)(2,1)} %basis.5) | copy-start | bytes 110596
  1.3 1.9 %copy-start.3 = (f32[768]{0:T(1024)S(1)}, f32[768]{0:T(1024)}, u32[]{:S(2)}) copy-start(f32[768]{0:T(1024)} %param.16) | copy-start | bytes 9220
  3.2 23.9 %copy-start.4 = (f32[2,768]{1,0:T(2,128)S(1)}, f32[2,768]{1,0:T(2,128)}, u32[]{:S(2)}) copy-start(f32[2,768]{1,0:T(2,128)} %rhs.1) | copy-start | bytes 18436
  3.2 60.8 %copy-start.1 = (bf16[768,768]{1,0:T(8,128)(2,1)S(1)}, bf16[768,768]{1,0:T(8,128)(2,1)}, u32[]{:S(2)}) copy-start(bf16[768,768]{1,0:T(8,128)(2,1)} %held.1) | copy-start | bytes 3538948
  4.9 59.1 %collective-permute-start.2 = (f32[24,9472]{1,0:T(8,128)}, f32[24,9472]{1,0:T(8,128)S(1)}, u32[]{:S(2)}, u32[]{:S(2)}) collective-permute-start(f32[24,9472]{1,0:T(8,128)} %get-tuple-element.29), channel_id=1, source_target_pairs={{0,4},{4,0},{1,5},{5,1},{2,6},{6,2},{3,7},{7,3},{8,12},{12,8},{9,1... | collective-permute-start | bytes 2727944 | tf_op jit(solution)/shard_map/ppermute | solution.py:284
  19.6 5.6 %collective-permute-start = (f32[3,2,128]{2,1,0:T(2,128)S(1)}, f32[3,2,128]{2,1,0:T(2,128)S(1)}, u32[]{:S(2)}, u32[]{:S(2)}) collective-permute-start(f32[3,2,128]{2,1,0:T(2,128)S(1)} %maximum_select_fusion), channel_id=1, source_target_pairs={{0,8},{8,16},{16,24},{24,32},{32,40},{40,48},{48,56},{56,64},{64,7... | collective-permute-start | bytes 9224 | tf_op jit(solution)/shard_map/ppermute | solution.py:83
  20.9 4.3 %collective-permute-start.1 = (f32[2,2,128]{2,1,0:T(2,128)S(1)}, f32[2,2,128]{2,1,0:T(2,128)S(1)}, u32[]{:S(2)}, u32[]{:S(2)}) collective-permute-start(f32[2,2,128]{2,1,0:T(2,128)S(1)} %maximum_select_fusion.2), channel_id=1, source_target_pairs={{0,1},{1,2},{2,3},{5,4},{6,5},{7,6},{8,9},{9,10},{10,11},{13,12},{... | collective-permute-start | bytes 6152 | tf_op jit(solution)/shard_map/ppermute | solution.py:84
  69.6 5.6 %collective-permute-start.3 = (f32[3,2,128]{2,1,0:T(2,128)S(1)}, f32[3,2,128]{2,1,0:T(2,128)S(1)}, u32[]{:S(2)}, u32[]{:S(2)}) collective-permute-start(f32[3,2,128]{2,1,0:T(2,128)S(1)} %maximum_select_fusion.1), channel_id=1, source_target_pairs={{0,8},{8,16},{16,24},{24,32},{32,40},{40,48},{48,56},{56,64},{64,7... | collective-permute-start | bytes 9224 | tf_op jit(solution)/shard_map/ppermute | solution.py:83
  71.0 4.3 %collective-permute-start.4 = (f32[2,2,128]{2,1,0:T(2,128)S(1)}, f32[2,2,128]{2,1,0:T(2,128)S(1)}, u32[]{:S(2)}, u32[]{:S(2)}) collective-permute-start(f32[2,2,128]{2,1,0:T(2,128)S(1)} %maximum_select_fusion.3), channel_id=1, source_target_pairs={{0,1},{1,2},{2,3},{5,4},{6,5},{7,6},{8,9},{9,10},{10,11},{13,12},{... | collective-permute-start | bytes 6152 | tf_op jit(solution)/shard_map/ppermute | solution.py:84

commit v8 on v7

--- a/solution.py
+++ b/solution.py
@@ -19,14 +19,14 @@
 LEAN = pltpu.CompilerParams(vmem_limit_bytes=8 << 20)
 
 
-def on_chip(kernel, out_shape, args, far=(), scratch=(), loose=(), work=None):
+def on_chip(kernel, out_shape, args, far=(), scratch=(), loose=(), work=None, place=pltpu.VMEM):
     spaces = [pl.ANY if i in loose else pltpu.HBM if i in far else pltpu.VMEM for i in range(len(args))]
     args = [a if i in loose else pltpu.with_memory_space_constraint(a, spaces[i]) for i, a in enumerate(args)]
     return pl.pallas_call(
         kernel,
         in_specs=[pl.BlockSpec(memory_space=space) for space in spaces],
-        out_specs=[pl.BlockSpec(memory_space=pltpu.VMEM)] * len(out_shape),
-        out_shape=[pltpu.VMEM(shape, dtype) for shape, dtype in out_shape],
+        out_specs=[pl.BlockSpec(memory_space=place)] * len(out_shape),
+        out_shape=[place(shape, dtype) for shape, dtype in out_shape],
         scratch_shapes=list(scratch),
         compiler_params=LEAN,
         cost_estimate=work,
@@ -238,11 +238,16 @@
         both[6 + j] = jnp.where(first, theirs, mine)
 
 
-def last_kernel(iterate, correction, both, moved, spread, solved):
+def last_kernel(iterate, correction, both, moved, spread, solved, value, done):
+    value[:, EDGE:] = iterate[:, EDGE:] + correction[:, EDGE:]
+    far = pltpu.make_async_copy(value.at[:, pl.ds(EDGE, N - EDGE)], solved.at[:, pl.ds(EDGE, N - EDGE)], done.at[0])
+    far.start()
     arrived = times_selection(arrivals(both, moved), spread[...])
-    value = iterate[...] + correction[...]
-    solved[...] = value
-    solved[:, :EDGE] = value[:, :EDGE] + arrived
+    value[:, :EDGE] = iterate[:, :EDGE] + correction[:, :EDGE] + arrived
+    near = pltpu.make_async_copy(value.at[:, pl.ds(0, EDGE)], solved.at[:, pl.ds(0, EDGE)], done.at[1])
+    near.start()
+    far.wait()
+    near.wait()
 
 
 def per_device(
@@ -303,7 +308,7 @@
         [in_pair(shared), local, basis, weights, mask, given, before],
     )
     moved = in_pair(jnp.concatenate(across(both)))
-    (solved,) = on_chip(last_kernel, [((2, N), F32)], [iterate, correction, both, moved, spread])
+    (solved,) = on_chip(last_kernel, [((2, N), F32)], [iterate, correction, both, moved, spread], place=pltpu.HBM, scratch=[pltpu.VMEM((2, N), F32), pltpu.SemaphoreType.DMA((2,))])
     return solved, residual
 
 

time: 79 us -> 79 us (level)
  no operation moved by 1% of the time
where the time goes in v8:
time: 79 us; the launch traced here: 78.6 us
  blocking collectives  47.7 us (60%)
  starting transfers between devices  17.5 us (22%)
  Pallas kernels  5.65 us (7%)
  waiting for transfers between devices  5.47 us (7%)
  between operations  1.41 us (2%)
  local copies, waits for them, and re-layouts  0.84 us (1%)
    all_to_all x1, blocking collectives, per_device(): gathered = lax.all_to_all(gathered, 'z', 0, 0)  24.2 us
    ppermute x1, starting transfers between devices, per_device(): given = lax.ppermute(theirs, 'c', [(0, 1), (1, 0)])  12.4 us
    all_to_all x1, blocking collectives, per_device(): lax.all_to_all(rows.reshape(LAYER, 1, 128), ('y', 'x'), 0, 0)  12.2 us
    all_gather x4, blocking collectives, in_pair(): return lax.all_gather(value, 'c', axis=0, tiled=True)  11.3 us
    pallas_call x7, Pallas kernels, on_chip(): pl.pallas_call(kernel, in_specs=[pl.BlockSpec(memory_space=space) for spa...  5.65 us
    ppermute x2, waiting for transfers between devices, across(): got_x = lax.ppermute(along_x, ('c', 'x'), route_x)  5.46 us
    ppermute x2, starting transfers between devices, across(): got_x = lax.ppermute(along_x, ('c', 'x'), route_x)  2.58 us
    ppermute x2, starting transfers between devices, across(): got_y = lax.ppermute(along_y, CHIPS, route_y)  2.58 us
  transfers between devices with their start and end apart: 5, of which 2 were waited for; matrix products, arithmetic and copies ran while one was open for 1% of the time, Pallas kernels for 1%

profile of v8, /device:TPU:1, one launch (start us, length us, event | category | flops | bytes accessed | tf_op | source)
XLA Modules:
  0.0 78.6 jit_solution(2853407118136230014)
XLA Ops:
  1.3 0.0 copy-start
  1.3 0.0 copy-start.2
  1.3 0.0 copy-start.3
  1.3 1.6 %shard_map.122 = (f32[2,256]{1,0:T(2,128)S(1)}, f32[1,768]{1,0:T(1,128)S(1)}, f32[2,768]{1,0:T(2,128)S(1)}, f32[9,2,128]{2,1,0:T(2,128)S(1)}, bf16[768,512]{1,0:T(8,128)(2,1)S(1)}, /*index=5*/s32[6,1,128]{2,1,0:T(1,128)S(1)}) custom-call(f32[2,768]{1,0:T(2,128)} %start.1, bf16[768,768]{1,0:T(8,128)(2,1)} %stiff.1, s32[1]{0:T(128)S(6)} %copy.15.orders, ...), custom_call_target="tpu_custom_call" | custom-call | flops 2000000000 | bytes 2097152 | tf_op jit(solution)/shard_map/pallas_call | solution.py:25
  2.9 0.2 copy-done
  3.2 0.0 copy-done.2
  3.2 0.0 copy-done.3
  3.2 0.0 copy-start.4
  3.2 0.0 copy-start.1
  3.2 1.7 %shard_map.123 = (bf16[768,256]{1,0:T(8,128)(2,1)S(1)}, f32[2,512]{1,0:T(2,128)S(1)}, f32[24,9216]{1,0:T(8,128)S(1)}, f32[24,9472]{1,0:T(8,128)}) custom-call(f32[2,768]{1,0:T(2,128)S(1)} %get-tuple-element.19.iterate, bf16[768,512]{1,0:T(8,128)(2,1)S(1)} %get-tuple-element.21.beyond, f32[1,768]{1,0:T(1,128)S(1)} %get-tuple-element.22.mask, ...), custom_call_target="tpu_custom_call" | custom-call | tf_op jit(solution)/shard_map/pallas_call | solution.py:25
  4.9 12.4 %collective-permute-start.2 = (f32[24,9472]{1,0:T(8,128)}, f32[24,9472]{1,0:T(8,128)S(1)}, u32[]{:S(2)}, u32[]{:S(2)}) collective-permute-start(f32[24,9472]{1,0:T(8,128)} %get-tuple-element.29), channel_id=1, source_target_pairs={{0,4},{4,0},{1,5},{5,1},{2,6},{6,2},{3,7},{7,3},{8,12},{12,8},{9,1... | collective-permute-start | bytes 2727944 | tf_op jit(solution)/shard_map/ppermute | solution.py:289
  17.3 2.3 %all_gather.12.both.before = f32[18,2,128]{2,1,0:T(2,128)S(1)} all-gather(f32[9,2,128]{2,1,0:T(2,128)S(1)} %get-tuple-element.25), channel_id=1, replica_groups=mesh['z'=12,'y'=8,'c'=2,'x'=4] {'c'}, dimensions={0}, use_global_device_ids=true | all-gather | bytes 27648 | tf_op jit(solution)/shard_map/all_gather | solution.py:89
  19.6 1.3 %collective-permute-start = (f32[3,2,128]{2,1,0:T(2,128)S(1)}, f32[3,2,128]{2,1,0:T(2,128)S(1)}, u32[]{:S(2)}, u32[]{:S(2)}) collective-permute-start(f32[3,2,128]{2,1,0:T(2,128)S(1)} %maximum_select_fusion), channel_id=1, source_target_pairs={{0,8},{8,16},{16,24},{24,32},{32,40},{40,48},{48,56},{56,64},{64,7... | collective-permute-start | bytes 9224 | tf_op jit(solution)/shard_map/ppermute | solution.py:83
  20.9 1.3 %collective-permute-start.1 = (f32[2,2,128]{2,1,0:T(2,128)S(1)}, f32[2,2,128]{2,1,0:T(2,128)S(1)}, u32[]{:S(2)}, u32[]{:S(2)}) collective-permute-start(f32[2,2,128]{2,1,0:T(2,128)S(1)} %maximum_select_fusion.2), channel_id=1, source_target_pairs={{0,1},{1,2},{2,3},{5,4},{6,5},{7,6},{8,9},{9,10},{10,11},{13,12},{... | collective-permute-start | bytes 6152 | tf_op jit(solution)/shard_map/ppermute | solution.py:84
  22.2 3.0 %collective-permute-done.1 = f32[2,2,128]{2,1,0:T(2,128)S(1)} collective-permute-done((f32[2,2,128]{2,1,0:T(2,128)S(1)}, f32[2,2,128]{2,1,0:T(2,128)S(1)}, u32[]{:S(2)}, u32[]{:S(2)}) %collective-permute-start.1) | collective-permute-done | bytes 2080 | tf_op jit(solution)/shard_map/ppermute | solution.py:84
  25.2 0.0 collective-permute-done
  25.3 1.8 %all_gather.13.moved = f32[10,2,128]{2,1,0:T(2,128)S(1)} all-gather(f32[5,2,128]{2,1,0:T(2,128)S(1)} %pad_maximum_fusion), channel_id=1, replica_groups=mesh['z'=12,'y'=8,'c'=2,'x'=4] {'c'}, dimensions={0}, use_global_device_ids=true | all-gather | bytes 15360 | tf_op jit(solution)/shard_map/all_gather | solution.py:89
  27.1 0.0 copy-done.4
  27.1 0.5 shard_map.124
  27.5 12.2 %all_to_all.10 = f32[32,1,128]{2,1,0:T(1,128)S(1)} all-to-all(f32[32,1,128]{2,1,0:T(1,128)S(1)} %bitcast.11), channel_id=1, replica_groups=mesh['z'=12,'y'=8,'c'=2,'x'=4] {'y','x'}, dimensions={0} | all-to-all | bytes 32768 | tf_op jit(solution)/shard_map/all_to_all | solution.py:297
  39.7 0.1 shard_map.125
  39.8 24.2 %all_to_all.11.gathered = f32[12,12,128]{2,1,0:T(8,128)S(1)} all-to-all(f32[12,12,128]{2,1,0:T(8,128)S(1)} %shard_map.125), channel_id=1, replica_groups=mesh['z'=12,'y'=8,'c'=2,'x'=4] {'z'}, dimensions={0} | all-to-all | bytes 147456 | tf_op jit(solution)/shard_map/all_to_all | solution.py:299
  64.0 0.0 collective-permute-done.2.given
  64.0 0.0 copy-done.1
  64.0 0.5 shard_map.126
  64.6 4.7 %all_gather.14.shared = f32[64,128]{1,0:T(8,128)S(1)} all-gather(f32[32,128]{1,0:T(8,128)S(1)} %get-tuple-element.31), channel_id=1, replica_groups=mesh['z'=12,'y'=8,'c'=2,'x'=4] {'c'}, dimensions={0}, use_global_device_ids=true | all-gather | bytes 49152 | tf_op jit(solution)/shard_map/all_gather | solution.py:89
  69.2 0.4 shard_map.127
  69.6 1.3 %collective-permute-start.3 = (f32[3,2,128]{2,1,0:T(2,128)S(1)}, f32[3,2,128]{2,1,0:T(2,128)S(1)}, u32[]{:S(2)}, u32[]{:S(2)}) collective-permute-start(f32[3,2,128]{2,1,0:T(2,128)S(1)} %maximum_select_fusion.1), channel_id=1, source_target_pairs={{0,8},{8,16},{16,24},{24,32},{32,40},{40,48},{48,56},{56,64},{64,7... | collective-permute-start | bytes 9224 | tf_op jit(solution)/shard_map/ppermute | solution.py:83
  71.0 1.3 %collective-permute-start.4 = (f32[2,2,128]{2,1,0:T(2,128)S(1)}, f32[2,2,128]{2,1,0:T(2,128)S(1)}, u32[]{:S(2)}, u32[]{:S(2)}) collective-permute-start(f32[2,2,128]{2,1,0:T(2,128)S(1)} %maximum_select_fusion.3), channel_id=1, source_target_pairs={{0,1},{1,2},{2,3},{5,4},{6,5},{7,6},{8,9},{9,10},{10,11},{13,12},{... | collective-permute-start | bytes 6152 | tf_op jit(solution)/shard_map/ppermute | solution.py:84
  72.3 0.6 copy.14
  72.9 2.4 %collective-permute-done.4 = f32[2,2,128]{2,1,0:T(2,128)S(1)} collective-permute-done((f32[2,2,128]{2,1,0:T(2,128)S(1)}, f32[2,2,128]{2,1,0:T(2,128)S(1)}, u32[]{:S(2)}, u32[]{:S(2)}) %collective-permute-start.4) | collective-permute-done | bytes 2080 | tf_op jit(solution)/shard_map/ppermute | solution.py:84
  75.3 0.0 collective-permute-done.3
  75.3 2.5 %all_gather.15.moved = f32[10,2,128]{2,1,0:T(2,128)S(1)} all-gather(f32[5,2,128]{2,1,0:T(2,128)S(1)} %pad_maximum_fusion.1), channel_id=1, replica_groups=mesh['z'=12,'y'=8,'c'=2,'x'=4] {'c'}, dimensions={0}, use_global_device_ids=true | all-gather | bytes 15360 | tf_op jit(solution)/shard_map/all_gather | solution.py:89
  77.8 0.8 shard_map.128
  (8 shorter events, 0.1 us)
Async XLA Ops:
  1.3 1.9 %copy-start = (f32[24,18432]{1,0:T(8,128)S(1)}, f32[24,18432]{1,0:T(8,128)}, u32[]{:S(2)}) copy-start(f32[24,18432]{1,0:T(8,128)} %inverse.1) | copy-start | bytes 5308420
  1.3 1.9 %copy-start.2 = (bf16[24,768]{1,0:T(8,128)(2,1)S(1)}, bf16[24,768]{1,0:T(8,128)(2,1)}, u32[]{:S(2)}) copy-start(bf16[24,768]{1,0:T(8,128)(2,1)} %basis.5) | copy-start | bytes 110596
  1.3 1.9 %copy-start.3 = (f32[768]{0:T(1024)S(1)}, f32[768]{0:T(1024)}, u32[]{:S(2)}) copy-start(f32[768]{0:T(1024)} %param.16) | copy-start | bytes 9220
  3.2 23.9 %copy-start.4 = (f32[2,768]{1,0:T(2,128)S(1)}, f32[2,768]{1,0:T(2,128)}, u32[]{:S(2)}) copy-start(f32[2,768]{1,0:T(2,128)} %rhs.1) | copy-start | bytes 18436
  3.2 60.8 %copy-start.1 = (bf16[768,768]{1,0:T(8,128)(2,1)S(1)}, bf16[768,768]{1,0:T(8,128)(2,1)}, u32[]{:S(2)}) copy-start(bf16[768,768]{1,0:T(8,128)(2,1)} %held.1) | copy-start | bytes 3538948
  4.9 59.1 %collective-permute-start.2 = (f32[24,9472]{1,0:T(8,128)}, f32[24,9472]{1,0:T(8,128)S(1)}, u32[]{:S(2)}, u32[]{:S(2)}) collective-permute-start(f32[24,9472]{1,0:T(8,128)} %get-tuple-element.29), channel_id=1, source_target_pairs={{0,4},{4,0},{1,5},{5,1},{2,6},{6,2},{3,7},{7,3},{8,12},{12,8},{9,1... | collective-permute-start | bytes 2727944 | tf_op jit(solution)/shard_map/ppermute | solution.py:289
  19.6 5.6 %collective-permute-start = (f32[3,2,128]{2,1,0:T(2,128)S(1)}, f32[3,2,128]{2,1,0:T(2,128)S(1)}, u32[]{:S(2)}, u32[]{:S(2)}) collective-permute-start(f32[3,2,128]{2,1,0:T(2,128)S(1)} %maximum_select_fusion), channel_id=1, source_target_pairs={{0,8},{8,16},{16,24},{24,32},{32,40},{40,48},{48,56},{56,64},{64,7... | collective-permute-start | bytes 9224 | tf_op jit(solution)/shard_map/ppermute | solution.py:83
  20.9 4.3 %collective-permute-start.1 = (f32[2,2,128]{2,1,0:T(2,128)S(1)}, f32[2,2,128]{2,1,0:T(2,128)S(1)}, u32[]{:S(2)}, u32[]{:S(2)}) collective-permute-start(f32[2,2,128]{2,1,0:T(2,128)S(1)} %maximum_select_fusion.2), channel_id=1, source_target_pairs={{0,1},{1,2},{2,3},{5,4},{6,5},{7,6},{8,9},{9,10},{10,11},{13,12},{... | collective-permute-start | bytes 6152 | tf_op jit(solution)/shard_map/ppermute | solution.py:84
  69.6 5.6 %collective-permute-start.3 = (f32[3,2,128]{2,1,0:T(2,128)S(1)}, f32[3,2,128]{2,1,0:T(2,128)S(1)}, u32[]{:S(2)}, u32[]{:S(2)}) collective-permute-start(f32[3,2,128]{2,1,0:T(2,128)S(1)} %maximum_select_fusion.1), channel_id=1, source_target_pairs={{0,8},{8,16},{16,24},{24,32},{32,40},{40,48},{48,56},{56,64},{64,7... | collective-permute-start | bytes 9224 | tf_op jit(solution)/shard_map/ppermute | solution.py:83
  71.0 4.3 %collective-permute-start.4 = (f32[2,2,128]{2,1,0:T(2,128)S(1)}, f32[2,2,128]{2,1,0:T(2,128)S(1)}, u32[]{:S(2)}, u32[]{:S(2)}) collective-permute-start(f32[2,2,128]{2,1,0:T(2,128)S(1)} %maximum_select_fusion.3), channel_id=1, source_target_pairs={{0,1},{1,2},{2,3},{5,4},{6,5},{7,6},{8,9},{9,10},{10,11},{13,12},{... | collective-permute-start | bytes 6152 | tf_op jit(solution)/shard_map/ppermute | solution.py:84
